TPU v7x, 512 devices: a whole 4x4x16 slice. The times are simulated.
512 devices in a mesh: space: 32 (over y, z_lo), chan: 16 (over x, z_hi, core).
Axes of the slice: x: 4, y: 4, z: 16 (z_hi: 2, z_lo: 8; z = z_hi * 8 + z_lo), core: 2. Of those that a mesh axis runs over, the one named last changes fastest.
Arguments:
- latent: bfloat16 [1, 32, 160, 512], P(None, 'space', None, 'chan'), may hold values from -12 to 12
- cache_mid: bfloat16 [2, 32, 160, 512], P(None, 'space', None, 'chan'), may hold values from -6 to 6
- norm1_gain: float32 [512], P('chan'), may hold values from 0.1 to 1.9
- norm1_bias: float32 [512], P('chan'), may hold values from -3 to 3
- conv1_weight: bfloat16 [3, 3, 3, 512, 512], P(None, None, None, 'chan'), may hold values from -0.0625 to 0.0625
- conv1_bias: float32 [512], P('chan'), may hold values from -2 to 2
- cache_up: bfloat16 [2, 64, 320, 512], P(None, 'space', 'chan'), may hold values from -6 to 6
- norm2_gain: float32 [512], replicated, may hold values from 0.1 to 1.9
- norm2_bias: float32 [512], replicated, may hold values from -3 to 3
- conv2_weight: bfloat16 [3, 3, 3, 512, 512], P(None, None, None, None, 'chan'), may hold values from -0.0546875 to 0.0546875
- conv2_bias: float32 [512], replicated, may hold values from -2 to 2
Outputs:
- up_features: bfloat16 [1, 64, 320, 512], P(None, 'space', 'chan')
All inputs are finite; a program needn't handle non-finite values.
Results may differ from a plain program's by a relative error of at most 0.0038.
The roundings to bfloat16 on the way count: a program that leaves them out, or rounds other values in their place, can miss the bound.
Values may be sent and summed in bfloat16 or wider, within the bound.
No kernel may reach another device: no remote copies, remote signals or barrier semaphores. Data moves between devices by JAX's collectives and lax.ppermute only.
A program may use at most 64 MiB of HBM per device.

v0:
```python
import jax
import jax.numpy as jnp
from jax import lax
from jax.sharding import PartitionSpec as P

GROUPS = 32
GS = 16


epsilon = 1e-06


def extended(cells, sides, width):
    for axis, dim in sides:
        count = lax.axis_size(axis)
        ends = count - 1
        head = lax.slice_in_dim(cells, 0, width, axis=dim)
        tail = lax.slice_in_dim(cells, cells.shape[dim] - width, cells.shape[dim], axis=dim)
        cells = jnp.concatenate(
            [
                lax.ppermute(tail, axis, [(i, (i + 1) % count) for i in range(ends)]),
                cells,
                lax.ppermute(head, axis, [((i + 1) % count, i) for i in range(ends)]),
            ],
            axis=dim,
        )
    return cells


def unfold(padded, frames, height, breadth):
    pieces = []
    for shift_time in range(3):
        for shift_row in range(3):
            for shift_col in range(3):
                pieces.append(
                    padded[
                        shift_time : shift_time + frames,
                        shift_row : shift_row + height,
                        shift_col : shift_col + breadth,
                        :,
                    ]
                )
    return jnp.concatenate(pieces, axis=-1)


def norm_apply(upsampled, mean_chan, scale_chan, gain, bias):
    scaled = (upsampled.astype(jnp.float32) - mean_chan) * scale_chan
    return jax.nn.silu(scaled * gain + bias).astype(jnp.bfloat16)


def on_device(
    latent,
    cache_mid,
    norm1_gain,
    norm1_bias,
    conv1_weight,
    conv1_bias,
    cache_up,
    norm2_gain,
    norm2_bias,
    conv2_weight,
    conv2_bias,
):
    frames, height, breadth, chan_here = latent.shape
    groups_here = chan_here // GS
    values = latent.astype(jnp.float32)
    grouped = values.reshape(frames, height, breadth, groups_here, GS)
    entries = frames * height * lax.axis_size("space") * breadth * GS
    group_mean = lax.psum(jnp.sum(grouped, axis=(0, 1, 2, 4)), "space") / entries
    centred = grouped - group_mean[:, None]
    group_var = lax.psum(jnp.sum(centred * centred, axis=(0, 1, 2, 4)), "space") / entries
    scaled = (centred * lax.rsqrt(group_var + epsilon)[:, None]).reshape(
        frames, height, breadth, chan_here
    )
    normed_mid = jax.nn.silu(scaled * norm1_gain + norm1_bias).astype(jnp.bfloat16)
    joined = jnp.concatenate([cache_mid, normed_mid], axis=0)
    rimmed = extended(joined, (("space", 1),), 1)
    padded = jnp.pad(rimmed, ((0, 0), (0, 0), (1, 1), (0, 0)))
    columns = unfold(padded, frames, height, breadth).reshape(frames * height * breadth, -1)
    kernel = conv1_weight.reshape(-1, conv1_weight.shape[-1])
    summed = lax.psum_scatter(
        lax.dot_general(
            kernel, columns, (((0,), (1,)), ((), ())), preferred_element_type=jnp.float32
        ),
        "chan",
        scatter_dimension=0,
        tiled=True,
    )
    conv_mid = summed.T.reshape(frames, height, breadth, chan_here)
    merged = (values + conv_mid + conv1_bias).astype(jnp.bfloat16)
    merged_groups = merged.astype(jnp.float32).reshape(frames, height, breadth, groups_here, GS)
    first_group = lax.axis_index("chan") * groups_here

    def place(partial_value):
        return lax.dynamic_update_slice_in_dim(
            jnp.zeros((GROUPS,), jnp.float32), partial_value, first_group, 0
        )

    own_sum = jnp.sum(merged_groups, axis=(0, 1, 2, 4))
    up_mean = lax.psum(place(own_sum), ("space", "chan")) / entries
    own_mean = lax.dynamic_slice_in_dim(up_mean, first_group, groups_here)
    deviation = merged_groups - own_mean[:, None]
    up_var = (
        lax.psum(place(jnp.sum(deviation * deviation, axis=(0, 1, 2, 4))), ("space", "chan"))
        / entries
    )
    mean_chan = jnp.repeat(up_mean, GS)
    scale_chan = jnp.repeat(lax.rsqrt(up_var + epsilon), GS)
    pixel_tile = lax.all_to_all(merged, "chan", split_axis=2, concat_axis=3, tiled=True)
    upsampled = jnp.repeat(jnp.repeat(pixel_tile, 2, axis=1), 2, axis=2)
    normed_up = norm_apply(upsampled, mean_chan, scale_chan, norm2_gain, norm2_bias)
    joined_up = jnp.concatenate([cache_up, normed_up], axis=0)
    rimmed_up = extended(joined_up, (("space", 1), ("chan", 2)), 1)
    up_height = normed_up.shape[1]
    up_breadth = normed_up.shape[2]
    up_columns = unfold(rimmed_up, frames, up_height, up_breadth).reshape(
        frames * up_height * up_breadth, -1
    )
    kernel_up = conv2_weight.reshape(-1, conv2_weight.shape[-1])
    up_conv = jnp.dot(
        up_columns,
        lax.all_gather(kernel_up, "chan", axis=1, tiled=True),
        preferred_element_type=jnp.float32,
    )
    result = (up_conv + conv2_bias).astype(jnp.bfloat16).reshape(frames, up_height, up_breadth, -1)
    return result


def solution(mesh):
    placed = (
        P(None, "space", None, "chan"),
        P(None, "space", None, "chan"),
        P("chan"),
        P("chan"),
        P(None, None, None, "chan", None),
        P("chan"),
        P(None, "space", "chan", None),
        P(),
        P(),
        P(None, None, None, None, "chan"),
        P(),
    )
    return jax.shard_map(
        on_device,
        mesh=mesh,
        in_specs=placed,
        out_specs=P(None, "space", "chan", None),
        check_vma=False,
    )
```

profile of v0, /device:TPU:480, one launch (start us, length us, event | category | flops | bytes accessed | tf_op | source)
XLA Modules:
  0.0 809.0 jit_solution(2814931638658902125)
XLA Ops:
  6.6 0.9 convert_reduce_fusion
  7.5 0.1 reduce_sum.47
  7.6 0.1 reduce_sum.51
  7.7 103.2 %psum.28 = f32[2]{0:T(128)S(1)} all-reduce(f32[2]{0:T(128)S(1)} %reduce_sum.51), channel_id=1, replica_groups=mesh['space'=32,'chan'=16] {'space'}, use_global_device_ids=true, to_apply=%region_2.0 | all-reduce | flops 2 | bytes 16 | tf_op jit(solution)/shard_map/psum | solution.py:69
  110.9 0.1 sub.57
  111.0 0.9 fusion.9
  111.9 0.1 reduce_sum.53
  112.0 0.1 reduce_sum.54
  112.1 105.8 %psum.29 = f32[2]{0:T(128)S(1)} all-reduce(f32[2]{0:T(128)S(1)} %reduce_sum.54), channel_id=1, replica_groups=mesh['space'=32,'chan'=16] {'space'}, use_global_device_ids=true, to_apply=%region_5.6 | all-reduce | flops 2 | bytes 16 | tf_op jit(solution)/shard_map/psum | solution.py:71
  218.0 0.1 mul.108
  218.1 0.8 fusion.17
  219.0 0.8 pad_maximum_fusion.2
  219.7 1.9 collective-permute-start.1
  221.7 11.4 %collective-permute-start = (bf16[3,1,160,32]{2,3,1,0:T(8,128)(2,1)S(1)}, bf16[3,1,160,32]{2,3,1,0:T(8,128)(2,1)S(1)}, u32[]{:S(2)}, u32[]{:S(2)}) collective-permute-start(bf16[3,1,160,32]{2,3,1,0:T(8,128)(2,1)S(1)} %pad_maximum_fusion.2), channel_id=1, source_target_pairs={{0,16},{16,32},{32,48},{48,64},{64,80},{80,96},{96,112},{112,128},... | collective-permute-start | bytes 92168 | tf_op jit(solution)/shard_map/ppermute | solution.py:21
  233.1 0.1 collective-permute-done.1
  233.2 2.5 collective-permute-done
  235.7 0.9 select_maximum_fusion
  236.6 0.1 constant_dynamic-update-slice_fusion.24
  236.7 0.7 constant_dynamic-update-slice_fusion.22
  237.6 0.7 constant_dynamic-update-slice_fusion.13
  238.6 0.1 constant_dynamic-update-slice_fusion.4
  238.7 0.1 constant_dynamic-update-slice_fusion.3
  238.9 0.4 convolution_bitcast_fusion
  239.3 1.0 copy.154
  240.4 0.8 copy.152
  241.1 2.0 reshape.194
  243.2 106.8 %reduce-scatter.4.cloned.1.call-done = f32[32,160]{1,0:T(8,128)} async-done(((f32[512,160]{1,0:T(8,128)}), f32[32,160]{1,0:T(8,128)}) %reduce-scatter.4.cloned.1.call-update) | async-done | bytes 20496 | tf_op jit(solution)/shard_map/reduce_scatter | solution.py:81
  350.0 0.9 convert_reduce_fusion.1
  350.9 0.1 reduce_sum.59
  351.0 0.1 reduce_sum.72
  351.1 0.2 dynamic_update_slice.6
  351.4 270.6 %psum.30 = f32[32]{0:T(128)S(1)} all-reduce(f32[32]{0:T(128)S(1)} %dynamic_update_slice.6), channel_id=1, replica_groups=mesh['space'=32,'chan'=16] {'space','chan'}, use_global_device_ids=true, to_apply=%region_9.10 | all-reduce | flops 32 | bytes 256 | tf_op jit(solution)/shard_map/psum | solution.py:100
  622.1 0.1 sub.64
  622.2 0.2 fusion.19
  622.4 0.1 reduce_sum.74
  622.5 0.1 reduce_sum.75
  622.6 0.2 dynamic_update_slice.7
  622.8 100.2 %psum.31 = f32[32]{0:T(128)S(1)} all-reduce(f32[32]{0:T(128)S(1)} %dynamic_update_slice.7), channel_id=1, replica_groups=mesh['space'=32,'chan'=16] {'space','chan'}, use_global_device_ids=true, to_apply=%region_12.13 | all-reduce | flops 32 | bytes 256 | tf_op jit(solution)/shard_map/psum | solution.py:104
  723.0 0.1 copy.124
  723.1 0.5 broadcast.171
  723.6 0.9 reduce.10
  724.5 0.7 reshape.200
  725.2 14.1 %all-to-all-start = ((bf16[16,2,160]{2,1,0:T(2,128)(2,1)}), bf16[16,2,160]{2,1,0:T(2,128)(2,1)S(1)}, u32[]{:S(2)}, u32[]{:S(2)}) async-start(bf16[16,2,160]{2,1,0:T(2,128)(2,1)} %reshape.200), calls=%async_computation | async-start | bytes 32768 | tf_op jit(solution)/shard_map/all_to_all | solution.py:109
  739.4 0.1 mul.116
  739.6 0.1 sub.60
  739.7 4.4 all-to-all-done
  744.1 0.1 reshape.201
  744.2 0.1 convert_bitcast_fusion
  744.3 0.1 reshape.196
  744.5 0.1 fusion.6
  744.6 0.2 slice_maximum_fusion
  744.9 5.9 collective-permute-start.2
  750.8 1.9 collective-permute-start.3
  752.8 1.6 collective-permute-done.2
  754.4 10.8 %collective-permute-done.3 = bf16[3,1,20,512]{3,1,2,0:T(2,128)(2,1)S(1)} collective-permute-done((bf16[3,1,20,512]{3,1,2,0:T(2,128)(2,1)S(1)}, bf16[3,1,20,512]{3,1,2,0:T(2,128)(2,1)S(1)}, u32[]{:S(2)}, u32[]{:S(2)}) %collective-permute-start.3) | collective-permute-done | bytes 61472 | tf_op jit(solution)/shard_map/ppermute | solution.py:23
  765.3 10.6 %collective-permute-start.5 = (bf16[3,4,1,512]{3,1,2,0:T(4,128)(2,1)S(1)}, bf16[3,4,1,512]{3,1,2,0:T(4,128)(2,1)S(1)}, u32[]{:S(2)}, u32[]{:S(2)}) collective-permute-start(bf16[3,4,1,512]{3,1,2,0:T(4,128)(2,1)S(1)} %get-tuple-element.9), channel_id=1, source_target_pairs={{1,0},{2,1},{3,2},{4,3},{5,4},{6,5},{7,6},{8,7},{9,8},{10,9},{11,1... | collective-permute-start | bytes 36872 | tf_op jit(solution)/shard_map/ppermute | solution.py:23
  775.9 1.9 collective-permute-start.4
  777.8 0.6 pad_maximum_fusion.3
  778.7 11.0 %collective-permute-done.4 = bf16[3,4,1,512]{3,1,2,0:T(4,128)(2,1)S(1)} collective-permute-done((bf16[3,4,1,512]{3,1,2,0:T(4,128)(2,1)S(1)}, bf16[3,4,1,512]{3,1,2,0:T(4,128)(2,1)S(1)}, u32[]{:S(2)}, u32[]{:S(2)}) %collective-permute-start.4) | collective-permute-done | bytes 12320 | tf_op jit(solution)/shard_map/ppermute | solution.py:21
  789.6 0.7 pad_maximum_fusion
  790.4 0.5 fusion.23
  792.0 0.3 copy-done.6
  792.3 9.2 %fusion = bf16[40,512]{1,0:T(8,128)(2,1)S(1)} fusion(bf16[40,13824]{1,0:T(8,128)(2,1)S(1)} %constant_dynamic-update-slice_fusion.27, bf16[13824,512]{0,1:T(8,128)(2,1)} %all-gather.2.cloned.1.call-done, f32[512]{0:T(512)S(1)} %copy-done.6), kind=kOutput, calls=%fused_computation.2 | convolution fusion | flops 566272000 | bytes 15304704 | tf_op jit(solution)/shard_map/dot_general | solution.py:120
  801.5 0.6 copy.153
  (147 shorter events, 2.2 us)
Async XLA Ops:
  6.5 232.4 %copy-start = (bf16[3,3,3,32,512]{4,3,2,1,0:T(8,128)(2,1)S(1)}, bf16[3,3,3,32,512]{4,3,2,1,0:T(8,128)(2,1)}, u32[]{:S(2)}) copy-start(bf16[3,3,3,32,512]{4,3,2,1,0:T(8,128)(2,1)} %param.15) | copy-start | bytes 2654212
  6.5 232.1 %copy-start.3 = (bf16[1,1,160,32]{2,3,1,0:T(8,128)(2,1)S(1)}, bf16[1,1,160,32]{2,3,1,0:T(8,128)(2,1)}, u32[]{:S(2)}) copy-start(bf16[1,1,160,32]{2,3,1,0:T(8,128)(2,1)} %param.11) | copy-start | bytes 30724
  6.5 232.1 %copy-start.7 = (f32[32]{0:T(128)S(1)}, f32[32]{0:T(128)}, u32[]{:S(2)}) copy-start(f32[32]{0:T(128)} %param.14) | copy-start | bytes 388
  6.5 232.1 %copy-start.8 = (f32[32]{0:T(128)S(1)}, f32[32]{0:T(128)}, u32[]{:S(2)}) copy-start(f32[32]{0:T(128)} %param.13) | copy-start | bytes 388
  6.5 343.4 %reduce-scatter.4.cloned.1.call-start = ((), (), s32[]{:S(2)}) async-start(), calls=%async_computation.3 | async-start | bytes 557056 | tf_op jit(solution)/shard_map/reduce_scatter | solution.py:81
  219.7 13.5 %collective-permute-start.1 = (bf16[3,1,160,32]{2,3,1,0:T(8,128)(2,1)S(1)}, bf16[3,1,160,32]{2,3,1,0:T(8,128)(2,1)S(1)}, u32[]{:S(2)}, u32[]{:S(2)}) collective-permute-start(bf16[3,1,160,32]{2,3,1,0:T(8,128)(2,1)S(1)} %pad_maximum_fusion.2), channel_id=1, source_target_pairs={{16,0},{32,16},{48,32},{64,48},{80,64},{96,80},{112,96},{128,112},... | collective-permute-start | bytes 92168 | tf_op jit(solution)/shard_map/ppermute | solution.py:23
  221.7 14.0 %collective-permute-start = (bf16[3,1,160,32]{2,3,1,0:T(8,128)(2,1)S(1)}, bf16[3,1,160,32]{2,3,1,0:T(8,128)(2,1)S(1)}, u32[]{:S(2)}, u32[]{:S(2)}) collective-permute-start(bf16[3,1,160,32]{2,3,1,0:T(8,128)(2,1)S(1)} %pad_maximum_fusion.2), channel_id=1, source_target_pairs={{0,16},{16,32},{32,48},{48,64},{64,80},{80,96},{96,112},{112,128},... | collective-permute-start | bytes 92168 | tf_op jit(solution)/shard_map/ppermute | solution.py:21
  238.9 1.5 copy-start.2
  240.3 551.7 %all-gather.2.cloned.1.call-start = ((), (), s32[]{:S(2)}) async-start(), calls=%async_computation.2 | async-start | bytes 15040512 | tf_op jit(solution)/shard_map/all_gather | solution.py:122
  241.1 108.9 %copy-start.9 = (f32[32]{0:T(128)S(1)}, f32[32]{0:T(128)}, u32[]{:S(2)}) copy-start(f32[32]{0:T(128)} %param.16) | copy-start | bytes 388
  243.2 501.3 %copy-start.4 = (f32[512]{0:T(512)S(1)}, f32[512]{0:T(512)}, u32[]{:S(2)}) copy-start(f32[512]{0:T(512)} %param.19) | copy-start | bytes 6148
  243.2 501.3 %copy-start.5 = (f32[512]{0:T(512)S(1)}, f32[512]{0:T(512)}, u32[]{:S(2)}) copy-start(f32[512]{0:T(512)} %param.18) | copy-start | bytes 6148
  243.2 501.5 %copy-start.1 = (bf16[2,2,20,512]{3,1,2,0:T(2,128)(2,1)S(1)}, bf16[2,2,20,512]{3,1,2,0:T(2,128)(2,1)}, u32[]{:S(2)}) copy-start(bf16[2,2,20,512]{3,1,2,0:T(2,128)(2,1)} %param.17) | copy-start | bytes 245764
  243.2 509.5 %slice-start = ((bf16[2,2,20,512]{3,1,2,0:T(2,128)(2,1)}), bf16[1,2,20,512]{3,1,2,0:T(2,128)(2,1)S(1)}, s32[]{:S(2)}) async-start(bf16[2,2,20,512]{3,1,2,0:T(2,128)(2,1)} %param.17), calls=%async_computation.4 | async-start | bytes 81920 | tf_op jit(solution)/shard_map/slice | solution.py:36
  725.2 18.9 %all-to-all-start = ((bf16[16,2,160]{2,1,0:T(2,128)(2,1)}), bf16[16,2,160]{2,1,0:T(2,128)(2,1)S(1)}, u32[]{:S(2)}, u32[]{:S(2)}) async-start(bf16[16,2,160]{2,1,0:T(2,128)(2,1)} %reshape.200), calls=%async_computation | async-start | bytes 32768 | tf_op jit(solution)/shard_map/all_to_all | solution.py:109
  744.9 9.5 %collective-permute-start.2 = (bf16[3,1,20,512]{3,1,2,0:T(2,128)(2,1)S(1)}, bf16[3,1,20,512]{3,1,2,0:T(2,128)(2,1)S(1)}, u32[]{:S(2)}, u32[]{:S(2)}) collective-permute-start(bf16[3,1,20,512]{3,1,2,0:T(2,128)(2,1)S(1)} %get-tuple-element.38), channel_id=1, source_target_pairs={{0,16},{16,32},{32,48},{48,64},{64,80},{80,96},{96,112},{112,128},... | collective-permute-start | bytes 184328 | tf_op jit(solution)/shard_map/ppermute | solution.py:21
  750.8 14.5 %collective-permute-start.3 = (bf16[3,1,20,512]{3,1,2,0:T(2,128)(2,1)S(1)}, bf16[3,1,20,512]{3,1,2,0:T(2,128)(2,1)S(1)}, u32[]{:S(2)}, u32[]{:S(2)}) collective-permute-start(bf16[3,1,20,512]{3,1,2,0:T(2,128)(2,1)S(1)} %get-tuple-element.39), channel_id=1, source_target_pairs={{16,0},{32,16},{48,32},{64,48},{80,64},{96,80},{112,96},{128,112},... | collective-permute-start | bytes 184328 | tf_op jit(solution)/shard_map/ppermute | solution.py:23
  765.3 13.4 %collective-permute-start.5 = (bf16[3,4,1,512]{3,1,2,0:T(4,128)(2,1)S(1)}, bf16[3,4,1,512]{3,1,2,0:T(4,128)(2,1)S(1)}, u32[]{:S(2)}, u32[]{:S(2)}) collective-permute-start(bf16[3,4,1,512]{3,1,2,0:T(4,128)(2,1)S(1)} %get-tuple-element.9), channel_id=1, source_target_pairs={{1,0},{2,1},{3,2},{4,3},{5,4},{6,5},{7,6},{8,7},{9,8},{10,9},{11,1... | collective-permute-start | bytes 36872 | tf_op jit(solution)/shard_map/ppermute | solution.py:23
  775.9 13.7 %collective-permute-start.4 = (bf16[3,4,1,512]{3,1,2,0:T(4,128)(2,1)S(1)}, bf16[3,4,1,512]{3,1,2,0:T(4,128)(2,1)S(1)}, u32[]{:S(2)}, u32[]{:S(2)}) collective-permute-start(bf16[3,4,1,512]{3,1,2,0:T(4,128)(2,1)S(1)} %get-tuple-element.10), channel_id=1, source_target_pairs={{0,1},{1,2},{2,3},{3,4},{4,5},{5,6},{6,7},{7,8},{8,9},{9,10},{10,1... | collective-permute-start | bytes 36872 | tf_op jit(solution)/shard_map/ppermute | solution.py:21
  791.6 0.7 copy-start.6
Sparse Core Ops, SparseCore 0:
  240.4 109.5 reduce-scatter.3
  353.3 250.6 all-gather.1
where the time goes:
time: 810 us; the launch traced here: 809 us
  blocking collectives  580 us (72%)
  waiting for transfers between devices  137 us (17%)
  starting transfers between devices  47.9 us (6%)
  between operations  14.4 us (2%)
  local copies, waits for them, and re-layouts  11.5 us (1%)
  matrix products  9.58 us (1%)
  other arithmetic  8.67 us (1%)
    psum x1, blocking collectives, on_device(): up_mean = lax.psum(place(own_sum), ('space', 'chan')) / entries  271 us
    reduce_scatter x1, waiting for transfers between devices, on_device(): lax.psum_scatter(lax.dot_general(kernel, columns, (((0,), (1,)), ((), ())...  107 us
    psum x1, blocking collectives, on_device(): lax.psum(jnp.sum(centred * centred, axis=(0, 1, 2, 4)), 'space') / entries  106 us
    psum x1, blocking collectives, on_device(): lax.psum(jnp.sum(grouped, axis=(0, 1, 2, 4)), 'space') / entries  103 us
    psum x1, blocking collectives, on_device(): lax.psum(place(jnp.sum(deviation * deviation, axis=(0, 1, 2, 4))), ('spac...  100 us
    ppermute x3, starting transfers between devices, extended(): lax.ppermute(tail, axis, [(i, (i + 1) % count) for i in range(ends)])  19.2 us
  transfers between devices with their start and end apart: 9, of which 7 were waited for; matrix products, arithmetic and copies ran while one was open for 1% of the time, Pallas kernels for 0%

commit v1 on v0

v1 whole, which is shorter than its diff:
```python
import functools

import jax
import jax.numpy as jnp
from jax import lax
from jax.experimental import pallas as pl
from jax.experimental.pallas import tpu as pltpu
from jax.sharding import Mesh
from jax.sharding import PartitionSpec as P

GS = 16
EPS = 1e-06
F32 = jnp.float32
BF16 = jnp.bfloat16
USE_KERNELS = True


def run(fn, out_shapes, args, scalars=(), name=None):
    if not USE_KERNELS:
        return fn(*scalars, *args)
    n_s, n_a, single = len(scalars), len(args), isinstance(out_shapes, tuple)
    shapes = [out_shapes] if single else list(out_shapes)

    def body(*refs):
        ins = list(refs[:n_s]) + [r[...] for r in refs[n_s : n_s + n_a]]
        outs = fn(*ins)
        outs = [outs] if single else outs
        for ref, value in zip(refs[n_s + n_a :], outs):
            ref[...] = value

    vmem = pl.BlockSpec(memory_space=pltpu.VMEM)
    res = pl.pallas_call(
        body,
        out_shape=[jax.ShapeDtypeStruct(s, d) for s, d in shapes],
        in_specs=[pl.BlockSpec(memory_space=pltpu.SMEM)] * n_s + [vmem] * n_a,
        out_specs=[vmem] * len(shapes),
        name=name,
    )(*scalars, *args)
    return res[0] if single else res


def to_row(col):
    n = col.shape[0]
    eye = lax.broadcasted_iota(jnp.int32, (n, n), 0) == lax.broadcasted_iota(jnp.int32, (n, n), 1)
    return jnp.sum(jnp.where(eye, col, 0.0), axis=0, keepdims=True)


def to_col(row, repeat):
    n = row.shape[1]
    rows = lax.broadcasted_iota(jnp.int32, (n * repeat, n), 0)
    lanes = lax.broadcasted_iota(jnp.int32, (n * repeat, n), 1)
    pick = (rows >= lanes * repeat) & (rows < lanes * repeat + repeat)
    return jnp.sum(jnp.where(pick, row, 0.0), axis=1, keepdims=True)


def partial_stats(values, peers):
    rows, cols = values.shape
    groups = rows // GS
    x = values.astype(F32)
    mean = jnp.sum(jnp.sum(x, axis=1, keepdims=True).reshape(groups, GS, 1), axis=1) / (GS * cols)
    dev = x.reshape(groups, GS, cols) - mean[:, :, None]
    sq = jnp.sum(jnp.sum(dev * dev, axis=2, keepdims=True), axis=1)
    row = jnp.concatenate(
        [to_row(mean), to_row(sq), jnp.zeros((1, 128 - 2 * groups), F32)], axis=1
    )
    return jnp.broadcast_to(row[None], (peers, 1, 128))


def merge_stats(parts, groups, count):
    peers = parts.shape[0]
    means = parts[:, 0, :groups]
    sq = parts[:, 0, groups : 2 * groups]
    mean = jnp.sum(means, axis=0, keepdims=True) / peers
    gap = means - mean
    var = (jnp.sum(sq, axis=0, keepdims=True) + count * jnp.sum(gap * gap, axis=0, keepdims=True)) / (
        count * peers
    )
    return mean, lax.rsqrt(var + EPS)


def norm_silu(x, mean, scale, gain, bias):
    v = (x.astype(F32) - mean) * scale * gain + bias
    low = v < -80.0
    e = jnp.exp(jnp.where(low, v, -v))
    return jnp.where(low, v * e, v / (1.0 + jnp.where(low, 0.0, e)))


def right(a):
    return jnp.concatenate([jnp.zeros((a.shape[0], 1), a.dtype), a[:, :-1]], axis=1)


def left(a):
    return jnp.concatenate([a[:, 1:], jnp.zeros((a.shape[0], 1), a.dtype)], axis=1)


def mid_conv(place, parts, raw, above, below, gain, bias, kernel):
    chans, cols = raw.shape[1:]
    groups = chans // GS
    mean, scale = merge_stats(parts, groups, GS * cols)
    mean, scale = to_col(mean, GS), to_col(scale, GS)
    pieces = []
    for t in range(3):
        for dy, src in enumerate((above, raw, below)):
            x = src[t].astype(F32)
            if t == 2:
                x = norm_silu(x, mean, scale, gain, bias)
                if dy != 1:
                    x = jnp.where(place[0 if dy == 0 else 1] == 1, x, 0.0)
            pieces += [right(x).astype(BF16), x.astype(BF16), left(x).astype(BF16)]
    columns = jnp.concatenate(pieces, axis=0)
    out = jnp.dot(kernel, columns, preferred_element_type=F32)
    return out.reshape(8, out.shape[0] // 8, cols)


def fold(place, parts, own, bias):
    total = jnp.sum(parts, axis=0)
    half = total.shape[0] // 2
    extra = own.astype(F32) + bias
    zero = jnp.zeros_like(extra)
    first = place[2] == 0
    return total + jnp.concatenate(
        [jnp.where(first, extra, zero), jnp.where(first, zero, extra)], axis=0
    )


def row_stats(gathered, peers):
    cols = gathered.shape[2]
    blocks = gathered.reshape(4, 2, 2, 32, cols)
    row = jnp.concatenate(
        [blocks[x, k, h] for x in range(4) for h in range(2) for k in range(2)], axis=0
    )
    return row, partial_stats(row, peers)


def taps(prod):
    return [[prod[(dy * 3 + dx) * 32 : (dy * 3 + dx + 1) * 32] for dx in range(3)] for dy in range(3)]


def cache_conv(images, kernel):
    per = 9 * 32
    sums = {}

    def add(key, value):
        sums[key] = sums[key] + value if key in sums else value

    for t in range(2):
        w = kernel[t * per : (t + 1) * per]
        for r in range(2):
            even, odd = (
                taps(
                    lax.dot_general(
                        w, images[t, r, p], (((1,), (1,)), ((), ())), preferred_element_type=F32
                    )
                )
                for p in range(2)
            )
            for dy in range(3):
                o = r + 1 - dy
                add((o, "m", 0), even[dy][1] + odd[dy][2])
                add((o, "r", 0), odd[dy][0])
                add((o, "m", 1), even[dy][0] + odd[dy][1])
                add((o, "l", 1), even[dy][2])

    def out(o):
        return jnp.concatenate(
            [
                sums[(o, "m", 0)] + right(sums[(o, "r", 0)]),
                sums[(o, "m", 1)] + left(sums[(o, "l", 1)]),
            ],
            axis=0,
        )

    return jnp.concatenate([out(0), out(1)], axis=0), out(-1), out(2)


def up_conv(place, parts, row, above, below, gain, bias, kernel, held, from_above, from_below, out_bias):
    chans, cols = row.shape
    groups = chans // GS
    mean, scale = merge_stats(parts, groups, GS * cols)
    mean, scale = to_col(mean, GS), to_col(scale, GS)
    per = 9 * 32
    w = kernel[2 * per :]

    def image(x, keep=None):
        v = norm_silu(x, mean, scale, gain, bias)
        if keep is not None:
            v = jnp.where(keep == 1, v, 0.0)
        return v.astype(BF16)

    lhs = jnp.concatenate([w[dy * 3 * 32 : (dy + 1) * 3 * 32] for dy in range(3)], axis=1)
    here = image(row)
    outs = []
    for images in (
        (image(above, place[0]), here, here),
        (here, here, image(below, place[1])),
    ):
        prod = jnp.dot(lhs, jnp.concatenate(images, axis=0), preferred_element_type=F32)
        cut = [prod[dx * 32 : (dx + 1) * 32] for dx in range(3)]
        outs += [right(cut[0]) + cut[1] + cut[2], cut[0] + cut[1] + left(cut[2])]
    total = jnp.concatenate(outs, axis=0) + held
    total = total + jnp.concatenate([from_above, from_below], axis=0) + out_bias
    return total.T.astype(BF16)


def on_device(
    sizes,
    latent,
    cache_mid,
    norm1_gain,
    norm1_bias,
    conv1_weight,
    conv1_bias,
    cache_up,
    norm2_gain,
    norm2_bias,
    conv2_weight,
    conv2_bias,
):
    n_y, n_l = sizes
    peers = n_y * n_l
    cols, chans = latent.shape[2], latent.shape[3]
    place_s = lax.axis_index(("y", "l"))
    hi = lax.axis_index("h")
    chan = lax.axis_index(("x", "h", "k"))
    place = jnp.stack(
        [(place_s > 0).astype(jnp.int32), (place_s < peers - 1).astype(jnp.int32), hi.astype(jnp.int32)]
    )
    space = ("y", "l")
    own = latent[0, 0].T
    stats = run(
        functools.partial(partial_stats, peers=peers), ((peers, 1, 128), F32), (own,), name="stats_mid"
    )
    stats = lax.all_to_all(stats, space, 0, 0, tiled=True)
    raw = jnp.concatenate([cache_mid[:, 0], latent[0]], axis=0).transpose(0, 2, 1)
    down = [(i, i + 1) for i in range(peers - 1)]
    up = [(i + 1, i) for i in range(peers - 1)]
    above = lax.ppermute(raw, space, down)
    below = lax.ppermute(raw, space, up)
    kernel1 = conv1_weight.reshape(27 * chans, 4, 2, 2, 32).transpose(1, 3, 2, 4, 0).reshape(512, -1)
    partial = run(
        mid_conv,
        ((8, 64, cols), F32),
        (stats, raw, above, below, norm1_gain[:, None], norm1_bias[:, None], kernel1),
        (place,),
        name="mid_conv",
    )
    partial = lax.all_to_all(partial, ("x", "k"), 0, 0, tiled=True)
    mine = run(fold, ((64, cols), F32), (partial, own, conv1_bias[:, None]), (place,), name="fold")
    other = lax.ppermute(mine, "h", [(0, 1), (1, 0)])
    merged = (mine + other).astype(BF16)
    gathered = lax.all_to_all(
        jnp.broadcast_to(merged[None], (8, 64, cols)), ("x", "k"), 0, 0, tiled=True
    )
    row, stats2 = run(
        functools.partial(row_stats, peers=peers),
        [((512, cols), BF16), ((peers, 1, 128), F32)],
        (gathered,),
        name="row_stats",
    )
    stats2 = lax.all_to_all(stats2, space, 0, 0, tiled=True)

    def at(y, l, h):
        return (y * n_l + l) * 2 + h

    down_h, up_h = [], []
    for y in range(n_y):
        for l in range(n_l):
            for h in range(2):
                if l < n_l - 1:
                    pair = (at(y, l, h), at(y, l + 1, h))
                elif y < n_y - 1:
                    pair = (at(y, l, h), at(y + 1, 0, 1 - h))
                else:
                    continue
                down_h.append(pair)
                up_h.append(pair[::-1])
    row_above = lax.ppermute(row, ("y", "l", "h"), down_h)
    row_below = lax.ppermute(row, ("y", "l", "h"), up_h)

    tile = cache_up.reshape(2, 2, 10, 2, 512).transpose(0, 1, 3, 2, 4)
    swapped = lax.ppermute(tile, "h", [(0, 1), (1, 0)])
    pair = jnp.where(hi == 0, jnp.stack([tile, swapped]), jnp.stack([swapped, tile]))
    spread = lax.all_to_all(
        jnp.broadcast_to(pair[None], (8,) + pair.shape), ("x", "k"), 0, 0, tiled=True
    )
    images = (
        spread.reshape(4, 2, 2, 2, 2, 2, 10, 512)
        .transpose(3, 4, 5, 0, 2, 1, 6, 7)
        .reshape(2, 2, 2, cols, 512)
    )
    kernel2 = conv2_weight.transpose(0, 1, 2, 4, 3).reshape(27 * 32, 512)
    held, to_above, to_below = run(
        cache_conv,
        [((128, cols), F32), ((64, cols), F32), ((64, cols), F32)],
        (images, kernel2),
        name="cache_conv",
    )
    from_above = lax.ppermute(to_below, space, down)
    from_below = lax.ppermute(to_above, space, up)
    bias_here = lax.dynamic_slice_in_dim(conv2_bias, chan * 32, 32)
    out = run(
        up_conv,
        ((cols, 128), BF16),
        (
            stats2,
            row,
            row_above,
            row_below,
            norm2_gain[:, None],
            norm2_bias[:, None],
            kernel2,
            held,
            from_above,
            from_below,
            jnp.tile(bias_here, 4)[:, None],
        ),
        (place,),
        name="up_conv",
    )
    out = lax.all_to_all(out.reshape(16, 10, 128), ("x", "h", "k"), 0, 0, tiled=True)
    out = out.reshape(16, 10, 2, 2, 32).transpose(2, 1, 3, 0, 4)
    return out.reshape(1, 2, 20, 512)


def solution(mesh):
    peers = mesh.shape["space"]
    n_l = 8 if peers % 8 == 0 else 2
    n_y = peers // n_l
    fine = Mesh(mesh.devices.reshape(n_y, n_l, 4, 2, 2), ("y", "l", "x", "h", "k"))
    space, chan = ("y", "l"), ("x", "h", "k")
    placed = (
        P(None, space, None, chan),
        P(None, space, None, chan),
        P(chan),
        P(chan),
        P(None, None, None, chan, None),
        P(chan),
        P(None, space, chan, None),
        P(),
        P(),
        P(None, None, None, None, chan),
        P(),
    )
    return jax.shard_map(
        functools.partial(on_device, (n_y, n_l)),
        mesh=fine,
        in_specs=placed,
        out_specs=P(None, space, chan, None),
        check_vma=False,
    )
```

time: 810 us -> 187 us (0.23)
  the two profiles are of different devices: /device:TPU:480 before, /device:TPU:9 now
where the time goes in v1:
time: 187 us; the launch traced here: 186 us
  starting transfers between devices  90.1 us (48%)
  local copies, waits for them, and re-layouts  30.3 us (16%)
  blocking collectives  27.9 us (15%)
  waiting for transfers between devices  19.7 us (11%)
  Pallas kernels  15.1 us (8%)
  other arithmetic  3.07 us (2%)
    all_to_all x1, blocking collectives, on_device(): lax.all_to_all(out.reshape(16, 10, 128), ('x', 'h', 'k'), 0, 0, tiled=True)  27.9 us
    pallas_call x6, Pallas kernels, run(): pl.pallas_call(body, out_shape=[jax.ShapeDtypeStruct(s, d) for s, d in sh...  15.1 us
    all_to_all x1, starting transfers between devices, on_device(): stats2 = lax.all_to_all(stats2, space, 0, 0, tiled=True)  12.6 us
    ppermute x1, starting transfers between devices, on_device(): other = lax.ppermute(mine, 'h', [(0, 1), (1, 0)])  11.8 us
    ppermute x1, starting transfers between devices, on_device(): below = lax.ppermute(raw, space, up)  11.1 us
    ppermute x1, starting transfers between devices, on_device(): from_below = lax.ppermute(to_above, space, up)  9.69 us
    ppermute x1, starting transfers between devices, on_device(): row_below = lax.ppermute(row, ('y', 'l', 'h'), up_h)  9.41 us
    all_to_all x1, waiting for transfers between devices, on_device(): partial = lax.all_to_all(partial, ('x', 'k'), 0, 0, tiled=True)  8.66 us
  transfers between devices with their start and end apart: 13, of which 5 were waited for; matrix products, arithmetic and copies ran while one was open for 14% of the time, Pallas kernels for 4%

profile of v1, /device:TPU:9, one launch (start us, length us, event | category | flops | bytes accessed | tf_op | source)
XLA Modules:
  0.0 186.4 jit_solution(14142568312885814170)
XLA Ops:
  0.0 1.4 maximum_bitcast_fusion.refs_2_
  1.4 3.5 %collective-permute-start = (bf16[3,32,160]{2,1,0:T(8,128)(2,1)}, bf16[3,32,160]{2,1,0:T(8,128)(2,1)}, u32[]{:S(2)}, u32[]{:S(2)}) collective-permute-start(bf16[3,32,160]{2,1,0:T(8,128)(2,1)} %maximum_bitcast_fusion.refs_2_), channel_id=1, source_target_pairs={{0,16},{16,32},{32,48},{48,64},{64,80},{80,96},{96,112},{112,128},... | collective-permute-start | bytes 92168 | tf_op jit(solution)/shard_map/ppermute | solution.py:237
  4.9 11.1 %collective-permute-start.1 = (bf16[3,32,160]{2,1,0:T(8,128)(2,1)}, bf16[3,32,160]{2,1,0:T(8,128)(2,1)}, u32[]{:S(2)}, u32[]{:S(2)}) collective-permute-start(bf16[3,32,160]{2,1,0:T(8,128)(2,1)} %maximum_bitcast_fusion.refs_2_), channel_id=1, source_target_pairs={{16,0},{32,16},{48,32},{64,48},{80,64},{96,80},{112,96},{128,112},... | collective-permute-start | bytes 92168 | tf_op jit(solution)/shard_map/ppermute | solution.py:238
  16.1 1.6 stats_mid.1
  17.7 6.2 %all-to-all-start = ((f32[32,1,128]{2,1,0:T(1,128)}), f32[32,1,128]{2,1,0:T(1,128)S(1)}, u32[]{:S(2)}, u32[]{:S(2)}) async-start(f32[32,1,128]{2,1,0:T(1,128)} %stats_mid.1), calls=%async_computation | async-start | bytes 32768 | tf_op jit(solution)/shard_map/all_to_all | solution.py:233
  23.9 0.6 pad_add_fusion.refs_0_
  24.5 7.8 %reshape.62 = bf16[864,4,2,2,32]{4,3,2,1,0:T(2,128)(2,1)S(1)} reshape(bf16[3,3,3,32,512]{4,3,2,1,0:T(8,128)(2,1)} %param.15) | data formatting | bytes 1769472 | tf_op jit(solution)/shard_map/reshape | solution.py:239
  32.3 6.4 %copy.30 = bf16[4,2,2,32,864]{4,3,2,1,0:T(8,128)(2,1)} copy(bf16[4,2,2,32,864]{3,1,2,0,4:T(2,128)(2,1)S(1)} %bitcast.39) | data formatting | bytes 1769472 | tf_op jit(solution)/shard_map/transpose | solution.py:239
  38.8 1.3 copy.31.refs_5_
  40.1 1.3 copy.32.refs_6_
  41.4 0.0 collective-permute-done.refs_3_
  41.4 0.0 collective-permute-done.1.refs_4_
  41.4 0.0 all-to-all-done.refs_1_
  41.4 0.0 copy-start.6
  41.4 0.6 copy-done.6
  42.0 3.0 %mid_conv.1 = f32[8,64,160]{2,1,0:T(8,128)} custom-call(s32[3]{0:T(128)} %pad_add_fusion.refs_0_, f32[32,1,128]{2,1,0:T(1,128)} %copy-done.6, bf16[3,32,160]{2,1,0:T(8,128)(2,1)} %maximum_bitcast_fusion.refs_2_, bf16[3,32,160]{2,1,0:T(8,128)(2,1)} %collective-permute-done.refs_3_, bf16[3,32,160]{2,1,0:T(8,128)(2,1)} %collective-permute-done.1.refs_4_, ...), custom_call_target="tpu_custom_call" | custom-call | tf_op jit(solution)/shard_map/mid_conv/pallas_call | solution.py:32
  45.0 6.1 %all-to-all-start.1 = ((f32[8,64,160]{2,1,0:T(8,128)}), f32[8,64,160]{2,1,0:T(8,128)S(1)}, u32[]{:S(2)}, u32[]{:S(2)}) async-start(f32[8,64,160]{2,1,0:T(8,128)} %mid_conv.1), calls=%async_computation.1 | async-start | bytes 1048576 | tf_op jit(solution)/shard_map/all_to_all | solution.py:247
  51.1 0.0 copy-done.11
  51.1 0.7 copy.33.refs_3_
  51.8 8.7 %all-to-all-done.1.refs_1_ = f32[8,64,160]{2,1,0:T(8,128)S(1)} async-done(((f32[8,64,160]{2,1,0:T(8,128)}), f32[8,64,160]{2,1,0:T(8,128)S(1)}, u32[]{:S(2)}, u32[]{:S(2)}) %all-to-all-start.1) | async-done | bytes 327712 | tf_op jit(solution)/shard_map/all_to_all | solution.py:247
  60.4 0.8 copy-done
  61.3 1.8 fold.1
  63.0 11.8 %collective-permute-start.2 = (f32[64,160]{1,0:T(8,128)}, f32[64,160]{1,0:T(8,128)S(1)}, u32[]{:S(2)}, u32[]{:S(2)}) collective-permute-start(f32[64,160]{1,0:T(8,128)} %fold.1), channel_id=1, source_target_pairs={{0,2},{2,0},{1,3},{3,1},{4,6},{6,4},{5,7},{7,5},{8,10},{10,8},{9,1... | collective-permute-start | bytes 122888 | tf_op jit(solution)/shard_map/ppermute | solution.py:249
  74.9 2.2 %collective-permute-start.5 = (bf16[2,2,2,10,512]{4,1,2,3,0:T(2,128)(2,1)S(1)}, bf16[2,2,2,10,512]{4,1,2,3,0:T(2,128)(2,1)S(1)}, u32[]{:S(2)}, u32[]{:S(2)}) collective-permute-start(bf16[2,2,2,10,512]{4,1,2,3,0:T(2,128)(2,1)S(1)} %bitcast.49), channel_id=1, source_target_pairs={{0,2},{2,0},{1,3},{3,1},{4,6},{6,4},{5,7},{7,5},{8,10},{10,8},{9,1... | collective-permute-start | bytes 245768 | tf_op jit(solution)/shard_map/ppermute | solution.py:281
  77.0 0.2 collective-permute-done.2
  77.2 0.8 add_convert_fusion
  78.0 0.7 broadcast_in_dim.30
  78.8 8.0 %all-to-all-start.2 = ((bf16[8,64,160]{2,1,0:T(8,128)(2,1)}), bf16[8,64,160]{2,1,0:T(8,128)(2,1)S(1)}, u32[]{:S(2)}, u32[]{:S(2)}) async-start(bf16[8,64,160]{2,1,0:T(8,128)(2,1)} %broadcast_in_dim.30), calls=%async_computation.2 | async-start | bytes 524288 | tf_op jit(solution)/shard_map/all_to_all | solution.py:251
  86.8 6.2 %collective-permute-done.5 = bf16[2,2,2,10,512]{4,1,2,3,0:T(2,128)(2,1)S(1)} collective-permute-done((bf16[2,2,2,10,512]{4,1,2,3,0:T(2,128)(2,1)S(1)}, bf16[2,2,2,10,512]{4,1,2,3,0:T(2,128)(2,1)S(1)}, u32[]{:S(2)}, u32[]{:S(2)}) %collective-permute-start.5) | collective-permute-done | bytes 81952 | tf_op jit(solution)/shard_map/ppermute | solution.py:281
  93.0 0.2 broadcast_select_fusion
  93.2 0.1 copy.34
  93.4 0.1 all-to-all-done.2.refs_0_
  93.4 2.1 %broadcast_in_dim.33 = bf16[8,2,2,2,2,10,512]{6,4,5,3,2,1,0:T(2,128)(2,1)} broadcast(bf16[2,2,2,2,10,512]{5,3,4,2,1,0:T(2,128)(2,1)S(1)} %copy.34), dimensions={1,2,3,4,5,6} | broadcast | bytes 1474560 | tf_op jit(solution)/shard_map/broadcast_in_dim | solution.py:284
  95.6 4.4 %all-to-all-start.4 = ((bf16[8,2,2,2,2,10,512]{6,4,5,3,2,1,0:T(2,128)(2,1)}), bf16[8,2,2,2,2,10,512]{6,4,5,3,2,1,0:T(2,128)(2,1)S(1)}, u32[]{:S(2)}, u32[]{:S(2)}) async-start(bf16[8,2,2,2,2,10,512]{6,4,5,3,2,1,0:T(2,128)(2,1)} %broadcast_in_dim.33), calls=%async_computation.4 | async-start | bytes 2621440 | tf_op jit(solution)/shard_map/all_to_all | solution.py:283
  100.0 1.9 %row_stats.1 = (bf16[512,160]{1,0:T(8,128)(2,1)}, f32[32,1,128]{2,1,0:T(1,128)}) custom-call(bf16[8,64,160]{2,1,0:T(8,128)(2,1)} %copy-done.1), custom_call_target="tpu_custom_call" | custom-call | tf_op jit(solution)/shard_map/row_stats/pallas_call | solution.py:32
  101.9 1.9 %collective-permute-start.3 = (bf16[512,160]{1,0:T(8,128)(2,1)}, bf16[512,160]{1,0:T(8,128)(2,1)S(1)}, u32[]{:S(2)}, u32[]{:S(2)}) collective-permute-start(bf16[512,160]{1,0:T(8,128)(2,1)} %get-tuple-element.11.refs_2_), channel_id=1, source_target_pairs={{0,16},{2,18},{16,32},{18,34},{32,48},{34,50},{48,64},{50,66},{64,... | collective-permute-start | bytes 491528 | tf_op jit(solution)/shard_map/ppermute | solution.py:277
  103.8 9.4 %collective-permute-start.4 = (bf16[512,160]{1,0:T(8,128)(2,1)}, bf16[512,160]{1,0:T(8,128)(2,1)S(1)}, u32[]{:S(2)}, u32[]{:S(2)}) collective-permute-start(bf16[512,160]{1,0:T(8,128)(2,1)} %get-tuple-element.11.refs_2_), channel_id=1, source_target_pairs={{16,0},{18,2},{32,16},{34,18},{48,32},{50,34},{64,48},{66,50},{80,... | collective-permute-start | bytes 491528 | tf_op jit(solution)/shard_map/ppermute | solution.py:278
  113.2 4.6 %all-to-all-done.4 = bf16[8,2,2,2,2,10,512]{6,4,5,3,2,1,0:T(2,128)(2,1)S(1)} async-done(((bf16[8,2,2,2,2,10,512]{6,4,5,3,2,1,0:T(2,128)(2,1)}), bf16[8,2,2,2,2,10,512]{6,4,5,3,2,1,0:T(2,128)(2,1)S(1)}, u32[]{:S(2)}, u32[]{:S(2)}) %all-to-all-start.4) | async-done | bytes 1310752 | tf_op jit(solution)/shard_map/all_to_all | solution.py:283
  117.8 12.6 %all-to-all-start.3 = ((f32[32,1,128]{2,1,0:T(1,128)}), f32[32,1,128]{2,1,0:T(1,128)S(1)}, u32[]{:S(2)}, u32[]{:S(2)}) async-start(f32[32,1,128]{2,1,0:T(1,128)} %get-tuple-element.10), calls=%async_computation.3 | async-start | bytes 32768 | tf_op jit(solution)/shard_map/all_to_all | solution.py:260
  130.4 1.2 copy.35
  131.6 1.3 copy.36.refs_0_
  132.9 3.1 %cache_conv.1 = (f32[128,160]{1,0:T(8,128)}, f32[64,160]{1,0:T(8,128)}, f32[64,160]{1,0:T(8,128)}) custom-call(bf16[2,2,2,160,512]{4,3,2,1,0:T(8,128)(2,1)} %copy.36.refs_0_, bf16[864,512]{1,0:T(8,128)(2,1)} %bitcast.43), custom_call_target="tpu_custom_call" | custom-call | tf_op jit(solution)/shard_map/cache_conv/pallas_call | solution.py:32
  136.0 3.1 %collective-permute-start.6 = (f32[64,160]{1,0:T(8,128)}, f32[64,160]{1,0:T(8,128)S(1)}, u32[]{:S(2)}, u32[]{:S(2)}) collective-permute-start(f32[64,160]{1,0:T(8,128)} %get-tuple-element.13), channel_id=1, source_target_pairs={{0,16},{16,32},{32,48},{48,64},{64,80},{80,96},{96,112},{112,128},... | collective-permute-start | bytes 122888 | tf_op jit(solution)/shard_map/ppermute | solution.py:298
  139.1 9.7 %collective-permute-start.7 = (f32[64,160]{1,0:T(8,128)}, f32[64,160]{1,0:T(8,128)S(1)}, u32[]{:S(2)}, u32[]{:S(2)}) collective-permute-start(f32[64,160]{1,0:T(8,128)} %get-tuple-element.14), channel_id=1, source_target_pairs={{16,0},{32,16},{48,32},{64,48},{80,64},{96,80},{112,96},{128,112},... | collective-permute-start | bytes 122888 | tf_op jit(solution)/shard_map/ppermute | solution.py:299
  148.8 0.8 dynamic_slice.3
  149.6 0.7 broadcast_in_dim_tile.4.refs_11_
  150.3 0.9 copy.37.refs_5_
  151.2 0.9 copy.38.refs_6_
  152.1 0.0 all-to-all-done.3.refs_1_
  152.1 0.0 collective-permute-done.3.refs_3_
  152.1 0.0 copy-start.2
  152.1 0.0 collective-permute-done.4.refs_4_
  152.1 0.0 collective-permute-done.6.refs_9_
  152.2 0.0 collective-permute-done.7.refs_10_
  152.2 0.0 copy-start.8
  152.2 0.5 copy-done.5
  152.7 0.1 copy-done.2
  152.8 0.1 copy-done.3
  152.9 0.0 copy-done.8
  152.9 3.8 %up_conv.1 = bf16[160,128]{1,0:T(8,128)(2,1)} custom-call(s32[3]{0:T(128)} %pad_add_fusion.refs_0_, f32[32,1,128]{2,1,0:T(1,128)} %copy-done.5, bf16[512,160]{1,0:T(8,128)(2,1)} %get-tuple-element.11.refs_2_, bf16[512,160]{1,0:T(8,128)(2,1)} %copy-done.2, bf16[512,160]{1,0:T(8,128)(2,1)} %copy-done.3, f32[512,1]{1,0:T(8,128)} %copy.37.refs_5_, ...), custom_call_target="tpu_custom_call" | custom-call | tf_op jit(solution)/shard_map/up_conv/pallas_call | solution.py:32
  156.7 0.8 reshape.68
  157.5 27.9 %all_to_all.30 = bf16[16,10,128]{2,1,0:T(8,128)(2,1)S(1)} all-to-all(bf16[16,10,128]{2,1,0:T(8,128)(2,1)S(1)} %reshape.68), channel_id=1, replica_groups=mesh['y'=4,'l'=8,'x'=4,'h'=2,'k'=2] {'x','h','k'}, dimensions={0} | all-to-all | bytes 81920 | tf_op jit(solution)/shard_map/all_to_all | solution.py:320
  185.4 0.1 reshape.69
  185.6 0.8 reshape.70
  (17 shorter events, 0.1 us)
Async XLA Ops:
  1.4 40.0 %collective-permute-start = (bf16[3,32,160]{2,1,0:T(8,128)(2,1)}, bf16[3,32,160]{2,1,0:T(8,128)(2,1)}, u32[]{:S(2)}, u32[]{:S(2)}) collective-permute-start(bf16[3,32,160]{2,1,0:T(8,128)(2,1)} %maximum_bitcast_fusion.refs_2_), channel_id=1, source_target_pairs={{0,16},{16,32},{32,48},{48,64},{64,80},{80,96},{96,112},{112,128},... | collective-permute-start | bytes 92168 | tf_op jit(solution)/shard_map/ppermute | solution.py:237
  4.9 36.5 %collective-permute-start.1 = (bf16[3,32,160]{2,1,0:T(8,128)(2,1)}, bf16[3,32,160]{2,1,0:T(8,128)(2,1)}, u32[]{:S(2)}, u32[]{:S(2)}) collective-permute-start(bf16[3,32,160]{2,1,0:T(8,128)(2,1)} %maximum_bitcast_fusion.refs_2_), channel_id=1, source_target_pairs={{16,0},{32,16},{48,32},{64,48},{80,64},{96,80},{112,96},{128,112},... | collective-permute-start | bytes 92168 | tf_op jit(solution)/shard_map/ppermute | solution.py:238
  17.7 23.7 %all-to-all-start = ((f32[32,1,128]{2,1,0:T(1,128)}), f32[32,1,128]{2,1,0:T(1,128)S(1)}, u32[]{:S(2)}, u32[]{:S(2)}) async-start(f32[32,1,128]{2,1,0:T(1,128)} %stats_mid.1), calls=%async_computation | async-start | bytes 32768 | tf_op jit(solution)/shard_map/all_to_all | solution.py:233
  41.4 0.6 copy-start.6
  42.0 9.1 %copy-start.11 = (f32[32]{0:T(128)S(1)}, f32[32]{0:T(128)}, u32[]{:S(2)}) copy-start(f32[32]{0:T(128)} %param.16) | copy-start | bytes 388
  42.0 32.8 %copy-start.4 = (bf16[2,2,20,512]{3,1,2,0:T(2,128)(2,1)S(1)}, bf16[2,2,20,512]{3,1,2,0:T(2,128)(2,1)}, u32[]{:S(2)}) copy-start(bf16[2,2,20,512]{3,1,2,0:T(2,128)(2,1)} %param.17) | copy-start | bytes 245764
  45.0 15.4 %all-to-all-start.1 = ((f32[8,64,160]{2,1,0:T(8,128)}), f32[8,64,160]{2,1,0:T(8,128)S(1)}, u32[]{:S(2)}, u32[]{:S(2)}) async-start(f32[8,64,160]{2,1,0:T(8,128)} %mid_conv.1), calls=%async_computation.1 | async-start | bytes 1048576 | tf_op jit(solution)/shard_map/all_to_all | solution.py:247
  60.4 0.8 copy-start
  63.0 14.2 %collective-permute-start.2 = (f32[64,160]{1,0:T(8,128)}, f32[64,160]{1,0:T(8,128)S(1)}, u32[]{:S(2)}, u32[]{:S(2)}) collective-permute-start(f32[64,160]{1,0:T(8,128)} %fold.1), channel_id=1, source_target_pairs={{0,2},{2,0},{1,3},{3,1},{4,6},{6,4},{5,7},{7,5},{8,10},{10,8},{9,1... | collective-permute-start | bytes 122888 | tf_op jit(solution)/shard_map/ppermute | solution.py:249
  74.9 18.1 %collective-permute-start.5 = (bf16[2,2,2,10,512]{4,1,2,3,0:T(2,128)(2,1)S(1)}, bf16[2,2,2,10,512]{4,1,2,3,0:T(2,128)(2,1)S(1)}, u32[]{:S(2)}, u32[]{:S(2)}) collective-permute-start(bf16[2,2,2,10,512]{4,1,2,3,0:T(2,128)(2,1)S(1)} %bitcast.49), channel_id=1, source_target_pairs={{0,2},{2,0},{1,3},{3,1},{4,6},{6,4},{5,7},{7,5},{8,10},{10,8},{9,1... | collective-permute-start | bytes 245768 | tf_op jit(solution)/shard_map/ppermute | solution.py:281
  78.8 14.7 %all-to-all-start.2 = ((bf16[8,64,160]{2,1,0:T(8,128)(2,1)}), bf16[8,64,160]{2,1,0:T(8,128)(2,1)S(1)}, u32[]{:S(2)}, u32[]{:S(2)}) async-start(bf16[8,64,160]{2,1,0:T(8,128)(2,1)} %broadcast_in_dim.30), calls=%async_computation.2 | async-start | bytes 524288 | tf_op jit(solution)/shard_map/all_to_all | solution.py:251
  93.4 2.1 %copy-start.1 = (bf16[8,64,160]{2,1,0:T(8,128)(2,1)}, bf16[8,64,160]{2,1,0:T(8,128)(2,1)S(1)}, u32[]{:S(2)}) copy-start(bf16[8,64,160]{2,1,0:T(8,128)(2,1)S(1)} %all-to-all-done.2.refs_0_) | copy-start | bytes 491524
  95.6 22.2 %all-to-all-start.4 = ((bf16[8,2,2,2,2,10,512]{6,4,5,3,2,1,0:T(2,128)(2,1)}), bf16[8,2,2,2,2,10,512]{6,4,5,3,2,1,0:T(2,128)(2,1)S(1)}, u32[]{:S(2)}, u32[]{:S(2)}) async-start(bf16[8,2,2,2,2,10,512]{6,4,5,3,2,1,0:T(2,128)(2,1)} %broadcast_in_dim.33), calls=%async_computation.4 | async-start | bytes 2621440 | tf_op jit(solution)/shard_map/all_to_all | solution.py:283
  101.9 50.2 %collective-permute-start.3 = (bf16[512,160]{1,0:T(8,128)(2,1)}, bf16[512,160]{1,0:T(8,128)(2,1)S(1)}, u32[]{:S(2)}, u32[]{:S(2)}) collective-permute-start(bf16[512,160]{1,0:T(8,128)(2,1)} %get-tuple-element.11.refs_2_), channel_id=1, source_target_pairs={{0,16},{2,18},{16,32},{18,34},{32,48},{34,50},{48,64},{50,66},{64,... | collective-permute-start | bytes 491528 | tf_op jit(solution)/shard_map/ppermute | solution.py:277
  103.8 48.3 %collective-permute-start.4 = (bf16[512,160]{1,0:T(8,128)(2,1)}, bf16[512,160]{1,0:T(8,128)(2,1)S(1)}, u32[]{:S(2)}, u32[]{:S(2)}) collective-permute-start(bf16[512,160]{1,0:T(8,128)(2,1)} %get-tuple-element.11.refs_2_), channel_id=1, source_target_pairs={{16,0},{18,2},{32,16},{34,18},{48,32},{50,34},{64,48},{66,50},{80,... | collective-permute-start | bytes 491528 | tf_op jit(solution)/shard_map/ppermute | solution.py:278
  117.8 34.3 %all-to-all-start.3 = ((f32[32,1,128]{2,1,0:T(1,128)}), f32[32,1,128]{2,1,0:T(1,128)S(1)}, u32[]{:S(2)}, u32[]{:S(2)}) async-start(f32[32,1,128]{2,1,0:T(1,128)} %get-tuple-element.10), calls=%async_computation.3 | async-start | bytes 32768 | tf_op jit(solution)/shard_map/all_to_all | solution.py:260
  132.9 17.4 %copy-start.9 = (f32[512]{0:T(512)S(1)}, f32[512]{0:T(512)}, u32[]{:S(2)}) copy-start(f32[512]{0:T(512)} %param.18) | copy-start | bytes 6148
  132.9 18.3 %copy-start.10 = (f32[512]{0:T(512)S(1)}, f32[512]{0:T(512)}, u32[]{:S(2)}) copy-start(f32[512]{0:T(512)} %param.19) | copy-start | bytes 6148
  136.0 16.1 %collective-permute-start.6 = (f32[64,160]{1,0:T(8,128)}, f32[64,160]{1,0:T(8,128)S(1)}, u32[]{:S(2)}, u32[]{:S(2)}) collective-permute-start(f32[64,160]{1,0:T(8,128)} %get-tuple-element.13), channel_id=1, source_target_pairs={{0,16},{16,32},{32,48},{48,64},{64,80},{80,96},{96,112},{112,128},... | collective-permute-start | bytes 122888 | tf_op jit(solution)/shard_map/ppermute | solution.py:298
  139.1 13.0 %collective-permute-start.7 = (f32[64,160]{1,0:T(8,128)}, f32[64,160]{1,0:T(8,128)S(1)}, u32[]{:S(2)}, u32[]{:S(2)}) collective-permute-start(f32[64,160]{1,0:T(8,128)} %get-tuple-element.14), channel_id=1, source_target_pairs={{16,0},{32,16},{48,32},{64,48},{80,64},{96,80},{112,96},{128,112},... | collective-permute-start | bytes 122888 | tf_op jit(solution)/shard_map/ppermute | solution.py:299
  152.1 0.6 copy-start.5
  152.1 0.7 copy-start.2
  152.1 0.8 copy-start.3
  152.1 0.8 copy-start.7
  152.2 0.8 copy-start.8

commit v2 on v1

--- a/solution.py
+++ b/solution.py
@@ -15,27 +15,27 @@
 USE_KERNELS = True
 
 
-def run(fn, out_shapes, args, scalars=(), name=None):
+def run(fn, out_shapes, args, name, grant=8):
     if not USE_KERNELS:
-        return fn(*scalars, *args)
-    n_s, n_a, single = len(scalars), len(args), isinstance(out_shapes, tuple)
+        return fn(*args)
+    n_a, single = len(args), isinstance(out_shapes, tuple)
     shapes = [out_shapes] if single else list(out_shapes)
 
     def body(*refs):
-        ins = list(refs[:n_s]) + [r[...] for r in refs[n_s : n_s + n_a]]
-        outs = fn(*ins)
+        outs = fn(*[r[...] for r in refs[:n_a]])
         outs = [outs] if single else outs
-        for ref, value in zip(refs[n_s + n_a :], outs):
+        for ref, value in zip(refs[n_a:], outs):
             ref[...] = value
 
     vmem = pl.BlockSpec(memory_space=pltpu.VMEM)
     res = pl.pallas_call(
         body,
         out_shape=[jax.ShapeDtypeStruct(s, d) for s, d in shapes],
-        in_specs=[pl.BlockSpec(memory_space=pltpu.SMEM)] * n_s + [vmem] * n_a,
+        in_specs=[vmem] * n_a,
         out_specs=[vmem] * len(shapes),
         name=name,
-    )(*scalars, *args)
+        compiler_params=pltpu.CompilerParams(vmem_limit_bytes=grant << 20),
+    )(*args)
     return res[0] if single else res
 
 
@@ -85,6 +85,21 @@
     return jnp.where(low, v * e, v / (1.0 + jnp.where(low, 0.0, e)))
 
 
+def wide_col(row):
+    n = row.shape[1]
+    return jnp.concatenate([to_col(row[:, i : i + 128], 1) for i in range(0, n, 128)], axis=0)
+
+
+def pack(a):
+    tail = jnp.concatenate([a[16 * i : 16 * i + 16, 128:] for i in range(4)], axis=1)
+    return jnp.concatenate([a[:, :128], tail], axis=0)
+
+
+def unpack(a):
+    tail = jnp.concatenate([a[64:, 32 * i : 32 * i + 32] for i in range(4)], axis=0)
+    return jnp.concatenate([a[:64], tail], axis=1)
+
+
 def right(a):
     return jnp.concatenate([jnp.zeros((a.shape[0], 1), a.dtype), a[:, :-1]], axis=1)
 
@@ -93,11 +108,23 @@
     return jnp.concatenate([a[:, 1:], jnp.zeros((a.shape[0], 1), a.dtype)], axis=1)
 
 
-def mid_conv(place, parts, raw, above, below, gain, bias, kernel):
+def edges(sizes):
+    n_y, n_l = sizes
+    row = lax.axis_index("y") * n_l + lax.axis_index("l")
+    return row > 0, row < n_y * n_l - 1
+
+
+def first_pass(own, cache, peers):
+    return partial_stats(own, peers), jnp.concatenate([cache, own[None]], axis=0)
+
+
+def mid_conv(parts, raw, above, below, gain, bias, kernel, sizes):
     chans, cols = raw.shape[1:]
     groups = chans // GS
     mean, scale = merge_stats(parts, groups, GS * cols)
     mean, scale = to_col(mean, GS), to_col(scale, GS)
+    gain, bias = to_col(gain, 1), to_col(bias, 1)
+    has = edges(sizes)
     pieces = []
     for t in range(3):
         for dy, src in enumerate((above, raw, below)):
@@ -105,31 +132,49 @@
             if t == 2:
                 x = norm_silu(x, mean, scale, gain, bias)
                 if dy != 1:
-                    x = jnp.where(place[0 if dy == 0 else 1] == 1, x, 0.0)
+                    x = jnp.where(has[0 if dy == 0 else 1], x, 0.0)
             pieces += [right(x).astype(BF16), x.astype(BF16), left(x).astype(BF16)]
     columns = jnp.concatenate(pieces, axis=0)
-    out = jnp.dot(kernel, columns, preferred_element_type=F32)
-    return out.reshape(8, out.shape[0] // 8, cols)
-
-
-def fold(place, parts, own, bias):
-    total = jnp.sum(parts, axis=0)
-    half = total.shape[0] // 2
-    extra = own.astype(F32) + bias
+    out = jnp.dot(columns.T, kernel, preferred_element_type=F32).T
+    blocks = []
+    for x in range(4):
+        for k in range(2):
+            both = [out[(x * 4 + h * 2 + k) * 32 :][:32] for h in range(2)]
+            blocks.append(pack(jnp.concatenate(both, axis=0)))
+    return jnp.stack(blocks)
+
+
+def fold(parts, own, bias):
+    total = unpack(jnp.sum(parts, axis=0))
+    extra = own.astype(F32) + to_col(bias, 1)
     zero = jnp.zeros_like(extra)
-    first = place[2] == 0
-    return total + jnp.concatenate(
-        [jnp.where(first, extra, zero), jnp.where(first, zero, extra)], axis=0
+    first = lax.axis_index("h") == 0
+    return pack(
+        total
+        + jnp.concatenate([jnp.where(first, extra, zero), jnp.where(first, zero, extra)], axis=0)
+    )
+
+
+def merge(mine, other):
+    merged = (mine + other).astype(BF16)
+    return jnp.broadcast_to(merged[None], (8,) + merged.shape)
+
+
+def rows_of(gathered):
+    blocks = [unpack(gathered[i].astype(F32)) for i in range(8)]
+    return jnp.concatenate(
+        [
+            blocks[x * 2 + k][h * 32 : (h + 1) * 32]
+            for x in range(4)
+            for h in range(2)
+            for k in range(2)
+        ],
+        axis=0,
     )
 
 
 def row_stats(gathered, peers):
-    cols = gathered.shape[2]
-    blocks = gathered.reshape(4, 2, 2, 32, cols)
-    row = jnp.concatenate(
-        [blocks[x, k, h] for x in range(4) for h in range(2) for k in range(2)], axis=0
-    )
-    return row, partial_stats(row, peers)
+    return partial_stats(rows_of(gathered), peers)
 
 
 def taps(prod):
@@ -173,33 +218,39 @@
     return jnp.concatenate([out(0), out(1)], axis=0), out(-1), out(2)
 
 
-def up_conv(place, parts, row, above, below, gain, bias, kernel, held, from_above, from_below, out_bias):
+def up_conv(parts, row, above, below, gain, bias, kernel, held, from_above, from_below, out_bias, sizes):
+    row, above, below = rows_of(row), rows_of(above), rows_of(below)
     chans, cols = row.shape
     groups = chans // GS
     mean, scale = merge_stats(parts, groups, GS * cols)
     mean, scale = to_col(mean, GS), to_col(scale, GS)
+    gain, bias = wide_col(gain), wide_col(bias)
+    has = edges(sizes)
     per = 9 * 32
     w = kernel[2 * per :]
 
     def image(x, keep=None):
         v = norm_silu(x, mean, scale, gain, bias)
         if keep is not None:
-            v = jnp.where(keep == 1, v, 0.0)
+            v = jnp.where(keep, v, 0.0)
         return v.astype(BF16)
 
     lhs = jnp.concatenate([w[dy * 3 * 32 : (dy + 1) * 3 * 32] for dy in range(3)], axis=1)
     here = image(row)
     outs = []
-    for images in (
-        (image(above, place[0]), here, here),
-        (here, here, image(below, place[1])),
-    ):
+    for images in ((image(above, has[0]), here, here), (here, here, image(below, has[1]))):
         prod = jnp.dot(lhs, jnp.concatenate(images, axis=0), preferred_element_type=F32)
         cut = [prod[dx * 32 : (dx + 1) * 32] for dx in range(3)]
         outs += [right(cut[0]) + cut[1] + cut[2], cut[0] + cut[1] + left(cut[2])]
     total = jnp.concatenate(outs, axis=0) + held
-    total = total + jnp.concatenate([from_above, from_below], axis=0) + out_bias
-    return total.T.astype(BF16)
+    chan = lax.axis_index("x") * 4 + lax.axis_index("h") * 2 + lax.axis_index("k")
+    rows = lax.broadcasted_iota(jnp.int32, (32, chans), 0)
+    lanes = lax.broadcasted_iota(jnp.int32, (32, chans), 1)
+    picked = jnp.sum(jnp.where(lanes == rows + chan * 32, out_bias, 0.0), axis=1, keepdims=True)
+    total = total + jnp.concatenate([from_above, from_below], axis=0)
+    total = (total + jnp.concatenate([picked] * 4, axis=0)).T
+    part = cols // 16
+    return jnp.stack([total[c * part : (c + 1) * part] for c in range(16)]).astype(BF16)
 
 
 def on_device(
@@ -219,43 +270,34 @@
     n_y, n_l = sizes
     peers = n_y * n_l
     cols, chans = latent.shape[2], latent.shape[3]
-    place_s = lax.axis_index(("y", "l"))
+    sizes = (n_y, n_l)
     hi = lax.axis_index("h")
-    chan = lax.axis_index(("x", "h", "k"))
-    place = jnp.stack(
-        [(place_s > 0).astype(jnp.int32), (place_s < peers - 1).astype(jnp.int32), hi.astype(jnp.int32)]
-    )
     space = ("y", "l")
     own = latent[0, 0].T
-    stats = run(
-        functools.partial(partial_stats, peers=peers), ((peers, 1, 128), F32), (own,), name="stats_mid"
+    stats, raw = run(
+        functools.partial(first_pass, peers=peers),
+        [((peers, 1, 128), F32), ((3, chans, cols), BF16)],
+        (own, cache_mid[:, 0].transpose(0, 2, 1)),
+        "first_pass",
     )
     stats = lax.all_to_all(stats, space, 0, 0, tiled=True)
-    raw = jnp.concatenate([cache_mid[:, 0], latent[0]], axis=0).transpose(0, 2, 1)
     down = [(i, i + 1) for i in range(peers - 1)]
     up = [(i + 1, i) for i in range(peers - 1)]
     above = lax.ppermute(raw, space, down)
     below = lax.ppermute(raw, space, up)
-    kernel1 = conv1_weight.reshape(27 * chans, 4, 2, 2, 32).transpose(1, 3, 2, 4, 0).reshape(512, -1)
     partial = run(
-        mid_conv,
-        ((8, 64, cols), F32),
-        (stats, raw, above, below, norm1_gain[:, None], norm1_bias[:, None], kernel1),
-        (place,),
-        name="mid_conv",
+        functools.partial(mid_conv, sizes=sizes),
+        ((8, 80, 128), F32),
+        (stats, raw, above, below, norm1_gain[None], norm1_bias[None], conv1_weight.reshape(27 * chans, 512)),
+        "mid_conv",
     )
     partial = lax.all_to_all(partial, ("x", "k"), 0, 0, tiled=True)
-    mine = run(fold, ((64, cols), F32), (partial, own, conv1_bias[:, None]), (place,), name="fold")
+    mine = run(fold, ((80, 128), F32), (partial, own, conv1_bias[None]), "fold")
     other = lax.ppermute(mine, "h", [(0, 1), (1, 0)])
-    merged = (mine + other).astype(BF16)
-    gathered = lax.all_to_all(
-        jnp.broadcast_to(merged[None], (8, 64, cols)), ("x", "k"), 0, 0, tiled=True
-    )
-    row, stats2 = run(
-        functools.partial(row_stats, peers=peers),
-        [((512, cols), BF16), ((peers, 1, 128), F32)],
-        (gathered,),
-        name="row_stats",
+    gathered = run(merge, ((8, 80, 128), BF16), (mine, other), "merge")
+    gathered = lax.all_to_all(gathered, ("x", "k"), 0, 0, tiled=True)
+    stats2 = run(
+        functools.partial(row_stats, peers=peers), ((peers, 1, 128), F32), (gathered,), "row_stats"
     )
     stats2 = lax.all_to_all(stats2, space, 0, 0, tiled=True)
 
@@ -274,8 +316,8 @@
                     continue
                 down_h.append(pair)
                 up_h.append(pair[::-1])
-    row_above = lax.ppermute(row, ("y", "l", "h"), down_h)
-    row_below = lax.ppermute(row, ("y", "l", "h"), up_h)
+    row_above = lax.ppermute(gathered, ("y", "l", "h"), down_h)
+    row_below = lax.ppermute(gathered, ("y", "l", "h"), up_h)
 
     tile = cache_up.reshape(2, 2, 10, 2, 512).transpose(0, 1, 3, 2, 4)
     swapped = lax.ppermute(tile, "h", [(0, 1), (1, 0)])
@@ -293,31 +335,31 @@
         cache_conv,
         [((128, cols), F32), ((64, cols), F32), ((64, cols), F32)],
         (images, kernel2),
-        name="cache_conv",
+        "cache_conv",
+        16,
     )
     from_above = lax.ppermute(to_below, space, down)
     from_below = lax.ppermute(to_above, space, up)
-    bias_here = lax.dynamic_slice_in_dim(conv2_bias, chan * 32, 32)
     out = run(
-        up_conv,
-        ((cols, 128), BF16),
+        functools.partial(up_conv, sizes=sizes),
+        ((16, cols // 16, 128), BF16),
         (
             stats2,
-            row,
+            gathered,
             row_above,
             row_below,
-            norm2_gain[:, None],
-            norm2_bias[:, None],
+            norm2_gain[None],
+            norm2_bias[None],
             kernel2,
             held,
             from_above,
             from_below,
-            jnp.tile(bias_here, 4)[:, None],
+            conv2_bias[None],
         ),
-        (place,),
-        name="up_conv",
-    )
-    out = lax.all_to_all(out.reshape(16, 10, 128), ("x", "h", "k"), 0, 0, tiled=True)
+        "up_conv",
+        16,
+    )
+    out = lax.all_to_all(out, ("x", "h", "k"), 0, 0, tiled=True)
     out = out.reshape(16, 10, 2, 2, 32).transpose(2, 1, 3, 0, 4)
     return out.reshape(1, 2, 20, 512)
 

time: 187 us -> 158 us (0.84)
  local copies, waits for them, and re-layouts: 30.3 us -> 9.49 us
  waiting for transfers between devices: 19.7 us -> 34.7 us
  starting transfers between devices: 90.1 us -> 81.9 us
  Pallas kernels: 15.1 us -> 7.03 us
  blocking collectives: 27.9 us -> 23.7 us
  other arithmetic: 3.07 us -> 0.24 us
    ppermute x1, waiting for transfers between devices: 0.01 us -> 10.4 us  [on_device(): above = lax.ppermute(raw, space, down)]
    all_to_all x1, starting transfers between devices: 6.22 us -> 15.2 us  [on_device(): stats = lax.all_to_all(stats, space, 0, 0, tiled=True)]
    all_to_all x1, waiting for transfers between devices: 8.66 us -> 0.01 us  [on_device(): partial = lax.all_to_all(partial, ('x', 'k'), 0, 0, tiled=True)]
    reshape x2 -> x0, local copies, waits for them, and re-layouts: 8.6 us -> none  [the longest x1 7.81 us: on_device(): conv1_weight.reshape(27 * chans, 4, 2, 2, 32).transpose(1, 3, 2, 4, 0)]
    all_to_all x1, starting transfers between devices: 12.6 us -> 4.44 us  [on_device(): stats2 = lax.all_to_all(stats2, space, 0, 0, tiled=True)]
    pallas_call x6 -> x7, Pallas kernels: 15.1 us -> 7.03 us  [run(): pl.pallas_call(body, out_shape=[jax.ShapeDtypeStruct(s, d) for s, d in sh...]
    all_to_all x1, waiting for transfers between devices: 4.56 us -> 11.5 us  [on_device(): lax.all_to_all(jnp.broadcast_to(pair[None], (8,) + pair.shape), ('x', 'k'...]
    transpose x1 -> x0, local copies, waits for them, and re-layouts: 6.43 us -> none  [on_device(): conv1_weight.reshape(27 * chans, 4, 2, 2, 32).transpose(1, 3, 2, 4, 0)]
  transfers between devices with their start and end apart: 13 -> 13, of which waited for: 5 -> 5; matrix products, arithmetic and copies ran while one was open for 14% -> 1% of each run, Pallas kernels for 4% -> 2%
where the time goes in v2:
time: 158 us; the launch traced here: 157 us
  starting transfers between devices  81.9 us (52%)
  waiting for transfers between devices  34.7 us (22%)
  blocking collectives  23.7 us (15%)
  local copies, waits for them, and re-layouts  9.49 us (6%)
  Pallas kernels  7.03 us (4%)
    all_to_all x1, blocking collectives, on_device(): out = lax.all_to_all(out, ('x', 'h', 'k'), 0, 0, tiled=True)  23.7 us
    all_to_all x1, starting transfers between devices, on_device(): stats = lax.all_to_all(stats, space, 0, 0, tiled=True)  15.2 us
    all_to_all x1, waiting for transfers between devices, on_device(): lax.all_to_all(jnp.broadcast_to(pair[None], (8,) + pair.shape), ('x', 'k'...  11.5 us
    ppermute x1, waiting for transfers between devices, on_device(): above = lax.ppermute(raw, space, down)  10.4 us
    ppermute x1, starting transfers between devices, on_device(): below = lax.ppermute(raw, space, up)  9.69 us
    ppermute x1, starting transfers between devices, on_device(): from_below = lax.ppermute(to_above, space, up)  9.69 us
    ppermute x1, starting transfers between devices, on_device(): swapped = lax.ppermute(tile, 'h', [(0, 1), (1, 0)])  7.93 us
    ppermute x1, starting transfers between devices, on_device(): other = lax.ppermute(mine, 'h', [(0, 1), (1, 0)])  7.05 us
  transfers between devices with their start and end apart: 13, of which 5 were waited for; matrix products, arithmetic and copies ran while one was open for 1% of the time, Pallas kernels for 2%

profile of v2, /device:TPU:9, one launch (start us, length us, event | category | flops | bytes accessed | tf_op | source)
XLA Modules:
  0.0 157.3 jit_solution(15202768403114165894)
XLA Ops:
  0.0 0.0 copy-start.10
  0.0 0.0 copy-start.2
  0.0 0.7 copy-done.2
  0.7 0.0 copy-start.4
  0.7 0.8 copy-done.4
  1.5 0.0 copy-start.3
  1.5 0.9 first_pass.1
  2.4 15.2 %all-to-all-start = ((f32[32,1,128]{2,1,0:T(1,128)}), f32[32,1,128]{2,1,0:T(1,128)S(1)}, u32[]{:S(2)}, u32[]{:S(2)}) async-start(f32[32,1,128]{2,1,0:T(1,128)} %get-tuple-element.10), calls=%async_computation | async-start | bytes 32768 | tf_op jit(solution)/shard_map/all_to_all | solution.py:283
  17.6 9.7 %collective-permute-start.1 = (bf16[3,32,160]{2,1,0:T(8,128)(2,1)S(1)}, bf16[3,32,160]{2,1,0:T(8,128)(2,1)S(1)}, u32[]{:S(2)}, u32[]{:S(2)}) collective-permute-start(bf16[3,32,160]{2,1,0:T(8,128)(2,1)S(1)} %get-tuple-element.11.refs_1_), channel_id=1, source_target_pairs={{16,0},{32,16},{48,32},{64,48},{80,64},{96,80},{112,96},{128,112},... | collective-permute-start | bytes 92168 | tf_op jit(solution)/shard_map/ppermute | solution.py:287
  27.3 1.9 %collective-permute-start = (bf16[3,32,160]{2,1,0:T(8,128)(2,1)S(1)}, bf16[3,32,160]{2,1,0:T(8,128)(2,1)S(1)}, u32[]{:S(2)}, u32[]{:S(2)}) collective-permute-start(bf16[3,32,160]{2,1,0:T(8,128)(2,1)S(1)} %get-tuple-element.11.refs_1_), channel_id=1, source_target_pairs={{0,16},{16,32},{32,48},{48,64},{64,80},{80,96},{96,112},{112,128},... | collective-permute-start | bytes 92168 | tf_op jit(solution)/shard_map/ppermute | solution.py:286
  29.2 0.0 collective-permute-done.1.refs_3_
  29.2 10.4 %collective-permute-done.refs_2_ = bf16[3,32,160]{2,1,0:T(8,128)(2,1)S(1)} collective-permute-done((bf16[3,32,160]{2,1,0:T(8,128)(2,1)S(1)}, bf16[3,32,160]{2,1,0:T(8,128)(2,1)S(1)}, u32[]{:S(2)}, u32[]{:S(2)}) %collective-permute-start) | collective-permute-done | bytes 30752 | tf_op jit(solution)/shard_map/ppermute | solution.py:286
  39.6 0.0 all-to-all-done.refs_0_
  39.6 1.2 copy-done.1
  40.8 0.0 copy-start.8
  40.8 0.7 copy-done.8
  41.4 0.0 copy-start.9
  41.4 0.7 copy-done.9
  42.1 0.0 copy-start.11
  42.1 1.7 %mid_conv.1 = f32[8,80,128]{2,1,0:T(8,128)} custom-call(f32[32,1,128]{2,1,0:T(1,128)S(1)} %all-to-all-done.refs_0_, bf16[3,32,160]{2,1,0:T(8,128)(2,1)S(1)} %get-tuple-element.11.refs_1_, bf16[3,32,160]{2,1,0:T(8,128)(2,1)S(1)} %collective-permute-done.refs_2_, bf16[3,32,160]{2,1,0:T(8,128)(2,1)S(1)} %collective-permute-done.1.refs_3_, ...), custom_call_target="tpu_custom_call" | custom-call | tf_op jit(solution)/shard_map/mid_conv/pallas_call | solution.py:31
  43.8 7.0 %all-to-all-start.1 = ((f32[8,80,128]{2,1,0:T(8,128)}), f32[8,80,128]{2,1,0:T(8,128)S(1)}, u32[]{:S(2)}, u32[]{:S(2)}) async-start(f32[8,80,128]{2,1,0:T(8,128)} %mid_conv.1), calls=%async_computation.1 | async-start | bytes 655360 | tf_op jit(solution)/shard_map/all_to_all | solution.py:294
  50.7 0.0 copy-done.11
  50.8 7.9 %collective-permute-start.5 = (bf16[2,2,2,10,512]{4,1,2,3,0:T(2,128)(2,1)S(1)}, bf16[2,2,2,10,512]{4,1,2,3,0:T(2,128)(2,1)S(1)}, u32[]{:S(2)}, u32[]{:S(2)}) collective-permute-start(bf16[2,2,2,10,512]{4,1,2,3,0:T(2,128)(2,1)S(1)} %bitcast.48), channel_id=1, source_target_pairs={{0,2},{2,0},{1,3},{3,1},{4,6},{6,4},{5,7},{7,5},{8,10},{10,8},{9,1... | collective-permute-start | bytes 245768 | tf_op jit(solution)/shard_map/ppermute | solution.py:323
  58.7 0.0 all-to-all-done.1.refs_0_
  58.7 0.0 copy-done.10
  58.7 0.0 copy-done.3
  58.7 0.2 fold.1.refs_0_
  58.9 7.1 %collective-permute-start.2 = (f32[80,128]{1,0:T(8,128)S(1)}, f32[80,128]{1,0:T(8,128)S(1)}, u32[]{:S(2)}, u32[]{:S(2)}) collective-permute-start(f32[80,128]{1,0:T(8,128)S(1)} %fold.1.refs_0_), channel_id=1, source_target_pairs={{0,2},{2,0},{1,3},{3,1},{4,6},{6,4},{5,7},{7,5},{8,10},{10,8},{9,1... | collective-permute-start | bytes 122888 | tf_op jit(solution)/shard_map/ppermute | solution.py:296
  65.9 6.4 %collective-permute-done.2.refs_1_ = f32[80,128]{1,0:T(8,128)S(1)} collective-permute-done((f32[80,128]{1,0:T(8,128)S(1)}, f32[80,128]{1,0:T(8,128)S(1)}, u32[]{:S(2)}, u32[]{:S(2)}) %collective-permute-start.2) | collective-permute-done | bytes 40992 | tf_op jit(solution)/shard_map/ppermute | solution.py:296
  72.3 0.7 merge.1
  73.0 6.2 %all-to-all-start.2 = ((bf16[8,80,128]{2,1,0:T(8,128)(2,1)}), bf16[8,80,128]{2,1,0:T(8,128)(2,1)S(1)}, u32[]{:S(2)}, u32[]{:S(2)}) async-start(bf16[8,80,128]{2,1,0:T(8,128)(2,1)} %merge.1), calls=%async_computation.2 | async-start | bytes 327680 | tf_op jit(solution)/shard_map/all_to_all | solution.py:298
  79.3 0.0 collective-permute-done.5
  79.3 0.2 broadcast_select_fusion
  79.5 0.1 copy.18
  79.6 5.2 %all-to-all-done.2.refs_0_.refs_1_ = bf16[8,80,128]{2,1,0:T(8,128)(2,1)S(1)} async-done(((bf16[8,80,128]{2,1,0:T(8,128)(2,1)}), bf16[8,80,128]{2,1,0:T(8,128)(2,1)S(1)}, u32[]{:S(2)}, u32[]{:S(2)}) %all-to-all-start.2) | async-done | bytes 163872 | tf_op jit(solution)/shard_map/all_to_all | solution.py:298
  84.8 2.1 %broadcast_in_dim.29 = bf16[8,2,2,2,2,10,512]{6,4,5,3,2,1,0:T(2,128)(2,1)} broadcast(bf16[2,2,2,2,10,512]{5,3,4,2,1,0:T(2,128)(2,1)S(1)} %copy.18), dimensions={1,2,3,4,5,6} | broadcast | bytes 1474560 | tf_op jit(solution)/shard_map/broadcast_in_dim | solution.py:326
  86.9 4.4 %all-to-all-start.4 = ((bf16[8,2,2,2,2,10,512]{6,4,5,3,2,1,0:T(2,128)(2,1)}), bf16[8,2,2,2,2,10,512]{6,4,5,3,2,1,0:T(2,128)(2,1)S(1)}, u32[]{:S(2)}, u32[]{:S(2)}) async-start(bf16[8,2,2,2,2,10,512]{6,4,5,3,2,1,0:T(2,128)(2,1)} %broadcast_in_dim.29), calls=%async_computation.4 | async-start | bytes 2621440 | tf_op jit(solution)/shard_map/all_to_all | solution.py:325
  91.3 1.9 %collective-permute-start.4 = (bf16[8,80,128]{2,1,0:T(8,128)(2,1)S(1)}, bf16[8,80,128]{2,1,0:T(8,128)(2,1)S(1)}, u32[]{:S(2)}, u32[]{:S(2)}) collective-permute-start(bf16[8,80,128]{2,1,0:T(8,128)(2,1)S(1)} %all-to-all-done.2.refs_0_.refs_1_), channel_id=1, source_target_pairs={{16,0},{18,2},{32,16},{34,18},{48,32},{50,34},{64,48},{66,50},{80,... | collective-permute-start | bytes 491528 | tf_op jit(solution)/shard_map/ppermute | solution.py:320
  93.2 3.4 %collective-permute-start.3 = (bf16[8,80,128]{2,1,0:T(8,128)(2,1)S(1)}, bf16[8,80,128]{2,1,0:T(8,128)(2,1)S(1)}, u32[]{:S(2)}, u32[]{:S(2)}) collective-permute-start(bf16[8,80,128]{2,1,0:T(8,128)(2,1)S(1)} %all-to-all-done.2.refs_0_.refs_1_), channel_id=1, source_target_pairs={{0,16},{2,18},{16,32},{18,34},{32,48},{34,50},{48,64},{50,66},{64,... | collective-permute-start | bytes 491528 | tf_op jit(solution)/shard_map/ppermute | solution.py:319
  96.6 1.0 row_stats.1
  97.6 11.5 %all-to-all-done.4 = bf16[8,2,2,2,2,10,512]{6,4,5,3,2,1,0:T(2,128)(2,1)S(1)} async-done(((bf16[8,2,2,2,2,10,512]{6,4,5,3,2,1,0:T(2,128)(2,1)}), bf16[8,2,2,2,2,10,512]{6,4,5,3,2,1,0:T(2,128)(2,1)S(1)}, u32[]{:S(2)}, u32[]{:S(2)}) %all-to-all-start.4) | async-done | bytes 1310752 | tf_op jit(solution)/shard_map/all_to_all | solution.py:325
  109.1 4.4 %all-to-all-start.3 = ((f32[32,1,128]{2,1,0:T(1,128)}), f32[32,1,128]{2,1,0:T(1,128)S(1)}, u32[]{:S(2)}, u32[]{:S(2)}) async-start(f32[32,1,128]{2,1,0:T(1,128)} %row_stats.1), calls=%async_computation.3 | async-start | bytes 32768 | tf_op jit(solution)/shard_map/all_to_all | solution.py:302
  113.5 1.2 copy.19
  114.7 0.0 copy-start
  114.8 0.2 copy.20.refs_0_
  115.0 0.0 copy-start.5
  115.0 0.0 copy-start.6
  115.0 0.0 copy-start.7
  115.0 0.9 copy-done
  115.9 0.8 cache_conv.1
  116.8 3.1 %collective-permute-start.6 = (f32[64,160]{1,0:T(8,128)S(1)}, f32[64,160]{1,0:T(8,128)S(1)}, u32[]{:S(2)}, u32[]{:S(2)}) collective-permute-start(f32[64,160]{1,0:T(8,128)S(1)} %get-tuple-element.13), channel_id=1, source_target_pairs={{0,16},{16,32},{32,48},{48,64},{64,80},{80,96},{96,112},{112,128},... | collective-permute-start | bytes 122888 | tf_op jit(solution)/shard_map/ppermute | solution.py:341
  119.9 9.7 %collective-permute-start.7 = (f32[64,160]{1,0:T(8,128)S(1)}, f32[64,160]{1,0:T(8,128)S(1)}, u32[]{:S(2)}, u32[]{:S(2)}) collective-permute-start(f32[64,160]{1,0:T(8,128)S(1)} %get-tuple-element.14), channel_id=1, source_target_pairs={{16,0},{32,16},{48,32},{64,48},{80,64},{96,80},{112,96},{128,112},... | collective-permute-start | bytes 122888 | tf_op jit(solution)/shard_map/ppermute | solution.py:342
  129.6 0.0 all-to-all-done.3.refs_0_
  129.6 0.0 collective-permute-done.4.refs_3_
  129.6 0.0 collective-permute-done.3.refs_2_
  129.6 0.0 collective-permute-done.6.refs_8_
  129.6 1.3 collective-permute-done.7.refs_9_
  130.9 0.0 copy-done.5
  130.9 0.0 copy-done.6
  130.9 0.0 copy-done.7
  130.9 1.7 %up_conv.1 = bf16[16,10,128]{2,1,0:T(8,128)(2,1)S(1)} custom-call(f32[32,1,128]{2,1,0:T(1,128)S(1)} %all-to-all-done.3.refs_0_, bf16[8,80,128]{2,1,0:T(8,128)(2,1)S(1)} %all-to-all-done.2.refs_0_.refs_1_, bf16[8,80,128]{2,1,0:T(8,128)(2,1)S(1)} %collective-permute-done.3.refs_2_, bf16[8,80,128]{2,1,0:T(8,128)(2,1)S(1)} %collective-permute-done.4.refs_3_, ...), custom_call_target="tpu_custom_call" | custom-call | tf_op jit(solution)/shard_map/up_conv/pallas_call | solution.py:31
  132.6 23.7 %all_to_all.30 = bf16[16,10,128]{2,1,0:T(8,128)(2,1)S(1)} all-to-all(bf16[16,10,128]{2,1,0:T(8,128)(2,1)S(1)} %up_conv.1), channel_id=1, replica_groups=mesh['y'=4,'l'=8,'x'=4,'h'=2,'k'=2] {'x','h','k'}, dimensions={0} | all-to-all | bytes 81920 | tf_op jit(solution)/shard_map/all_to_all | solution.py:362
  156.3 0.1 reshape.59
  156.5 0.8 reshape.60
  (3 shorter events, 0.0 us)
Async XLA Ops:
  0.0 58.7 %copy-start.10 = (f32[32]{0:T(128)S(1)}, f32[32]{0:T(128)}, u32[]{:S(2)}) copy-start(f32[32]{0:T(128)} %param.16) | copy-start | bytes 388
  0.0 0.7 copy-start.2
  0.7 0.8 copy-start.4
  1.5 57.2 %copy-start.3 = (bf16[1,1,160,32]{2,3,1,0:T(8,128)(2,1)S(1)}, bf16[1,1,160,32]{2,3,1,0:T(8,128)(2,1)}, u32[]{:S(2)}) copy-start(bf16[1,1,160,32]{2,3,1,0:T(8,128)(2,1)} %param.11) | copy-start | bytes 30724
  2.4 37.3 %all-to-all-start = ((f32[32,1,128]{2,1,0:T(1,128)}), f32[32,1,128]{2,1,0:T(1,128)S(1)}, u32[]{:S(2)}, u32[]{:S(2)}) async-start(f32[32,1,128]{2,1,0:T(1,128)} %get-tuple-element.10), calls=%async_computation | async-start | bytes 32768 | tf_op jit(solution)/shard_map/all_to_all | solution.py:283
  17.6 11.6 %collective-permute-start.1 = (bf16[3,32,160]{2,1,0:T(8,128)(2,1)S(1)}, bf16[3,32,160]{2,1,0:T(8,128)(2,1)S(1)}, u32[]{:S(2)}, u32[]{:S(2)}) collective-permute-start(bf16[3,32,160]{2,1,0:T(8,128)(2,1)S(1)} %get-tuple-element.11.refs_1_), channel_id=1, source_target_pairs={{16,0},{32,16},{48,32},{64,48},{80,64},{96,80},{112,96},{128,112},... | collective-permute-start | bytes 92168 | tf_op jit(solution)/shard_map/ppermute | solution.py:287
  27.3 12.3 %collective-permute-start = (bf16[3,32,160]{2,1,0:T(8,128)(2,1)S(1)}, bf16[3,32,160]{2,1,0:T(8,128)(2,1)S(1)}, u32[]{:S(2)}, u32[]{:S(2)}) collective-permute-start(bf16[3,32,160]{2,1,0:T(8,128)(2,1)S(1)} %get-tuple-element.11.refs_1_), channel_id=1, source_target_pairs={{0,16},{16,32},{32,48},{48,64},{64,80},{80,96},{96,112},{112,128},... | collective-permute-start | bytes 92168 | tf_op jit(solution)/shard_map/ppermute | solution.py:286
  39.6 1.2 copy-start.1
  40.8 0.7 copy-start.8
  41.4 0.7 copy-start.9
  42.1 8.7 %copy-start.11 = (bf16[2,2,20,512]{3,1,2,0:T(2,128)(2,1)S(1)}, bf16[2,2,20,512]{3,1,2,0:T(2,128)(2,1)}, u32[]{:S(2)}) copy-start(bf16[2,2,20,512]{3,1,2,0:T(2,128)(2,1)} %param.17) | copy-start | bytes 245764
  43.8 14.9 %all-to-all-start.1 = ((f32[8,80,128]{2,1,0:T(8,128)}), f32[8,80,128]{2,1,0:T(8,128)S(1)}, u32[]{:S(2)}, u32[]{:S(2)}) async-start(f32[8,80,128]{2,1,0:T(8,128)} %mid_conv.1), calls=%async_computation.1 | async-start | bytes 655360 | tf_op jit(solution)/shard_map/all_to_all | solution.py:294
  50.8 28.5 %collective-permute-start.5 = (bf16[2,2,2,10,512]{4,1,2,3,0:T(2,128)(2,1)S(1)}, bf16[2,2,2,10,512]{4,1,2,3,0:T(2,128)(2,1)S(1)}, u32[]{:S(2)}, u32[]{:S(2)}) collective-permute-start(bf16[2,2,2,10,512]{4,1,2,3,0:T(2,128)(2,1)S(1)} %bitcast.48), channel_id=1, source_target_pairs={{0,2},{2,0},{1,3},{3,1},{4,6},{6,4},{5,7},{7,5},{8,10},{10,8},{9,1... | collective-permute-start | bytes 245768 | tf_op jit(solution)/shard_map/ppermute | solution.py:323
  58.9 13.5 %collective-permute-start.2 = (f32[80,128]{1,0:T(8,128)S(1)}, f32[80,128]{1,0:T(8,128)S(1)}, u32[]{:S(2)}, u32[]{:S(2)}) collective-permute-start(f32[80,128]{1,0:T(8,128)S(1)} %fold.1.refs_0_), channel_id=1, source_target_pairs={{0,2},{2,0},{1,3},{3,1},{4,6},{6,4},{5,7},{7,5},{8,10},{10,8},{9,1... | collective-permute-start | bytes 122888 | tf_op jit(solution)/shard_map/ppermute | solution.py:296
  73.0 11.8 %all-to-all-start.2 = ((bf16[8,80,128]{2,1,0:T(8,128)(2,1)}), bf16[8,80,128]{2,1,0:T(8,128)(2,1)S(1)}, u32[]{:S(2)}, u32[]{:S(2)}) async-start(bf16[8,80,128]{2,1,0:T(8,128)(2,1)} %merge.1), calls=%async_computation.2 | async-start | bytes 327680 | tf_op jit(solution)/shard_map/all_to_all | solution.py:298
  86.9 22.2 %all-to-all-start.4 = ((bf16[8,2,2,2,2,10,512]{6,4,5,3,2,1,0:T(2,128)(2,1)}), bf16[8,2,2,2,2,10,512]{6,4,5,3,2,1,0:T(2,128)(2,1)S(1)}, u32[]{:S(2)}, u32[]{:S(2)}) async-start(bf16[8,2,2,2,2,10,512]{6,4,5,3,2,1,0:T(2,128)(2,1)} %broadcast_in_dim.29), calls=%async_computation.4 | async-start | bytes 2621440 | tf_op jit(solution)/shard_map/all_to_all | solution.py:325
  91.3 38.3 %collective-permute-start.4 = (bf16[8,80,128]{2,1,0:T(8,128)(2,1)S(1)}, bf16[8,80,128]{2,1,0:T(8,128)(2,1)S(1)}, u32[]{:S(2)}, u32[]{:S(2)}) collective-permute-start(bf16[8,80,128]{2,1,0:T(8,128)(2,1)S(1)} %all-to-all-done.2.refs_0_.refs_1_), channel_id=1, source_target_pairs={{16,0},{18,2},{32,16},{34,18},{48,32},{50,34},{64,48},{66,50},{80,... | collective-permute-start | bytes 491528 | tf_op jit(solution)/shard_map/ppermute | solution.py:320
  93.2 36.4 %collective-permute-start.3 = (bf16[8,80,128]{2,1,0:T(8,128)(2,1)S(1)}, bf16[8,80,128]{2,1,0:T(8,128)(2,1)S(1)}, u32[]{:S(2)}, u32[]{:S(2)}) collective-permute-start(bf16[8,80,128]{2,1,0:T(8,128)(2,1)S(1)} %all-to-all-done.2.refs_0_.refs_1_), channel_id=1, source_target_pairs={{0,16},{2,18},{16,32},{18,34},{32,48},{34,50},{48,64},{50,66},{64,... | collective-permute-start | bytes 491528 | tf_op jit(solution)/shard_map/ppermute | solution.py:319
  109.1 20.5 %all-to-all-start.3 = ((f32[32,1,128]{2,1,0:T(1,128)}), f32[32,1,128]{2,1,0:T(1,128)S(1)}, u32[]{:S(2)}, u32[]{:S(2)}) async-start(f32[32,1,128]{2,1,0:T(1,128)} %row_stats.1), calls=%async_computation.3 | async-start | bytes 32768 | tf_op jit(solution)/shard_map/all_to_all | solution.py:302
  114.7 1.2 copy-start
  115.0 15.9 %copy-start.5 = (f32[512]{0:T(512)S(1)}, f32[512]{0:T(512)}, u32[]{:S(2)}) copy-start(f32[512]{0:T(512)} %param.18) | copy-start | bytes 6148
  115.0 15.9 %copy-start.6 = (f32[512]{0:T(512)S(1)}, f32[512]{0:T(512)}, u32[]{:S(2)}) copy-start(f32[512]{0:T(512)} %param.19) | copy-start | bytes 6148
  115.0 15.9 %copy-start.7 = (f32[512]{0:T(512)S(1)}, f32[512]{0:T(512)}, u32[]{:S(2)}) copy-start(f32[512]{0:T(512)} %param.21) | copy-start | bytes 6148
  116.8 12.8 %collective-permute-start.6 = (f32[64,160]{1,0:T(8,128)S(1)}, f32[64,160]{1,0:T(8,128)S(1)}, u32[]{:S(2)}, u32[]{:S(2)}) collective-permute-start(f32[64,160]{1,0:T(8,128)S(1)} %get-tuple-element.13), channel_id=1, source_target_pairs={{0,16},{16,32},{32,48},{48,64},{64,80},{80,96},{96,112},{112,128},... | collective-permute-start | bytes 122888 | tf_op jit(solution)/shard_map/ppermute | solution.py:341
  119.9 11.0 %collective-permute-start.7 = (f32[64,160]{1,0:T(8,128)S(1)}, f32[64,160]{1,0:T(8,128)S(1)}, u32[]{:S(2)}, u32[]{:S(2)}) collective-permute-start(f32[64,160]{1,0:T(8,128)S(1)} %get-tuple-element.14), channel_id=1, source_target_pairs={{16,0},{32,16},{48,32},{64,48},{80,64},{96,80},{112,96},{128,112},... | collective-permute-start | bytes 122888 | tf_op jit(solution)/shard_map/ppermute | solution.py:342

commit v3 on v2

--- a/solution.py
+++ b/solution.py
@@ -8,32 +8,50 @@
 from jax.sharding import Mesh
 from jax.sharding import PartitionSpec as P
 
+
 GS = 16
 EPS = 1e-06
 F32 = jnp.float32
 BF16 = jnp.bfloat16
 USE_KERNELS = True
-
-
-def run(fn, out_shapes, args, name, grant=8):
+FIRST_GRANT = 56
+
+
+def run(fn, out_shapes, args, grant=8, late=()):
     if not USE_KERNELS:
-        return fn(*args)
+        return fn(*[(lambda a=a: a) if i in late else a for i, a in enumerate(args)])
     n_a, single = len(args), isinstance(out_shapes, tuple)
     shapes = [out_shapes] if single else list(out_shapes)
+    n_o = len(shapes)
 
     def body(*refs):
-        outs = fn(*[r[...] for r in refs[:n_a]])
+        held = refs[n_a + n_o :]
+        ins = [None if i in late else r[...] for i, r in enumerate(refs[:n_a])]
+        for spot, i in enumerate(late):
+            copy = pltpu.make_async_copy(refs[i], held[2 * spot], held[2 * spot + 1])
+            copy.start()
+
+            def ready(copy=copy, buffer=held[2 * spot]):
+                copy.wait()
+                return buffer[...]
+
+            ins[i] = ready
+        outs = fn(*ins)
         outs = [outs] if single else outs
-        for ref, value in zip(refs[n_a:], outs):
+        for ref, value in zip(refs[n_a : n_a + n_o], outs):
             ref[...] = value
 
     vmem = pl.BlockSpec(memory_space=pltpu.VMEM)
+    far = pl.BlockSpec(memory_space=pltpu.HBM)
+    scratch = []
+    for i in late:
+        scratch += [pltpu.VMEM(args[i].shape, args[i].dtype), pltpu.SemaphoreType.DMA]
     res = pl.pallas_call(
         body,
         out_shape=[jax.ShapeDtypeStruct(s, d) for s, d in shapes],
-        in_specs=[vmem] * n_a,
-        out_specs=[vmem] * len(shapes),
-        name=name,
+        in_specs=[far if i in late else vmem for i in range(n_a)],
+        out_specs=[vmem] * n_o,
+        scratch_shapes=scratch,
         compiler_params=pltpu.CompilerParams(vmem_limit_bytes=grant << 20),
     )(*args)
     return res[0] if single else res
@@ -114,16 +132,17 @@
     return row > 0, row < n_y * n_l - 1
 
 
-def first_pass(own, cache, peers):
-    return partial_stats(own, peers), jnp.concatenate([cache, own[None]], axis=0)
-
-
-def mid_conv(parts, raw, above, below, gain, bias, kernel, sizes):
+def first_pass(own, cache, gain, bias, late_bias, peers):
+    cols = jnp.concatenate([to_col(v, 1) for v in (gain, bias, late_bias)], axis=1)
+    return partial_stats(own, peers), jnp.concatenate([cache, own[None]], axis=0), cols
+
+
+def mid_conv(parts, raw, above, below, affine, kernel, sizes):
     chans, cols = raw.shape[1:]
     groups = chans // GS
     mean, scale = merge_stats(parts, groups, GS * cols)
     mean, scale = to_col(mean, GS), to_col(scale, GS)
-    gain, bias = to_col(gain, 1), to_col(bias, 1)
+    gain, bias = affine[:, :1], affine[:, 1:2]
     has = edges(sizes)
     pieces = []
     for t in range(3):
@@ -135,7 +154,7 @@
                     x = jnp.where(has[0 if dy == 0 else 1], x, 0.0)
             pieces += [right(x).astype(BF16), x.astype(BF16), left(x).astype(BF16)]
     columns = jnp.concatenate(pieces, axis=0)
-    out = jnp.dot(columns.T, kernel, preferred_element_type=F32).T
+    out = jnp.dot(columns.T, kernel(), preferred_element_type=F32).T
     blocks = []
     for x in range(4):
         for k in range(2):
@@ -144,9 +163,9 @@
     return jnp.stack(blocks)
 
 
-def fold(parts, own, bias):
+def fold(parts, own, affine):
     total = unpack(jnp.sum(parts, axis=0))
-    extra = own.astype(F32) + to_col(bias, 1)
+    extra = own.astype(F32) + affine[:, 2:3]
     zero = jnp.zeros_like(extra)
     first = lax.axis_index("h") == 0
     return pack(
@@ -218,16 +237,30 @@
     return jnp.concatenate([out(0), out(1)], axis=0), out(-1), out(2)
 
 
-def up_conv(parts, row, above, below, gain, bias, kernel, held, from_above, from_below, out_bias, sizes):
+def up_columns(gain, bias, out_bias):
+    chan = lax.axis_index("x") * 4 + lax.axis_index("h") * 2 + lax.axis_index("k")
+    rows = lax.broadcasted_iota(jnp.int32, (32, out_bias.shape[1]), 0)
+    lanes = lax.broadcasted_iota(jnp.int32, (32, out_bias.shape[1]), 1)
+    picked = jnp.sum(jnp.where(lanes == rows + chan * 32, out_bias, 0.0), axis=1, keepdims=True)
+    return jnp.concatenate([wide_col(gain), wide_col(bias)], axis=1), jnp.concatenate(
+        [picked] * 4, axis=0
+    )
+
+
+def up_weights(kernel):
+    return jnp.concatenate(
+        [kernel[(18 + dy * 3) * 32 : (21 + dy * 3) * 32] for dy in range(3)], axis=1
+    )
+
+
+def up_conv(parts, row, above, below, affine, lhs, held, from_above, from_below, out_bias, sizes):
     row, above, below = rows_of(row), rows_of(above), rows_of(below)
     chans, cols = row.shape
     groups = chans // GS
     mean, scale = merge_stats(parts, groups, GS * cols)
     mean, scale = to_col(mean, GS), to_col(scale, GS)
-    gain, bias = wide_col(gain), wide_col(bias)
+    gain, bias = affine[:, :1], affine[:, 1:2]
     has = edges(sizes)
-    per = 9 * 32
-    w = kernel[2 * per :]
 
     def image(x, keep=None):
         v = norm_silu(x, mean, scale, gain, bias)
@@ -235,7 +268,6 @@
             v = jnp.where(keep, v, 0.0)
         return v.astype(BF16)
 
-    lhs = jnp.concatenate([w[dy * 3 * 32 : (dy + 1) * 3 * 32] for dy in range(3)], axis=1)
     here = image(row)
     outs = []
     for images in ((image(above, has[0]), here, here), (here, here, image(below, has[1]))):
@@ -243,12 +275,8 @@
         cut = [prod[dx * 32 : (dx + 1) * 32] for dx in range(3)]
         outs += [right(cut[0]) + cut[1] + cut[2], cut[0] + cut[1] + left(cut[2])]
     total = jnp.concatenate(outs, axis=0) + held
-    chan = lax.axis_index("x") * 4 + lax.axis_index("h") * 2 + lax.axis_index("k")
-    rows = lax.broadcasted_iota(jnp.int32, (32, chans), 0)
-    lanes = lax.broadcasted_iota(jnp.int32, (32, chans), 1)
-    picked = jnp.sum(jnp.where(lanes == rows + chan * 32, out_bias, 0.0), axis=1, keepdims=True)
     total = total + jnp.concatenate([from_above, from_below], axis=0)
-    total = (total + jnp.concatenate([picked] * 4, axis=0)).T
+    total = (total + out_bias).T
     part = cols // 16
     return jnp.stack([total[c * part : (c + 1) * part] for c in range(16)]).astype(BF16)
 
@@ -274,11 +302,11 @@
     hi = lax.axis_index("h")
     space = ("y", "l")
     own = latent[0, 0].T
-    stats, raw = run(
+    stats, raw, affine = run(
         functools.partial(first_pass, peers=peers),
-        [((peers, 1, 128), F32), ((3, chans, cols), BF16)],
-        (own, cache_mid[:, 0].transpose(0, 2, 1)),
-        "first_pass",
+        [((peers, 1, 128), F32), ((3, chans, cols), BF16), ((chans, 3), F32)],
+        (own, cache_mid[:, 0].transpose(0, 2, 1), norm1_gain[None], norm1_bias[None], conv1_bias[None]),
+        FIRST_GRANT,
     )
     stats = lax.all_to_all(stats, space, 0, 0, tiled=True)
     down = [(i, i + 1) for i in range(peers - 1)]
@@ -288,17 +316,16 @@
     partial = run(
         functools.partial(mid_conv, sizes=sizes),
         ((8, 80, 128), F32),
-        (stats, raw, above, below, norm1_gain[None], norm1_bias[None], conv1_weight.reshape(27 * chans, 512)),
-        "mid_conv",
+        (stats, raw, above, below, affine, conv1_weight.reshape(27 * chans, 512)),
+        FIRST_GRANT,
+        late=(5,),
     )
     partial = lax.all_to_all(partial, ("x", "k"), 0, 0, tiled=True)
-    mine = run(fold, ((80, 128), F32), (partial, own, conv1_bias[None]), "fold")
+    mine = run(fold, ((80, 128), F32), (partial, own, affine))
     other = lax.ppermute(mine, "h", [(0, 1), (1, 0)])
-    gathered = run(merge, ((8, 80, 128), BF16), (mine, other), "merge")
+    gathered = run(merge, ((8, 80, 128), BF16), (mine, other))
     gathered = lax.all_to_all(gathered, ("x", "k"), 0, 0, tiled=True)
-    stats2 = run(
-        functools.partial(row_stats, peers=peers), ((peers, 1, 128), F32), (gathered,), "row_stats"
-    )
+    stats2 = run(functools.partial(row_stats, peers=peers), ((peers, 1, 128), F32), (gathered,))
     stats2 = lax.all_to_all(stats2, space, 0, 0, tiled=True)
 
     def at(y, l, h):
@@ -322,9 +349,8 @@
     tile = cache_up.reshape(2, 2, 10, 2, 512).transpose(0, 1, 3, 2, 4)
     swapped = lax.ppermute(tile, "h", [(0, 1), (1, 0)])
     pair = jnp.where(hi == 0, jnp.stack([tile, swapped]), jnp.stack([swapped, tile]))
-    spread = lax.all_to_all(
-        jnp.broadcast_to(pair[None], (8,) + pair.shape), ("x", "k"), 0, 0, tiled=True
-    )
+    copies = jnp.broadcast_to(pair[None], (8,) + pair.shape)
+    spread = lax.all_to_all(copies, ("x", "k"), 0, 0, tiled=True)
     images = (
         spread.reshape(4, 2, 2, 2, 2, 2, 10, 512)
         .transpose(3, 4, 5, 0, 2, 1, 6, 7)
@@ -335,11 +361,16 @@
         cache_conv,
         [((128, cols), F32), ((64, cols), F32), ((64, cols), F32)],
         (images, kernel2),
-        "cache_conv",
         16,
     )
     from_above = lax.ppermute(to_below, space, down)
     from_below = lax.ppermute(to_above, space, up)
+    affine2, bias_here = run(
+        up_columns,
+        [((512, 2), F32), ((128, 1), F32)],
+        (norm2_gain[None], norm2_bias[None], conv2_bias[None]),
+    )
+    lhs = run(up_weights, ((3 * 32, 3 * 512), BF16), (kernel2,))
     out = run(
         functools.partial(up_conv, sizes=sizes),
         ((16, cols // 16, 128), BF16),
@@ -348,15 +379,13 @@
             gathered,
             row_above,
             row_below,
-            norm2_gain[None],
-            norm2_bias[None],
-            kernel2,
+            affine2,
+            lhs,
             held,
             from_above,
             from_below,
-            conv2_bias[None],
+            bias_here,
         ),
-        "up_conv",
         16,
     )
     out = lax.all_to_all(out, ("x", "h", "k"), 0, 0, tiled=True)
@@ -383,8 +412,12 @@
         P(None, None, None, None, chan),
         P(),
     )
+
+    def body(*args):
+        return on_device((n_y, n_l), *args)
+
     return jax.shard_map(
-        functools.partial(on_device, (n_y, n_l)),
+        body,
         mesh=fine,
         in_specs=placed,
         out_specs=P(None, space, chan, None),

time: 158 us -> 159 us (level)
  starting transfers between devices: 81.9 us -> 96.5 us
  waiting for transfers between devices: 34.7 us -> 20.7 us
  local copies, waits for them, and re-layouts: 9.49 us -> 6.17 us
  Pallas kernels: 7.03 us -> 10.1 us
    ppermute x1, waiting for transfers between devices: 10.4 us -> 0.01 us  [on_device(): above = lax.ppermute(raw, space, down)]
    all_to_all x1, starting transfers between devices: 4.44 us -> 13.3 us  [on_device(): stats2 = lax.all_to_all(stats2, space, 0, 0, tiled=True)]
    ppermute x1, starting transfers between devices: 1.91 us -> 8.08 us  [on_device(): row_below = lax.ppermute(gathered, ('y', 'l', 'h'), up_h)]
    all_to_all x1, waiting for transfers between devices: 11.5 us -> 6.76 us  [on_device(): spread = lax.all_to_all(copies, ('x', 'k'), 0, 0, tiled=True)]
    unnamed x24 -> x20, local copies, waits for them, and re-layouts: 4.89 us -> 1.56 us
    pallas_call x7 -> x9, Pallas kernels: 7.03 us -> 10.1 us  [run(): pl.pallas_call(body, out_shape=[jax.ShapeDtypeStruct(s, d) for s, d in sh...]
where the time goes in v3:
time: 159 us; the launch traced here: 158 us
  starting transfers between devices  96.5 us (61%)
  blocking collectives  23.7 us (15%)
  waiting for transfers between devices  20.7 us (13%)
  Pallas kernels  10.1 us (6%)
  local copies, waits for them, and re-layouts  6.17 us (4%)
    all_to_all x1, blocking collectives, on_device(): out = lax.all_to_all(out, ('x', 'h', 'k'), 0, 0, tiled=True)  23.7 us
    all_to_all x1, starting transfers between devices, on_device(): stats = lax.all_to_all(stats, space, 0, 0, tiled=True)  15.3 us
    all_to_all x1, starting transfers between devices, on_device(): stats2 = lax.all_to_all(stats2, space, 0, 0, tiled=True)  13.3 us
    pallas_call x9, Pallas kernels, run(): pl.pallas_call(body, out_shape=[jax.ShapeDtypeStruct(s, d) for s, d in sh...  10.1 us
    ppermute x1, starting transfers between devices, on_device(): below = lax.ppermute(raw, space, up)  9.69 us
    ppermute x1, starting transfers between devices, on_device(): from_below = lax.ppermute(to_above, space, up)  9.69 us
    ppermute x1, starting transfers between devices, on_device(): row_below = lax.ppermute(gathered, ('y', 'l', 'h'), up_h)  8.08 us
    ppermute x1, starting transfers between devices, on_device(): swapped = lax.ppermute(tile, 'h', [(0, 1), (1, 0)])  7.93 us
  transfers between devices with their start and end apart: 13, of which 5 were waited for; matrix products, arithmetic and copies ran while one was open for 1% of the time, Pallas kernels for 2%

profile of v3, /device:TPU:9, one launch (start us, length us, event | category | flops | bytes accessed | tf_op | source)
XLA Modules:
  0.0 157.6 jit_solution(7288504027903599665)
XLA Ops:
  0.0 0.0 copy-start.2
  0.0 0.0 copy-start.6
  0.0 1.7 %shard_map.109 = (f32[32,1,128]{2,1,0:T(1,128)}, bf16[3,32,160]{2,1,0:T(8,128)(2,1)}, f32[32,3]{1,0:T(8,128)}) custom-call(bf16[32,160]{1,0:T(8,128)(2,1)} %bitcast.35, bf16[2,32,160]{2,1,0:T(8,128)(2,1)} %bitcast.47, f32[1,32]{1,0:T(1,128)} %bitcast.48, f32[1,32]{1,0:T(1,128)} %bitcast.49, f32[1,32]{1,0:T(1,128)} %bitcast.50), custom_call_target="tpu_custom_call" | custom-call | tf_op jit(solution)/shard_map/pallas_call | solution.py:49
  1.7 0.0 copy-start.1
  1.7 15.3 %all-to-all-start = ((f32[32,1,128]{2,1,0:T(1,128)}), f32[32,1,128]{2,1,0:T(1,128)S(1)}, u32[]{:S(2)}, u32[]{:S(2)}) async-start(f32[32,1,128]{2,1,0:T(1,128)} %get-tuple-element.13), calls=%async_computation | async-start | bytes 32768 | tf_op jit(solution)/shard_map/all_to_all | solution.py:311
  17.0 3.1 %collective-permute-start = (bf16[3,32,160]{2,1,0:T(8,128)(2,1)}, bf16[3,32,160]{2,1,0:T(8,128)(2,1)S(1)}, u32[]{:S(2)}, u32[]{:S(2)}) collective-permute-start(bf16[3,32,160]{2,1,0:T(8,128)(2,1)} %get-tuple-element.14.refs_1_), channel_id=1, source_target_pairs={{0,16},{16,32},{32,48},{48,64},{64,80},{80,96},{96,112},{112,128},... | collective-permute-start | bytes 92168 | tf_op jit(solution)/shard_map/ppermute | solution.py:314
  20.1 9.7 %collective-permute-start.1 = (bf16[3,32,160]{2,1,0:T(8,128)(2,1)}, bf16[3,32,160]{2,1,0:T(8,128)(2,1)S(1)}, u32[]{:S(2)}, u32[]{:S(2)}) collective-permute-start(bf16[3,32,160]{2,1,0:T(8,128)(2,1)} %get-tuple-element.14.refs_1_), channel_id=1, source_target_pairs={{16,0},{32,16},{48,32},{64,48},{80,64},{96,80},{112,96},{128,112},... | collective-permute-start | bytes 92168 | tf_op jit(solution)/shard_map/ppermute | solution.py:315
  29.8 0.0 collective-permute-done.refs_2_
  29.8 0.0 copy-start.8
  29.8 1.5 collective-permute-done.1.refs_3_
  31.3 0.0 copy-start.9
  31.3 0.0 all-to-all-done.refs_0_
  31.3 0.0 copy-start.7
  31.3 0.0 copy-done.8
  31.3 0.6 copy-done.9
  31.9 0.0 copy-done.7
  31.9 3.8 %shard_map.110 = f32[8,80,128]{2,1,0:T(8,128)} custom-call(f32[32,1,128]{2,1,0:T(1,128)} %copy-done.7, bf16[3,32,160]{2,1,0:T(8,128)(2,1)} %get-tuple-element.14.refs_1_, bf16[3,32,160]{2,1,0:T(8,128)(2,1)} %copy-done.8, bf16[3,32,160]{2,1,0:T(8,128)(2,1)} %copy-done.9, f32[32,3]{1,0:T(8,128)} %get-tuple-element.15.refs_4_.refs_2_, bf16[864,512]{1,0:T(8,128)(2,1)} %bitcast.42), custom_call_target="tpu_custom_call" | custom-call | tf_op jit(solution)/shard_map/pallas_call | solution.py:49
  35.7 6.7 %all-to-all-start.1 = ((f32[8,80,128]{2,1,0:T(8,128)}), f32[8,80,128]{2,1,0:T(8,128)S(1)}, u32[]{:S(2)}, u32[]{:S(2)}) async-start(f32[8,80,128]{2,1,0:T(8,128)} %shard_map.110), calls=%async_computation.1 | async-start | bytes 655360 | tf_op jit(solution)/shard_map/all_to_all | solution.py:323
  42.3 0.0 copy-done.6
  42.3 7.9 %collective-permute-start.5 = (bf16[2,2,2,10,512]{4,1,2,3,0:T(2,128)(2,1)S(1)}, bf16[2,2,2,10,512]{4,1,2,3,0:T(2,128)(2,1)S(1)}, u32[]{:S(2)}, u32[]{:S(2)}) collective-permute-start(bf16[2,2,2,10,512]{4,1,2,3,0:T(2,128)(2,1)S(1)} %bitcast.44), channel_id=1, source_target_pairs={{0,2},{2,0},{1,3},{3,1},{4,6},{6,4},{5,7},{7,5},{8,10},{10,8},{9,1... | collective-permute-start | bytes 245768 | tf_op jit(solution)/shard_map/ppermute | solution.py:350
  50.3 0.0 all-to-all-done.1.refs_0_
  50.3 0.0 copy-done.2
  50.3 0.0 copy-done.1
  50.3 0.2 shard_map.111.refs_0_
  50.5 7.0 %collective-permute-start.2 = (f32[80,128]{1,0:T(8,128)S(1)}, f32[80,128]{1,0:T(8,128)S(1)}, u32[]{:S(2)}, u32[]{:S(2)}) collective-permute-start(f32[80,128]{1,0:T(8,128)S(1)} %shard_map.111.refs_0_), channel_id=1, source_target_pairs={{0,2},{2,0},{1,3},{3,1},{4,6},{6,4},{5,7},{7,5},{8,10},{10,8},{9,1... | collective-permute-start | bytes 122888 | tf_op jit(solution)/shard_map/ppermute | solution.py:325
  57.5 6.4 %collective-permute-done.2.refs_1_ = f32[80,128]{1,0:T(8,128)S(1)} collective-permute-done((f32[80,128]{1,0:T(8,128)S(1)}, f32[80,128]{1,0:T(8,128)S(1)}, u32[]{:S(2)}, u32[]{:S(2)}) %collective-permute-start.2) | collective-permute-done | bytes 40992 | tf_op jit(solution)/shard_map/ppermute | solution.py:325
  63.9 0.7 shard_map.112
  64.6 6.2 %all-to-all-start.2 = ((bf16[8,80,128]{2,1,0:T(8,128)(2,1)}), bf16[8,80,128]{2,1,0:T(8,128)(2,1)S(1)}, u32[]{:S(2)}, u32[]{:S(2)}) async-start(bf16[8,80,128]{2,1,0:T(8,128)(2,1)} %shard_map.112), calls=%async_computation.2 | async-start | bytes 327680 | tf_op jit(solution)/shard_map/all_to_all | solution.py:327
  70.8 0.0 collective-permute-done.5
  70.8 0.2 broadcast_select_fusion
  71.1 0.1 copy.18
  71.2 5.2 %all-to-all-done.2.refs_0_.refs_1_ = bf16[8,80,128]{2,1,0:T(8,128)(2,1)S(1)} async-done(((bf16[8,80,128]{2,1,0:T(8,128)(2,1)}), bf16[8,80,128]{2,1,0:T(8,128)(2,1)S(1)}, u32[]{:S(2)}, u32[]{:S(2)}) %all-to-all-start.2) | async-done | bytes 163872 | tf_op jit(solution)/shard_map/all_to_all | solution.py:327
  76.4 2.1 %broadcast_in_dim.30 = bf16[8,2,2,2,2,10,512]{6,4,5,3,2,1,0:T(2,128)(2,1)} broadcast(bf16[2,2,2,2,10,512]{5,3,4,2,1,0:T(2,128)(2,1)S(1)} %copy.18), dimensions={1,2,3,4,5,6} | broadcast | bytes 1474560 | tf_op jit(solution)/shard_map/broadcast_in_dim | solution.py:352
  78.5 4.4 %all-to-all-start.4 = ((bf16[8,2,2,2,2,10,512]{6,4,5,3,2,1,0:T(2,128)(2,1)}), bf16[8,2,2,2,2,10,512]{6,4,5,3,2,1,0:T(2,128)(2,1)S(1)}, u32[]{:S(2)}, u32[]{:S(2)}) async-start(bf16[8,2,2,2,2,10,512]{6,4,5,3,2,1,0:T(2,128)(2,1)} %broadcast_in_dim.30), calls=%async_computation.4 | async-start | bytes 2621440 | tf_op jit(solution)/shard_map/all_to_all | solution.py:353
  82.9 1.9 %collective-permute-start.3 = (bf16[8,80,128]{2,1,0:T(8,128)(2,1)S(1)}, bf16[8,80,128]{2,1,0:T(8,128)(2,1)S(1)}, u32[]{:S(2)}, u32[]{:S(2)}) collective-permute-start(bf16[8,80,128]{2,1,0:T(8,128)(2,1)S(1)} %all-to-all-done.2.refs_0_.refs_1_), channel_id=1, source_target_pairs={{0,16},{2,18},{16,32},{18,34},{32,48},{34,50},{48,64},{50,66},{64,... | collective-permute-start | bytes 491528 | tf_op jit(solution)/shard_map/ppermute | solution.py:346
  84.8 8.1 %collective-permute-start.4 = (bf16[8,80,128]{2,1,0:T(8,128)(2,1)S(1)}, bf16[8,80,128]{2,1,0:T(8,128)(2,1)S(1)}, u32[]{:S(2)}, u32[]{:S(2)}) collective-permute-start(bf16[8,80,128]{2,1,0:T(8,128)(2,1)S(1)} %all-to-all-done.2.refs_0_.refs_1_), channel_id=1, source_target_pairs={{16,0},{18,2},{32,16},{34,18},{48,32},{50,34},{64,48},{66,50},{80,... | collective-permute-start | bytes 491528 | tf_op jit(solution)/shard_map/ppermute | solution.py:347
  92.9 1.0 shard_map.113
  93.9 6.8 %all-to-all-done.4 = bf16[8,2,2,2,2,10,512]{6,4,5,3,2,1,0:T(2,128)(2,1)S(1)} async-done(((bf16[8,2,2,2,2,10,512]{6,4,5,3,2,1,0:T(2,128)(2,1)}), bf16[8,2,2,2,2,10,512]{6,4,5,3,2,1,0:T(2,128)(2,1)S(1)}, u32[]{:S(2)}, u32[]{:S(2)}) %all-to-all-start.4) | async-done | bytes 1310752 | tf_op jit(solution)/shard_map/all_to_all | solution.py:353
  100.7 13.3 %all-to-all-start.3 = ((f32[32,1,128]{2,1,0:T(1,128)}), f32[32,1,128]{2,1,0:T(1,128)S(1)}, u32[]{:S(2)}, u32[]{:S(2)}) async-start(f32[32,1,128]{2,1,0:T(1,128)} %shard_map.113), calls=%async_computation.3 | async-start | bytes 32768 | tf_op jit(solution)/shard_map/all_to_all | solution.py:329
  114.0 1.2 copy.19
  115.2 0.0 copy-start
  115.2 0.2 copy.20.refs_0_
  115.5 0.9 copy-done
  116.4 0.0 copy-start.3
  116.4 0.0 copy-start.4
  116.4 0.0 copy-start.5
  116.4 0.8 shard_map.116
  117.2 3.1 %collective-permute-start.6 = (f32[64,160]{1,0:T(8,128)S(1)}, f32[64,160]{1,0:T(8,128)S(1)}, u32[]{:S(2)}, u32[]{:S(2)}) collective-permute-start(f32[64,160]{1,0:T(8,128)S(1)} %get-tuple-element.18), channel_id=1, source_target_pairs={{0,16},{16,32},{32,48},{48,64},{64,80},{80,96},{96,112},{112,128},... | collective-permute-start | bytes 122888 | tf_op jit(solution)/shard_map/ppermute | solution.py:366
  120.3 9.7 %collective-permute-start.7 = (f32[64,160]{1,0:T(8,128)S(1)}, f32[64,160]{1,0:T(8,128)S(1)}, u32[]{:S(2)}, u32[]{:S(2)}) collective-permute-start(f32[64,160]{1,0:T(8,128)S(1)} %get-tuple-element.19), channel_id=1, source_target_pairs={{16,0},{32,16},{48,32},{64,48},{80,64},{96,80},{112,96},{128,112},... | collective-permute-start | bytes 122888 | tf_op jit(solution)/shard_map/ppermute | solution.py:367
  130.1 0.0 copy-done.3
  130.1 0.0 copy-done.4
  130.1 0.0 copy-done.5
  130.1 0.3 shard_map.114
  130.4 0.0 all-to-all-done.3.refs_0_
  130.4 0.0 collective-permute-done.3.refs_2_
  130.4 0.0 collective-permute-done.4.refs_3_
  130.4 0.0 collective-permute-done.6.refs_7_
  130.4 0.9 collective-permute-done.7.refs_8_
  131.4 1.6 %shard_map.117 = bf16[16,10,128]{2,1,0:T(8,128)(2,1)S(1)} custom-call(f32[32,1,128]{2,1,0:T(1,128)S(1)} %all-to-all-done.3.refs_0_, bf16[8,80,128]{2,1,0:T(8,128)(2,1)S(1)} %all-to-all-done.2.refs_0_.refs_1_, bf16[8,80,128]{2,1,0:T(8,128)(2,1)S(1)} %collective-permute-done.3.refs_2_, bf16[8,80,128]{2,1,0:T(8,128)(2,1)S(1)} %collective-permute-done.4.refs_3_, ...), custom_call_target="tpu_custom_call" | custom-call | tf_op jit(solution)/shard_map/pallas_call | solution.py:49
  133.0 23.7 %all_to_all.30 = bf16[16,10,128]{2,1,0:T(8,128)(2,1)S(1)} all-to-all(bf16[16,10,128]{2,1,0:T(8,128)(2,1)S(1)} %shard_map.117), channel_id=1, replica_groups=mesh['y'=4,'l'=8,'x'=4,'h'=2,'k'=2] {'x','h','k'}, dimensions={0} | all-to-all | bytes 81920 | tf_op jit(solution)/shard_map/all_to_all | solution.py:391
  156.7 0.1 reshape.59
  156.8 0.8 reshape.60
  (3 shorter events, 0.1 us)
Async XLA Ops:
  0.0 50.3 %copy-start.2 = (bf16[1,1,160,32]{2,3,1,0:T(8,128)(2,1)S(1)}, bf16[1,1,160,32]{2,3,1,0:T(8,128)(2,1)}, u32[]{:S(2)}) copy-start(bf16[1,1,160,32]{2,3,1,0:T(8,128)(2,1)} %param.11) | copy-start | bytes 30724
  0.0 42.3 %copy-start.6 = (bf16[2,2,20,512]{3,1,2,0:T(2,128)(2,1)S(1)}, bf16[2,2,20,512]{3,1,2,0:T(2,128)(2,1)}, u32[]{:S(2)}) copy-start(bf16[2,2,20,512]{3,1,2,0:T(2,128)(2,1)} %param.17) | copy-start | bytes 245764
  1.7 48.6 %copy-start.1 = (f32[32,3]{1,0:T(8,128)S(1)}, f32[32,3]{1,0:T(8,128)}, u32[]{:S(2)}) copy-start(f32[32,3]{1,0:T(8,128)} %get-tuple-element.15.refs_4_.refs_2_) | copy-start | bytes 1156
  1.7 29.6 %all-to-all-start = ((f32[32,1,128]{2,1,0:T(1,128)}), f32[32,1,128]{2,1,0:T(1,128)S(1)}, u32[]{:S(2)}, u32[]{:S(2)}) async-start(f32[32,1,128]{2,1,0:T(1,128)} %get-tuple-element.13), calls=%async_computation | async-start | bytes 32768 | tf_op jit(solution)/shard_map/all_to_all | solution.py:311
  17.0 12.8 %collective-permute-start = (bf16[3,32,160]{2,1,0:T(8,128)(2,1)}, bf16[3,32,160]{2,1,0:T(8,128)(2,1)S(1)}, u32[]{:S(2)}, u32[]{:S(2)}) collective-permute-start(bf16[3,32,160]{2,1,0:T(8,128)(2,1)} %get-tuple-element.14.refs_1_), channel_id=1, source_target_pairs={{0,16},{16,32},{32,48},{48,64},{64,80},{80,96},{96,112},{112,128},... | collective-permute-start | bytes 92168 | tf_op jit(solution)/shard_map/ppermute | solution.py:314
  20.1 11.2 %collective-permute-start.1 = (bf16[3,32,160]{2,1,0:T(8,128)(2,1)}, bf16[3,32,160]{2,1,0:T(8,128)(2,1)S(1)}, u32[]{:S(2)}, u32[]{:S(2)}) collective-permute-start(bf16[3,32,160]{2,1,0:T(8,128)(2,1)} %get-tuple-element.14.refs_1_), channel_id=1, source_target_pairs={{16,0},{32,16},{48,32},{64,48},{80,64},{96,80},{112,96},{128,112},... | collective-permute-start | bytes 92168 | tf_op jit(solution)/shard_map/ppermute | solution.py:315
  29.8 1.5 copy-start.8
  31.3 0.6 copy-start.9
  31.3 0.6 copy-start.7
  35.7 14.6 %all-to-all-start.1 = ((f32[8,80,128]{2,1,0:T(8,128)}), f32[8,80,128]{2,1,0:T(8,128)S(1)}, u32[]{:S(2)}, u32[]{:S(2)}) async-start(f32[8,80,128]{2,1,0:T(8,128)} %shard_map.110), calls=%async_computation.1 | async-start | bytes 655360 | tf_op jit(solution)/shard_map/all_to_all | solution.py:323
  42.3 28.5 %collective-permute-start.5 = (bf16[2,2,2,10,512]{4,1,2,3,0:T(2,128)(2,1)S(1)}, bf16[2,2,2,10,512]{4,1,2,3,0:T(2,128)(2,1)S(1)}, u32[]{:S(2)}, u32[]{:S(2)}) collective-permute-start(bf16[2,2,2,10,512]{4,1,2,3,0:T(2,128)(2,1)S(1)} %bitcast.44), channel_id=1, source_target_pairs={{0,2},{2,0},{1,3},{3,1},{4,6},{6,4},{5,7},{7,5},{8,10},{10,8},{9,1... | collective-permute-start | bytes 245768 | tf_op jit(solution)/shard_map/ppermute | solution.py:350
  50.5 13.5 %collective-permute-start.2 = (f32[80,128]{1,0:T(8,128)S(1)}, f32[80,128]{1,0:T(8,128)S(1)}, u32[]{:S(2)}, u32[]{:S(2)}) collective-permute-start(f32[80,128]{1,0:T(8,128)S(1)} %shard_map.111.refs_0_), channel_id=1, source_target_pairs={{0,2},{2,0},{1,3},{3,1},{4,6},{6,4},{5,7},{7,5},{8,10},{10,8},{9,1... | collective-permute-start | bytes 122888 | tf_op jit(solution)/shard_map/ppermute | solution.py:325
  64.6 11.8 %all-to-all-start.2 = ((bf16[8,80,128]{2,1,0:T(8,128)(2,1)}), bf16[8,80,128]{2,1,0:T(8,128)(2,1)S(1)}, u32[]{:S(2)}, u32[]{:S(2)}) async-start(bf16[8,80,128]{2,1,0:T(8,128)(2,1)} %shard_map.112), calls=%async_computation.2 | async-start | bytes 327680 | tf_op jit(solution)/shard_map/all_to_all | solution.py:327
  78.5 22.2 %all-to-all-start.4 = ((bf16[8,2,2,2,2,10,512]{6,4,5,3,2,1,0:T(2,128)(2,1)}), bf16[8,2,2,2,2,10,512]{6,4,5,3,2,1,0:T(2,128)(2,1)S(1)}, u32[]{:S(2)}, u32[]{:S(2)}) async-start(bf16[8,2,2,2,2,10,512]{6,4,5,3,2,1,0:T(2,128)(2,1)} %broadcast_in_dim.30), calls=%async_computation.4 | async-start | bytes 2621440 | tf_op jit(solution)/shard_map/all_to_all | solution.py:353
  82.9 47.5 %collective-permute-start.3 = (bf16[8,80,128]{2,1,0:T(8,128)(2,1)S(1)}, bf16[8,80,128]{2,1,0:T(8,128)(2,1)S(1)}, u32[]{:S(2)}, u32[]{:S(2)}) collective-permute-start(bf16[8,80,128]{2,1,0:T(8,128)(2,1)S(1)} %all-to-all-done.2.refs_0_.refs_1_), channel_id=1, source_target_pairs={{0,16},{2,18},{16,32},{18,34},{32,48},{34,50},{48,64},{50,66},{64,... | collective-permute-start | bytes 491528 | tf_op jit(solution)/shard_map/ppermute | solution.py:346
  84.8 45.6 %collective-permute-start.4 = (bf16[8,80,128]{2,1,0:T(8,128)(2,1)S(1)}, bf16[8,80,128]{2,1,0:T(8,128)(2,1)S(1)}, u32[]{:S(2)}, u32[]{:S(2)}) collective-permute-start(bf16[8,80,128]{2,1,0:T(8,128)(2,1)S(1)} %all-to-all-done.2.refs_0_.refs_1_), channel_id=1, source_target_pairs={{16,0},{18,2},{32,16},{34,18},{48,32},{50,34},{64,48},{66,50},{80,... | collective-permute-start | bytes 491528 | tf_op jit(solution)/shard_map/ppermute | solution.py:347
  100.7 29.7 %all-to-all-start.3 = ((f32[32,1,128]{2,1,0:T(1,128)}), f32[32,1,128]{2,1,0:T(1,128)S(1)}, u32[]{:S(2)}, u32[]{:S(2)}) async-start(f32[32,1,128]{2,1,0:T(1,128)} %shard_map.113), calls=%async_computation.3 | async-start | bytes 32768 | tf_op jit(solution)/shard_map/all_to_all | solution.py:329
  115.2 1.2 copy-start
  116.4 13.7 %copy-start.3 = (f32[512]{0:T(512)S(1)}, f32[512]{0:T(512)}, u32[]{:S(2)}) copy-start(f32[512]{0:T(512)} %param.18) | copy-start | bytes 6148
  116.4 13.7 %copy-start.4 = (f32[512]{0:T(512)S(1)}, f32[512]{0:T(512)}, u32[]{:S(2)}) copy-start(f32[512]{0:T(512)} %param.19) | copy-start | bytes 6148
  116.4 13.7 %copy-start.5 = (f32[512]{0:T(512)S(1)}, f32[512]{0:T(512)}, u32[]{:S(2)}) copy-start(f32[512]{0:T(512)} %param.21) | copy-start | bytes 6148
  117.2 13.2 %collective-permute-start.6 = (f32[64,160]{1,0:T(8,128)S(1)}, f32[64,160]{1,0:T(8,128)S(1)}, u32[]{:S(2)}, u32[]{:S(2)}) collective-permute-start(f32[64,160]{1,0:T(8,128)S(1)} %get-tuple-element.18), channel_id=1, source_target_pairs={{0,16},{16,32},{32,48},{48,64},{64,80},{80,96},{96,112},{112,128},... | collective-permute-start | bytes 122888 | tf_op jit(solution)/shard_map/ppermute | solution.py:366
  120.3 11.0 %collective-permute-start.7 = (f32[64,160]{1,0:T(8,128)S(1)}, f32[64,160]{1,0:T(8,128)S(1)}, u32[]{:S(2)}, u32[]{:S(2)}) collective-permute-start(f32[64,160]{1,0:T(8,128)S(1)} %get-tuple-element.19), channel_id=1, source_target_pairs={{16,0},{32,16},{48,32},{64,48},{80,64},{96,80},{112,96},{128,112},... | collective-permute-start | bytes 122888 | tf_op jit(solution)/shard_map/ppermute | solution.py:367

commit v4 on v3

--- a/solution.py
+++ b/solution.py
@@ -235,6 +235,17 @@
         )
 
     return jnp.concatenate([out(0), out(1)], axis=0), out(-1), out(2)
+
+
+def assemble(*came):
+    x = lax.axis_index("x")
+    out = []
+    for i in range(4):
+        block = came[(3 - i) % 4]
+        for here in range(3):
+            block = jnp.where(x == here, came[(here - i) % 4], block)
+        out.append(block)
+    return jnp.stack(out)
 
 
 def up_columns(gain, bias, out_bias):
@@ -349,13 +360,14 @@
     tile = cache_up.reshape(2, 2, 10, 2, 512).transpose(0, 1, 3, 2, 4)
     swapped = lax.ppermute(tile, "h", [(0, 1), (1, 0)])
     pair = jnp.where(hi == 0, jnp.stack([tile, swapped]), jnp.stack([swapped, tile]))
-    copies = jnp.broadcast_to(pair[None], (8,) + pair.shape)
-    spread = lax.all_to_all(copies, ("x", "k"), 0, 0, tiled=True)
-    images = (
-        spread.reshape(4, 2, 2, 2, 2, 2, 10, 512)
-        .transpose(3, 4, 5, 0, 2, 1, 6, 7)
-        .reshape(2, 2, 2, cols, 512)
-    )
+    came = [pair] + [
+        lax.ppermute(pair, "x", [(i, (i + d) % 4) for i in range(4)]) for d in range(1, 4)
+    ]
+    mine_k = run(assemble, ((4,) + pair.shape, BF16), came)
+    other_k = lax.ppermute(mine_k, "k", [(0, 1), (1, 0)])
+    core = lax.axis_index("k")
+    both = jnp.where(core == 0, jnp.stack([mine_k, other_k]), jnp.stack([other_k, mine_k]))
+    images = both.transpose(3, 4, 5, 1, 2, 0, 6, 7).reshape(2, 2, 2, cols, 512)
     kernel2 = conv2_weight.transpose(0, 1, 2, 4, 3).reshape(27 * 32, 512)
     held, to_above, to_below = run(
         cache_conv,

time: 159 us -> 190 us (1.19)
  starting transfers between devices: 96.5 us -> 113 us
  blocking collectives: 23.7 us -> 36.7 us
  waiting for transfers between devices: 20.7 us -> 22.9 us
    ppermute x0 -> x4, starting transfers between devices: none -> 14.7 us  [the longest x3 10.5 us: on_device(): lax.ppermute(pair, 'x', [(i, (i + d) % 4) for i in range(4)])]
    all_to_all x0 -> x1, blocking collectives: none -> 13.5 us  [on_device(): partial = lax.all_to_all(partial, ('x', 'k'), 0, 0, tiled=True)]
    all_to_all x2 -> x0, starting transfers between devices: 11.1 us -> none  [the longest x1 6.68 us: on_device(): partial = lax.all_to_all(partial, ('x', 'k'), 0, 0, tiled=True)]
    ppermute x1, starting transfers between devices: 7.93 us -> 15.4 us  [on_device(): swapped = lax.ppermute(tile, 'h', [(0, 1), (1, 0)])]
    ppermute x0 -> x4, waiting for transfers between devices: none -> 7.14 us  [the longest x3 7.14 us: on_device(): lax.ppermute(pair, 'x', [(i, (i + d) % 4) for i in range(4)])]
    all_to_all x2 -> x0, waiting for transfers between devices: 6.77 us -> none  [the longest x1 6.76 us: on_device(): spread = lax.all_to_all(copies, ('x', 'k'), 0, 0, tiled=True)]
    all_to_all x1, starting transfers between devices: 15.3 us -> 18.9 us  [on_device(): stats = lax.all_to_all(stats, space, 0, 0, tiled=True)]
    ppermute x1, waiting for transfers between devices: 0.01 us -> 3.18 us  [on_device(): swapped = lax.ppermute(tile, 'h', [(0, 1), (1, 0)])]
  transfers between devices with their start and end apart: 13 -> 15, of which waited for: 5 -> 7; matrix products, arithmetic and copies ran while one was open for 1% -> 1% of each run, Pallas kernels for 2% -> 4%
where the time goes in v4:
time: 190 us; the launch traced here: 189 us
  starting transfers between devices  113 us (59%)
  blocking collectives  36.7 us (19%)
  waiting for transfers between devices  22.9 us (12%)
  Pallas kernels  10.3 us (5%)
  local copies, waits for them, and re-layouts  5.75 us (3%)
    all_to_all x1, blocking collectives, on_device(): out = lax.all_to_all(out, ('x', 'h', 'k'), 0, 0, tiled=True)  23.2 us
    all_to_all x1, starting transfers between devices, on_device(): stats = lax.all_to_all(stats, space, 0, 0, tiled=True)  18.9 us
    ppermute x1, starting transfers between devices, on_device(): swapped = lax.ppermute(tile, 'h', [(0, 1), (1, 0)])  15.4 us
    all_to_all x1, blocking collectives, on_device(): partial = lax.all_to_all(partial, ('x', 'k'), 0, 0, tiled=True)  13.5 us
    all_to_all x1, starting transfers between devices, on_device(): stats2 = lax.all_to_all(stats2, space, 0, 0, tiled=True)  11.1 us
    ppermute x1, starting transfers between devices, on_device(): from_below = lax.ppermute(to_above, space, up)  10.9 us
    ppermute x3, starting transfers between devices, on_device(): lax.ppermute(pair, 'x', [(i, (i + d) % 4) for i in range(4)])  10.5 us
    pallas_call x10, Pallas kernels, run(): pl.pallas_call(body, out_shape=[jax.ShapeDtypeStruct(s, d) for s, d in sh...  10.3 us
  transfers between devices with their start and end apart: 15, of which 7 were waited for; matrix products, arithmetic and copies ran while one was open for 1% of the time, Pallas kernels for 4%

profile of v4, /device:TPU:9, one launch (start us, length us, event | category | flops | bytes accessed | tf_op | source)
XLA Modules:
  0.0 189.2 jit_solution(2957768002123271371)
XLA Ops:
  0.0 0.9 copy.34
  0.9 15.4 %collective-permute-start.5 = (bf16[2,2,2,10,512]{4,3,2,1,0:T(8,128)(2,1)S(1)}, bf16[2,2,2,10,512]{4,3,2,1,0:T(8,128)(2,1)S(1)}, u32[]{:S(2)}, u32[]{:S(2)}) collective-permute-start(bf16[2,2,2,10,512]{4,3,2,1,0:T(8,128)(2,1)S(1)} %bitcast.50), channel_id=1, source_target_pairs={{0,2},{2,0},{1,3},{3,1},{4,6},{6,4},{5,7},{7,5},{8,10},{10,8},{9,1... | collective-permute-start | bytes 245768 | tf_op jit(solution)/shard_map/ppermute | solution.py:361
  16.4 3.2 %collective-permute-done.5 = bf16[2,2,2,10,512]{4,3,2,1,0:T(8,128)(2,1)S(1)} collective-permute-done((bf16[2,2,2,10,512]{4,3,2,1,0:T(8,128)(2,1)S(1)}, bf16[2,2,2,10,512]{4,3,2,1,0:T(8,128)(2,1)S(1)}, u32[]{:S(2)}, u32[]{:S(2)}) %collective-permute-start.5) | collective-permute-done | bytes 81952 | tf_op jit(solution)/shard_map/ppermute | solution.py:361
  19.6 0.1 maximum_select_fusion.1.refs_0_
  19.6 3.1 %collective-permute-start.6 = (bf16[2,2,2,2,10,512]{5,4,3,2,1,0:T(8,128)(2,1)S(1)}, bf16[2,2,2,2,10,512]{5,4,3,2,1,0:T(8,128)(2,1)S(1)}, u32[]{:S(2)}, u32[]{:S(2)}) collective-permute-start(bf16[2,2,2,2,10,512]{5,4,3,2,1,0:T(8,128)(2,1)S(1)} %maximum_select_fusion.1.refs_0_), channel_id=1, source_target_pairs={{0,4},{4,8},{8,12},{12,0},{1,5},{5,9},{9,13},{13,1},{2,6},{6,10},{... | collective-permute-start | bytes 491528 | tf_op jit(solution)/shard_map/ppermute | solution.py:364
  22.7 4.4 %collective-permute-start.7 = (bf16[2,2,2,2,10,512]{5,4,3,2,1,0:T(8,128)(2,1)S(1)}, bf16[2,2,2,2,10,512]{5,4,3,2,1,0:T(8,128)(2,1)S(1)}, u32[]{:S(2)}, u32[]{:S(2)}) collective-permute-start(bf16[2,2,2,2,10,512]{5,4,3,2,1,0:T(8,128)(2,1)S(1)} %maximum_select_fusion.1.refs_0_), channel_id=1, source_target_pairs={{0,8},{4,12},{8,0},{12,4},{1,9},{5,13},{9,1},{13,5},{2,10},{6,14},... | collective-permute-start | bytes 491528 | tf_op jit(solution)/shard_map/ppermute | solution.py:364
  27.1 3.1 %collective-permute-start.8 = (bf16[2,2,2,2,10,512]{5,4,3,2,1,0:T(8,128)(2,1)S(1)}, bf16[2,2,2,2,10,512]{5,4,3,2,1,0:T(8,128)(2,1)S(1)}, u32[]{:S(2)}, u32[]{:S(2)}) collective-permute-start(bf16[2,2,2,2,10,512]{5,4,3,2,1,0:T(8,128)(2,1)S(1)} %maximum_select_fusion.1.refs_0_), channel_id=1, source_target_pairs={{0,12},{4,0},{8,4},{12,8},{1,13},{5,1},{9,5},{13,9},{2,14},{6,2},{... | collective-permute-start | bytes 491528 | tf_op jit(solution)/shard_map/ppermute | solution.py:364
  30.2 0.0 collective-permute-done.6.refs_1_
  30.2 5.5 %collective-permute-done.7.refs_2_ = bf16[2,2,2,2,10,512]{5,4,3,2,1,0:T(8,128)(2,1)S(1)} collective-permute-done((bf16[2,2,2,2,10,512]{5,4,3,2,1,0:T(8,128)(2,1)S(1)}, bf16[2,2,2,2,10,512]{5,4,3,2,1,0:T(8,128)(2,1)S(1)}, u32[]{:S(2)}, u32[]{:S(2)}) %collective-permute-start.7) | collective-permute-done | bytes 163872 | tf_op jit(solution)/shard_map/ppermute | solution.py:364
  35.6 1.7 collective-permute-done.8.refs_3_
  37.3 0.2 shard_map.116
  37.6 0.0 copy-start.2
  37.6 0.6 copy.24
  38.1 4.1 %collective-permute-start.9 = (bf16[4,2,2,2,2,10,512]{6,0,5,4,3,2,1:T(4,128)(2,1)S(1)}, bf16[4,2,2,2,2,10,512]{6,0,5,4,3,2,1:T(4,128)(2,1)S(1)}, u32[]{:S(2)}, u32[]{:S(2)}) collective-permute-start(bf16[4,2,2,2,2,10,512]{6,0,5,4,3,2,1:T(4,128)(2,1)S(1)} %copy.24), channel_id=1, source_target_pairs={{0,1},{1,0},{2,3},{3,2},{4,5},{5,4},{6,7},{7,6},{8,9},{9,8},{10,11... | collective-permute-start | bytes 1966088 | tf_op jit(solution)/shard_map/ppermute | solution.py:367
  42.3 1.6 shard_map.109
  43.9 18.9 %all-to-all-start = ((f32[32,1,128]{2,1,0:T(1,128)}), f32[32,1,128]{2,1,0:T(1,128)S(1)}, u32[]{:S(2)}, u32[]{:S(2)}) async-start(f32[32,1,128]{2,1,0:T(1,128)} %get-tuple-element.13), calls=%async_computation | async-start | bytes 32768 | tf_op jit(solution)/shard_map/all_to_all | solution.py:322
  62.8 3.1 %collective-permute-start = (bf16[3,32,160]{2,1,0:T(8,128)(2,1)}, bf16[3,32,160]{2,1,0:T(8,128)(2,1)S(1)}, u32[]{:S(2)}, u32[]{:S(2)}) collective-permute-start(bf16[3,32,160]{2,1,0:T(8,128)(2,1)} %get-tuple-element.14.refs_1_), channel_id=1, source_target_pairs={{0,16},{16,32},{32,48},{48,64},{64,80},{80,96},{96,112},{112,128},... | collective-permute-start | bytes 92168 | tf_op jit(solution)/shard_map/ppermute | solution.py:325
  65.9 9.7 %collective-permute-start.1 = (bf16[3,32,160]{2,1,0:T(8,128)(2,1)}, bf16[3,32,160]{2,1,0:T(8,128)(2,1)S(1)}, u32[]{:S(2)}, u32[]{:S(2)}) collective-permute-start(bf16[3,32,160]{2,1,0:T(8,128)(2,1)} %get-tuple-element.14.refs_1_), channel_id=1, source_target_pairs={{16,0},{32,16},{48,32},{64,48},{80,64},{96,80},{112,96},{128,112},... | collective-permute-start | bytes 92168 | tf_op jit(solution)/shard_map/ppermute | solution.py:326
  75.6 0.0 collective-permute-done.refs_2_
  75.6 0.0 copy-start.7
  75.6 1.5 collective-permute-done.1.refs_3_
  77.1 0.0 all-to-all-done.refs_0_
  77.1 0.0 copy-done.7
  77.1 0.6 copy-done.8
  77.7 0.0 copy-done.6
  77.7 3.7 %shard_map.110 = f32[8,80,128]{2,1,0:T(8,128)} custom-call(f32[32,1,128]{2,1,0:T(1,128)} %copy-done.6, bf16[3,32,160]{2,1,0:T(8,128)(2,1)} %get-tuple-element.14.refs_1_, bf16[3,32,160]{2,1,0:T(8,128)(2,1)} %copy-done.7, bf16[3,32,160]{2,1,0:T(8,128)(2,1)} %copy-done.8, f32[32,3]{1,0:T(8,128)} %get-tuple-element.15.refs_4_.refs_2_, bf16[864,512]{1,0:T(8,128)(2,1)} %bitcast.48), custom_call_target="tpu_custom_call" | custom-call | tf_op jit(solution)/shard_map/pallas_call | solution.py:49
  81.5 13.5 %all_to_all.25.refs_0_ = f32[8,80,128]{2,1,0:T(8,128)S(1)} all-to-all(f32[8,80,128]{2,1,0:T(8,128)} %shard_map.110), channel_id=1, replica_groups=mesh['y'=4,'l'=8,'x'=4,'h'=2,'k'=2] {'x','k'}, dimensions={0} | all-to-all | bytes 655360 | tf_op jit(solution)/shard_map/all_to_all | solution.py:334
  95.0 0.0 copy-done.2
  95.0 0.0 copy-done.1
  95.0 0.2 shard_map.111.refs_0_
  95.1 8.8 %collective-permute-start.2 = (f32[80,128]{1,0:T(8,128)S(1)}, f32[80,128]{1,0:T(8,128)S(1)}, u32[]{:S(2)}, u32[]{:S(2)}) collective-permute-start(f32[80,128]{1,0:T(8,128)S(1)} %shard_map.111.refs_0_), channel_id=1, source_target_pairs={{0,2},{2,0},{1,3},{3,1},{4,6},{6,4},{5,7},{7,5},{8,10},{10,8},{9,1... | collective-permute-start | bytes 122888 | tf_op jit(solution)/shard_map/ppermute | solution.py:336
  104.0 4.6 %collective-permute-done.2.refs_1_ = f32[80,128]{1,0:T(8,128)S(1)} collective-permute-done((f32[80,128]{1,0:T(8,128)S(1)}, f32[80,128]{1,0:T(8,128)S(1)}, u32[]{:S(2)}, u32[]{:S(2)}) %collective-permute-start.2) | collective-permute-done | bytes 40992 | tf_op jit(solution)/shard_map/ppermute | solution.py:336
  108.6 0.7 shard_map.112
  109.3 7.4 %all-to-all-start.2 = ((bf16[8,80,128]{2,1,0:T(8,128)(2,1)}), bf16[8,80,128]{2,1,0:T(8,128)(2,1)S(1)}, u32[]{:S(2)}, u32[]{:S(2)}) async-start(bf16[8,80,128]{2,1,0:T(8,128)(2,1)} %shard_map.112), calls=%async_computation.2 | async-start | bytes 327680 | tf_op jit(solution)/shard_map/all_to_all | solution.py:338
  116.7 5.6 %all-to-all-done.2.refs_0_.refs_1_ = bf16[8,80,128]{2,1,0:T(8,128)(2,1)S(1)} async-done(((bf16[8,80,128]{2,1,0:T(8,128)(2,1)}), bf16[8,80,128]{2,1,0:T(8,128)(2,1)S(1)}, u32[]{:S(2)}, u32[]{:S(2)}) %all-to-all-start.2) | async-done | bytes 163872 | tf_op jit(solution)/shard_map/all_to_all | solution.py:338
  122.3 1.0 shard_map.113
  123.3 11.1 %all-to-all-start.3 = ((f32[32,1,128]{2,1,0:T(1,128)}), f32[32,1,128]{2,1,0:T(1,128)S(1)}, u32[]{:S(2)}, u32[]{:S(2)}) async-start(f32[32,1,128]{2,1,0:T(1,128)} %shard_map.113), calls=%async_computation.3 | async-start | bytes 32768 | tf_op jit(solution)/shard_map/all_to_all | solution.py:340
  134.4 3.1 %collective-permute-start.3 = (bf16[8,80,128]{2,1,0:T(8,128)(2,1)S(1)}, bf16[8,80,128]{2,1,0:T(8,128)(2,1)S(1)}, u32[]{:S(2)}, u32[]{:S(2)}) collective-permute-start(bf16[8,80,128]{2,1,0:T(8,128)(2,1)S(1)} %all-to-all-done.2.refs_0_.refs_1_), channel_id=1, source_target_pairs={{0,16},{2,18},{16,32},{18,34},{32,48},{34,50},{48,64},{50,66},{64,... | collective-permute-start | bytes 491528 | tf_op jit(solution)/shard_map/ppermute | solution.py:357
  137.5 7.7 %collective-permute-start.4 = (bf16[8,80,128]{2,1,0:T(8,128)(2,1)S(1)}, bf16[8,80,128]{2,1,0:T(8,128)(2,1)S(1)}, u32[]{:S(2)}, u32[]{:S(2)}) collective-permute-start(bf16[8,80,128]{2,1,0:T(8,128)(2,1)S(1)} %all-to-all-done.2.refs_0_.refs_1_), channel_id=1, source_target_pairs={{16,0},{18,2},{32,16},{34,18},{48,32},{50,34},{64,48},{66,50},{80,... | collective-permute-start | bytes 491528 | tf_op jit(solution)/shard_map/ppermute | solution.py:358
  145.2 0.0 collective-permute-done.9
  145.2 0.2 copy.33
  145.4 0.5 fusion
  145.9 1.4 copy.26
  147.2 0.0 copy-start
  147.2 0.2 copy.27.refs_0_
  147.5 0.0 copy-start.3
  147.5 0.0 copy-start.4
  147.5 0.0 copy-start.5
  147.5 0.9 copy-done
  148.4 0.8 shard_map.117
  149.3 1.9 %collective-permute-start.10 = (f32[64,160]{1,0:T(8,128)S(1)}, f32[64,160]{1,0:T(8,128)S(1)}, u32[]{:S(2)}, u32[]{:S(2)}) collective-permute-start(f32[64,160]{1,0:T(8,128)S(1)} %get-tuple-element.18), channel_id=1, source_target_pairs={{0,16},{16,32},{32,48},{48,64},{64,80},{80,96},{96,112},{112,128},... | collective-permute-start | bytes 122888 | tf_op jit(solution)/shard_map/ppermute | solution.py:378
  151.2 10.9 %collective-permute-start.11 = (f32[64,160]{1,0:T(8,128)S(1)}, f32[64,160]{1,0:T(8,128)S(1)}, u32[]{:S(2)}, u32[]{:S(2)}) collective-permute-start(f32[64,160]{1,0:T(8,128)S(1)} %get-tuple-element.19), channel_id=1, source_target_pairs={{16,0},{32,16},{48,32},{64,48},{80,64},{96,80},{112,96},{128,112},... | collective-permute-start | bytes 122888 | tf_op jit(solution)/shard_map/ppermute | solution.py:379
  162.1 0.0 copy-done.3
  162.1 0.0 copy-done.4
  162.1 0.3 shard_map.114
  162.4 0.0 all-to-all-done.3.refs_0_
  162.4 0.0 collective-permute-done.3.refs_2_
  162.4 0.0 collective-permute-done.4.refs_3_
  162.4 0.0 collective-permute-done.10.refs_7_
  162.4 0.9 collective-permute-done.11.refs_8_
  163.4 1.7 shard_map.118
  165.0 23.2 %all_to_all.26 = bf16[16,10,128]{2,1,0:T(8,128)(2,1)S(1)} all-to-all(bf16[16,10,128]{2,1,0:T(8,128)(2,1)S(1)} %shard_map.118), channel_id=1, replica_groups=mesh['y'=4,'l'=8,'x'=4,'h'=2,'k'=2] {'x','h','k'}, dimensions={0} | all-to-all | bytes 81920 | tf_op jit(solution)/shard_map/all_to_all | solution.py:403
  188.3 0.1 reshape.22
  188.4 0.8 reshape.23
  (7 shorter events, 0.1 us)
Async XLA Ops:
  0.9 18.6 %collective-permute-start.5 = (bf16[2,2,2,10,512]{4,3,2,1,0:T(8,128)(2,1)S(1)}, bf16[2,2,2,10,512]{4,3,2,1,0:T(8,128)(2,1)S(1)}, u32[]{:S(2)}, u32[]{:S(2)}) collective-permute-start(bf16[2,2,2,10,512]{4,3,2,1,0:T(8,128)(2,1)S(1)} %bitcast.50), channel_id=1, source_target_pairs={{0,2},{2,0},{1,3},{3,1},{4,6},{6,4},{5,7},{7,5},{8,10},{10,8},{9,1... | collective-permute-start | bytes 245768 | tf_op jit(solution)/shard_map/ppermute | solution.py:361
  19.6 10.6 %collective-permute-start.6 = (bf16[2,2,2,2,10,512]{5,4,3,2,1,0:T(8,128)(2,1)S(1)}, bf16[2,2,2,2,10,512]{5,4,3,2,1,0:T(8,128)(2,1)S(1)}, u32[]{:S(2)}, u32[]{:S(2)}) collective-permute-start(bf16[2,2,2,2,10,512]{5,4,3,2,1,0:T(8,128)(2,1)S(1)} %maximum_select_fusion.1.refs_0_), channel_id=1, source_target_pairs={{0,4},{4,8},{8,12},{12,0},{1,5},{5,9},{9,13},{13,1},{2,6},{6,10},{... | collective-permute-start | bytes 491528 | tf_op jit(solution)/shard_map/ppermute | solution.py:364
  22.7 12.9 %collective-permute-start.7 = (bf16[2,2,2,2,10,512]{5,4,3,2,1,0:T(8,128)(2,1)S(1)}, bf16[2,2,2,2,10,512]{5,4,3,2,1,0:T(8,128)(2,1)S(1)}, u32[]{:S(2)}, u32[]{:S(2)}) collective-permute-start(bf16[2,2,2,2,10,512]{5,4,3,2,1,0:T(8,128)(2,1)S(1)} %maximum_select_fusion.1.refs_0_), channel_id=1, source_target_pairs={{0,8},{4,12},{8,0},{12,4},{1,9},{5,13},{9,1},{13,5},{2,10},{6,14},... | collective-permute-start | bytes 491528 | tf_op jit(solution)/shard_map/ppermute | solution.py:364
  27.1 10.2 %collective-permute-start.8 = (bf16[2,2,2,2,10,512]{5,4,3,2,1,0:T(8,128)(2,1)S(1)}, bf16[2,2,2,2,10,512]{5,4,3,2,1,0:T(8,128)(2,1)S(1)}, u32[]{:S(2)}, u32[]{:S(2)}) collective-permute-start(bf16[2,2,2,2,10,512]{5,4,3,2,1,0:T(8,128)(2,1)S(1)} %maximum_select_fusion.1.refs_0_), channel_id=1, source_target_pairs={{0,12},{4,0},{8,4},{12,8},{1,13},{5,1},{9,5},{13,9},{2,14},{6,2},{... | collective-permute-start | bytes 491528 | tf_op jit(solution)/shard_map/ppermute | solution.py:364
  37.6 57.4 %copy-start.2 = (bf16[1,1,160,32]{2,3,1,0:T(8,128)(2,1)S(1)}, bf16[1,1,160,32]{2,3,1,0:T(8,128)(2,1)}, u32[]{:S(2)}) copy-start(bf16[1,1,160,32]{2,3,1,0:T(8,128)(2,1)} %param.11) | copy-start | bytes 30724
  38.1 107.0 %collective-permute-start.9 = (bf16[4,2,2,2,2,10,512]{6,0,5,4,3,2,1:T(4,128)(2,1)S(1)}, bf16[4,2,2,2,2,10,512]{6,0,5,4,3,2,1:T(4,128)(2,1)S(1)}, u32[]{:S(2)}, u32[]{:S(2)}) collective-permute-start(bf16[4,2,2,2,2,10,512]{6,0,5,4,3,2,1:T(4,128)(2,1)S(1)} %copy.24), channel_id=1, source_target_pairs={{0,1},{1,0},{2,3},{3,2},{4,5},{5,4},{6,7},{7,6},{8,9},{9,8},{10,11... | collective-permute-start | bytes 1966088 | tf_op jit(solution)/shard_map/ppermute | solution.py:367
  43.9 51.1 %copy-start.1 = (f32[32,3]{1,0:T(8,128)S(1)}, f32[32,3]{1,0:T(8,128)}, u32[]{:S(2)}) copy-start(f32[32,3]{1,0:T(8,128)} %get-tuple-element.15.refs_4_.refs_2_) | copy-start | bytes 1156
  43.9 33.2 %all-to-all-start = ((f32[32,1,128]{2,1,0:T(1,128)}), f32[32,1,128]{2,1,0:T(1,128)S(1)}, u32[]{:S(2)}, u32[]{:S(2)}) async-start(f32[32,1,128]{2,1,0:T(1,128)} %get-tuple-element.13), calls=%async_computation | async-start | bytes 32768 | tf_op jit(solution)/shard_map/all_to_all | solution.py:322
  62.8 12.8 %collective-permute-start = (bf16[3,32,160]{2,1,0:T(8,128)(2,1)}, bf16[3,32,160]{2,1,0:T(8,128)(2,1)S(1)}, u32[]{:S(2)}, u32[]{:S(2)}) collective-permute-start(bf16[3,32,160]{2,1,0:T(8,128)(2,1)} %get-tuple-element.14.refs_1_), channel_id=1, source_target_pairs={{0,16},{16,32},{32,48},{48,64},{64,80},{80,96},{96,112},{112,128},... | collective-permute-start | bytes 92168 | tf_op jit(solution)/shard_map/ppermute | solution.py:325
  65.9 11.2 %collective-permute-start.1 = (bf16[3,32,160]{2,1,0:T(8,128)(2,1)}, bf16[3,32,160]{2,1,0:T(8,128)(2,1)S(1)}, u32[]{:S(2)}, u32[]{:S(2)}) collective-permute-start(bf16[3,32,160]{2,1,0:T(8,128)(2,1)} %get-tuple-element.14.refs_1_), channel_id=1, source_target_pairs={{16,0},{32,16},{48,32},{64,48},{80,64},{96,80},{112,96},{128,112},... | collective-permute-start | bytes 92168 | tf_op jit(solution)/shard_map/ppermute | solution.py:326
  75.6 1.5 copy-start.7
  77.1 0.6 copy-start.8
  77.1 0.6 copy-start.6
  95.1 13.4 %collective-permute-start.2 = (f32[80,128]{1,0:T(8,128)S(1)}, f32[80,128]{1,0:T(8,128)S(1)}, u32[]{:S(2)}, u32[]{:S(2)}) collective-permute-start(f32[80,128]{1,0:T(8,128)S(1)} %shard_map.111.refs_0_), channel_id=1, source_target_pairs={{0,2},{2,0},{1,3},{3,1},{4,6},{6,4},{5,7},{7,5},{8,10},{10,8},{9,1... | collective-permute-start | bytes 122888 | tf_op jit(solution)/shard_map/ppermute | solution.py:336
  109.3 13.0 %all-to-all-start.2 = ((bf16[8,80,128]{2,1,0:T(8,128)(2,1)}), bf16[8,80,128]{2,1,0:T(8,128)(2,1)S(1)}, u32[]{:S(2)}, u32[]{:S(2)}) async-start(bf16[8,80,128]{2,1,0:T(8,128)(2,1)} %shard_map.112), calls=%async_computation.2 | async-start | bytes 327680 | tf_op jit(solution)/shard_map/all_to_all | solution.py:338
  123.3 39.1 %all-to-all-start.3 = ((f32[32,1,128]{2,1,0:T(1,128)}), f32[32,1,128]{2,1,0:T(1,128)S(1)}, u32[]{:S(2)}, u32[]{:S(2)}) async-start(f32[32,1,128]{2,1,0:T(1,128)} %shard_map.113), calls=%async_computation.3 | async-start | bytes 32768 | tf_op jit(solution)/shard_map/all_to_all | solution.py:340
  134.4 28.0 %collective-permute-start.3 = (bf16[8,80,128]{2,1,0:T(8,128)(2,1)S(1)}, bf16[8,80,128]{2,1,0:T(8,128)(2,1)S(1)}, u32[]{:S(2)}, u32[]{:S(2)}) collective-permute-start(bf16[8,80,128]{2,1,0:T(8,128)(2,1)S(1)} %all-to-all-done.2.refs_0_.refs_1_), channel_id=1, source_target_pairs={{0,16},{2,18},{16,32},{18,34},{32,48},{34,50},{48,64},{50,66},{64,... | collective-permute-start | bytes 491528 | tf_op jit(solution)/shard_map/ppermute | solution.py:357
  137.5 24.9 %collective-permute-start.4 = (bf16[8,80,128]{2,1,0:T(8,128)(2,1)S(1)}, bf16[8,80,128]{2,1,0:T(8,128)(2,1)S(1)}, u32[]{:S(2)}, u32[]{:S(2)}) collective-permute-start(bf16[8,80,128]{2,1,0:T(8,128)(2,1)S(1)} %all-to-all-done.2.refs_0_.refs_1_), channel_id=1, source_target_pairs={{16,0},{18,2},{32,16},{34,18},{48,32},{50,34},{64,48},{66,50},{80,... | collective-permute-start | bytes 491528 | tf_op jit(solution)/shard_map/ppermute | solution.py:358
  147.2 1.2 copy-start
  147.5 14.6 %copy-start.3 = (f32[512]{0:T(512)S(1)}, f32[512]{0:T(512)}, u32[]{:S(2)}) copy-start(f32[512]{0:T(512)} %param.18) | copy-start | bytes 6148
  147.5 14.6 %copy-start.4 = (f32[512]{0:T(512)S(1)}, f32[512]{0:T(512)}, u32[]{:S(2)}) copy-start(f32[512]{0:T(512)} %param.19) | copy-start | bytes 6148
  147.5 14.6 %copy-start.5 = (f32[512]{0:T(512)S(1)}, f32[512]{0:T(512)}, u32[]{:S(2)}) copy-start(f32[512]{0:T(512)} %param.21) | copy-start | bytes 6148
  149.3 13.2 %collective-permute-start.10 = (f32[64,160]{1,0:T(8,128)S(1)}, f32[64,160]{1,0:T(8,128)S(1)}, u32[]{:S(2)}, u32[]{:S(2)}) collective-permute-start(f32[64,160]{1,0:T(8,128)S(1)} %get-tuple-element.18), channel_id=1, source_target_pairs={{0,16},{16,32},{32,48},{48,64},{64,80},{80,96},{96,112},{112,128},... | collective-permute-start | bytes 122888 | tf_op jit(solution)/shard_map/ppermute | solution.py:378
  151.2 12.2 %collective-permute-start.11 = (f32[64,160]{1,0:T(8,128)S(1)}, f32[64,160]{1,0:T(8,128)S(1)}, u32[]{:S(2)}, u32[]{:S(2)}) collective-permute-start(f32[64,160]{1,0:T(8,128)S(1)} %get-tuple-element.19), channel_id=1, source_target_pairs={{16,0},{32,16},{48,32},{64,48},{80,64},{96,80},{112,96},{128,112},... | collective-permute-start | bytes 122888 | tf_op jit(solution)/shard_map/ppermute | solution.py:379

commit v5 on v3

--- a/solution.py
+++ b/solution.py
@@ -192,8 +192,22 @@
     )
 
 
-def row_stats(gathered, peers):
-    return partial_stats(rows_of(gathered), peers)
+def row_stats(gathered, to_above, to_below, peers):
+    return (
+        partial_stats(rows_of(gathered), peers),
+        jnp.concatenate([gathered, to_above], axis=0),
+        jnp.concatenate([gathered, to_below], axis=0),
+    )
+
+
+def halves(a):
+    a = pack(a)
+    high = a.astype(BF16)
+    return jnp.stack([high, (a - high.astype(F32)).astype(BF16)])
+
+
+def whole(blocks):
+    return unpack(blocks[0].astype(F32) + blocks[1].astype(F32))
 
 
 def taps(prod):
@@ -234,7 +248,7 @@
             axis=0,
         )
 
-    return jnp.concatenate([out(0), out(1)], axis=0), out(-1), out(2)
+    return jnp.concatenate([out(0), out(1)], axis=0), halves(out(-1)), halves(out(2))
 
 
 def up_columns(gain, bias, out_bias):
@@ -253,8 +267,9 @@
     )
 
 
-def up_conv(parts, row, above, below, affine, lhs, held, from_above, from_below, out_bias, sizes):
-    row, above, below = rows_of(row), rows_of(above), rows_of(below)
+def up_conv(parts, row, above, below, affine, lhs, held, out_bias, sizes):
+    from_above, from_below = whole(above[8:]), whole(below[8:])
+    row, above, below = rows_of(row), rows_of(above[:8]), rows_of(below[:8])
     chans, cols = row.shape
     groups = chans // GS
     mean, scale = merge_stats(parts, groups, GS * cols)
@@ -299,7 +314,6 @@
     peers = n_y * n_l
     cols, chans = latent.shape[2], latent.shape[3]
     sizes = (n_y, n_l)
-    hi = lax.axis_index("h")
     space = ("y", "l")
     own = latent[0, 0].T
     stats, raw, affine = run(
@@ -325,46 +339,28 @@
     other = lax.ppermute(mine, "h", [(0, 1), (1, 0)])
     gathered = run(merge, ((8, 80, 128), BF16), (mine, other))
     gathered = lax.all_to_all(gathered, ("x", "k"), 0, 0, tiled=True)
-    stats2 = run(functools.partial(row_stats, peers=peers), ((peers, 1, 128), F32), (gathered,))
-    stats2 = lax.all_to_all(stats2, space, 0, 0, tiled=True)
-
-    def at(y, l, h):
-        return (y * n_l + l) * 2 + h
-
-    down_h, up_h = [], []
-    for y in range(n_y):
-        for l in range(n_l):
-            for h in range(2):
-                if l < n_l - 1:
-                    pair = (at(y, l, h), at(y, l + 1, h))
-                elif y < n_y - 1:
-                    pair = (at(y, l, h), at(y + 1, 0, 1 - h))
-                else:
-                    continue
-                down_h.append(pair)
-                up_h.append(pair[::-1])
-    row_above = lax.ppermute(gathered, ("y", "l", "h"), down_h)
-    row_below = lax.ppermute(gathered, ("y", "l", "h"), up_h)
-
-    tile = cache_up.reshape(2, 2, 10, 2, 512).transpose(0, 1, 3, 2, 4)
-    swapped = lax.ppermute(tile, "h", [(0, 1), (1, 0)])
-    pair = jnp.where(hi == 0, jnp.stack([tile, swapped]), jnp.stack([swapped, tile]))
-    copies = jnp.broadcast_to(pair[None], (8,) + pair.shape)
-    spread = lax.all_to_all(copies, ("x", "k"), 0, 0, tiled=True)
+    tile = cache_up.reshape(2, 2, 10, 2, 512).transpose(0, 1, 3, 2, 4).reshape(80, 512)
+    spread = lax.all_gather(tile, ("x", "h", "k"))
     images = (
-        spread.reshape(4, 2, 2, 2, 2, 2, 10, 512)
-        .transpose(3, 4, 5, 0, 2, 1, 6, 7)
+        spread.reshape(16, 2, 2, 2, 10, 512)
+        .transpose(1, 2, 3, 0, 4, 5)
         .reshape(2, 2, 2, cols, 512)
     )
     kernel2 = conv2_weight.transpose(0, 1, 2, 4, 3).reshape(27 * 32, 512)
     held, to_above, to_below = run(
         cache_conv,
-        [((128, cols), F32), ((64, cols), F32), ((64, cols), F32)],
+        [((128, cols), F32), ((2, 80, 128), BF16), ((2, 80, 128), BF16)],
         (images, kernel2),
         16,
     )
-    from_above = lax.ppermute(to_below, space, down)
-    from_below = lax.ppermute(to_above, space, up)
+    stats2, going_up, going_down = run(
+        functools.partial(row_stats, peers=peers),
+        [((peers, 1, 128), F32), ((10, 80, 128), BF16), ((10, 80, 128), BF16)],
+        (gathered, to_above, to_below),
+    )
+    row_above = lax.ppermute(going_down, space, down)
+    row_below = lax.ppermute(going_up, space, up)
+    stats2 = lax.all_to_all(stats2, space, 0, 0, tiled=True)
     affine2, bias_here = run(
         up_columns,
         [((512, 2), F32), ((128, 1), F32)],
@@ -382,8 +378,6 @@
             affine2,
             lhs,
             held,
-            from_above,
-            from_below,
             bias_here,
         ),
         16,

time: 159 us -> 164 us (1.031)
  the two profiles are of different devices: /device:TPU:9 before, /device:TPU:1 now
where the time goes in v5:
time: 164 us; the launch traced here: 163 us
  starting transfers between devices  49.2 us (30%)
  waiting for transfers between devices  44.9 us (27%)
  blocking collectives  37.7 us (23%)
  between operations  13.6 us (8%)
  Pallas kernels  10.1 us (6%)
  local copies, waits for them, and re-layouts  7.7 us (5%)
    all_to_all x1, blocking collectives, on_device(): out = lax.all_to_all(out, ('x', 'h', 'k'), 0, 0, tiled=True)  23.3 us
    all_gather x1, waiting for transfers between devices, on_device(): spread = lax.all_gather(tile, ('x', 'h', 'k'))  20.8 us
    all_to_all x1, starting transfers between devices, on_device(): stats = lax.all_to_all(stats, space, 0, 0, tiled=True)  16.2 us
    all_to_all x1, blocking collectives, on_device(): partial = lax.all_to_all(partial, ('x', 'k'), 0, 0, tiled=True)  14.4 us
    all_to_all x1, starting transfers between devices, on_device(): stats2 = lax.all_to_all(stats2, space, 0, 0, tiled=True)  13.4 us
    all_to_all x1, waiting for transfers between devices, on_device(): stats2 = lax.all_to_all(stats2, space, 0, 0, tiled=True)  10.9 us
    pallas_call x9, Pallas kernels, run(): pl.pallas_call(body, out_shape=[jax.ShapeDtypeStruct(s, d) for s, d in sh...  10.1 us
    ppermute x1, starting transfers between devices, on_device(): other = lax.ppermute(mine, 'h', [(0, 1), (1, 0)])  7.4 us
  transfers between devices with their start and end apart: 9, of which 6 were waited for; matrix products, arithmetic and copies ran while one was open for 2% of the time, Pallas kernels for 5%

profile of v5, /device:TPU:1, one launch (start us, length us, event | category | flops | bytes accessed | tf_op | source)
XLA Modules:
  0.0 163.1 jit_solution(10047086994215259462)
XLA Ops:
  6.5 0.0 all-gather.2.cloned.1.call-start
  6.5 0.0 copy-start.2
  6.5 0.9 copy.31
  7.5 0.7 all_gather_reshape.3
  8.1 0.0 all-gather.2.cloned.1.call-update
  8.2 1.6 %shard_map.109 = (f32[32,1,128]{2,1,0:T(1,128)}, bf16[3,32,160]{2,1,0:T(8,128)(2,1)}, f32[32,3]{1,0:T(8,128)}) custom-call(bf16[32,160]{1,0:T(8,128)(2,1)} %bitcast.33, bf16[2,32,160]{2,1,0:T(8,128)(2,1)} %bitcast.44, f32[1,32]{1,0:T(1,128)} %bitcast.45, f32[1,32]{1,0:T(1,128)} %bitcast.46, f32[1,32]{1,0:T(1,128)} %bitcast.47), custom_call_target="tpu_custom_call" | custom-call | tf_op jit(solution)/shard_map/pallas_call | solution.py:49
  9.8 0.0 copy-start.1
  9.8 16.2 %all-to-all-start = ((f32[32,1,128]{2,1,0:T(1,128)}), f32[32,1,128]{2,1,0:T(1,128)S(1)}, u32[]{:S(2)}, u32[]{:S(2)}) async-start(f32[32,1,128]{2,1,0:T(1,128)} %get-tuple-element.16), calls=%async_computation | async-start | bytes 32768 | tf_op jit(solution)/shard_map/all_to_all | solution.py:325
  26.0 3.1 %collective-permute-start = (bf16[3,32,160]{2,1,0:T(8,128)(2,1)}, bf16[3,32,160]{2,1,0:T(8,128)(2,1)S(1)}, u32[]{:S(2)}, u32[]{:S(2)}) collective-permute-start(bf16[3,32,160]{2,1,0:T(8,128)(2,1)} %get-tuple-element.17.refs_1_), channel_id=1, source_target_pairs={{0,16},{16,32},{32,48},{48,64},{64,80},{80,96},{96,112},{112,128},... | collective-permute-start | bytes 92168 | tf_op jit(solution)/shard_map/ppermute | solution.py:328
  29.2 1.3 collective-permute-start.1
  30.5 0.2 collective-permute-done.refs_2_
  30.6 0.0 copy-start.7
  30.6 3.9 %collective-permute-done.1.refs_3_ = bf16[3,32,160]{2,1,0:T(8,128)(2,1)S(1)} collective-permute-done((bf16[3,32,160]{2,1,0:T(8,128)(2,1)}, bf16[3,32,160]{2,1,0:T(8,128)(2,1)S(1)}, u32[]{:S(2)}, u32[]{:S(2)}) %collective-permute-start.1) | collective-permute-done | bytes 30752 | tf_op jit(solution)/shard_map/ppermute | solution.py:329
  34.5 0.0 copy-start.8
  34.5 2.8 %all-to-all-done.refs_0_ = f32[32,1,128]{2,1,0:T(1,128)S(1)} async-done(((f32[32,1,128]{2,1,0:T(1,128)}), f32[32,1,128]{2,1,0:T(1,128)S(1)}, u32[]{:S(2)}, u32[]{:S(2)}) %all-to-all-start) | async-done | bytes 16416 | tf_op jit(solution)/shard_map/all_to_all | solution.py:325
  37.3 0.0 copy-start.6
  37.3 0.0 copy-done.7
  37.3 0.0 copy-done.8
  37.3 0.6 copy-done.6
  37.9 3.8 %shard_map.110 = f32[8,80,128]{2,1,0:T(8,128)} custom-call(f32[32,1,128]{2,1,0:T(1,128)} %copy-done.6, bf16[3,32,160]{2,1,0:T(8,128)(2,1)} %get-tuple-element.17.refs_1_, bf16[3,32,160]{2,1,0:T(8,128)(2,1)} %copy-done.7, bf16[3,32,160]{2,1,0:T(8,128)(2,1)} %copy-done.8, f32[32,3]{1,0:T(8,128)} %get-tuple-element.18.refs_4_.refs_2_, bf16[864,512]{1,0:T(8,128)(2,1)} %bitcast.40), custom_call_target="tpu_custom_call" | custom-call | tf_op jit(solution)/shard_map/pallas_call | solution.py:49
  41.7 14.4 %all_to_all.25.refs_0_ = f32[8,80,128]{2,1,0:T(8,128)S(1)} all-to-all(f32[8,80,128]{2,1,0:T(8,128)} %shard_map.110), channel_id=1, replica_groups=mesh['y'=4,'l'=8,'x'=4,'h'=2,'k'=2] {'x','k'}, dimensions={0} | all-to-all | bytes 655360 | tf_op jit(solution)/shard_map/all_to_all | solution.py:337
  56.1 0.0 copy-done.2
  56.1 0.0 copy-done.1
  56.1 0.2 shard_map.111.refs_0_
  56.2 7.4 %collective-permute-start.2 = (f32[80,128]{1,0:T(8,128)S(1)}, f32[80,128]{1,0:T(8,128)S(1)}, u32[]{:S(2)}, u32[]{:S(2)}) collective-permute-start(f32[80,128]{1,0:T(8,128)S(1)} %shard_map.111.refs_0_), channel_id=1, source_target_pairs={{0,2},{2,0},{1,3},{3,1},{4,6},{6,4},{5,7},{7,5},{8,10},{10,8},{9,1... | collective-permute-start | bytes 122888 | tf_op jit(solution)/shard_map/ppermute | solution.py:339
  63.7 6.2 %collective-permute-done.2.refs_1_ = f32[80,128]{1,0:T(8,128)S(1)} collective-permute-done((f32[80,128]{1,0:T(8,128)S(1)}, f32[80,128]{1,0:T(8,128)S(1)}, u32[]{:S(2)}, u32[]{:S(2)}) %collective-permute-start.2) | collective-permute-done | bytes 40992 | tf_op jit(solution)/shard_map/ppermute | solution.py:339
  69.9 0.7 shard_map.112
  70.5 5.2 %all-to-all-start.2 = ((bf16[8,80,128]{2,1,0:T(8,128)(2,1)}), bf16[8,80,128]{2,1,0:T(8,128)(2,1)S(1)}, u32[]{:S(2)}, u32[]{:S(2)}) async-start(bf16[8,80,128]{2,1,0:T(8,128)(2,1)} %shard_map.112), calls=%async_computation.2 | async-start | bytes 327680 | tf_op jit(solution)/shard_map/all_to_all | solution.py:341
  75.7 20.8 %all-gather.2.cloned.1.call-done = bf16[16,80,512]{2,1,0:T(8,128)(2,1)} async-done(((bf16[1,80,512]{2,1,0:T(8,128)(2,1)}), bf16[16,80,512]{2,1,0:T(8,128)(2,1)}) %all-gather.2.cloned.1.call-update) | async-done | bytes 1310736 | tf_op jit(solution)/shard_map/all_gather | solution.py:343
  96.5 2.0 %copy.25 = bf16[16,80,512]{2,0,1:T(8,128)(2,1)S(1)} copy(bf16[16,80,512]{2,1,0:T(8,128)(2,1)} %all-gather.2.cloned.1.call-done) | data formatting | bytes 2621440 | tf_op jit(solution)/shard_map/all_gather | solution.py:343
  98.6 1.4 copy.26
  99.9 0.0 copy-start
  100.0 0.2 copy.27.refs_0_
  100.2 0.9 copy-done
  101.1 0.0 copy-start.3
  101.1 0.0 copy-start.4
  101.1 0.0 copy-start.5
  101.1 0.9 shard_map.113
  102.0 0.0 all-to-all-done.2.refs_0_.refs_1_
  102.0 1.1 shard_map.114
  103.0 1.3 collective-permute-start.3
  104.3 1.3 collective-permute-start.4
  105.6 13.4 %all-to-all-start.3 = ((f32[32,1,128]{2,1,0:T(1,128)}), f32[32,1,128]{2,1,0:T(1,128)S(1)}, u32[]{:S(2)}, u32[]{:S(2)}) async-start(f32[32,1,128]{2,1,0:T(1,128)} %get-tuple-element.21), calls=%async_computation.3 | async-start | bytes 32768 | tf_op jit(solution)/shard_map/all_to_all | solution.py:363
  119.1 0.0 copy-done.3
  119.1 0.0 copy-done.4
  119.1 0.0 copy-done.5
  119.1 0.3 shard_map.115
  119.4 10.9 %all-to-all-done.3.refs_0_ = f32[32,1,128]{2,1,0:T(1,128)S(1)} async-done(((f32[32,1,128]{2,1,0:T(1,128)}), f32[32,1,128]{2,1,0:T(1,128)S(1)}, u32[]{:S(2)}, u32[]{:S(2)}) %all-to-all-start.3) | async-done | bytes 16416 | tf_op jit(solution)/shard_map/all_to_all | solution.py:363
  130.3 0.0 collective-permute-done.3.refs_2_
  130.3 0.0 collective-permute-done.4.refs_3_
  130.3 1.7 %shard_map.117 = bf16[16,10,128]{2,1,0:T(8,128)(2,1)S(1)} custom-call(f32[32,1,128]{2,1,0:T(1,128)S(1)} %all-to-all-done.3.refs_0_, bf16[8,80,128]{2,1,0:T(8,128)(2,1)S(1)} %all-to-all-done.2.refs_0_.refs_1_, bf16[10,80,128]{2,1,0:T(8,128)(2,1)S(1)} %collective-permute-done.3.refs_2_, bf16[10,80,128]{2,1,0:T(8,128)(2,1)S(1)} %collective-permute-done.4.refs_3_, ...), custom_call_target="tpu_custom_call" | custom-call | tf_op jit(solution)/shard_map/pallas_call | solution.py:49
  132.0 23.3 %all_to_all.26 = bf16[16,10,128]{2,1,0:T(8,128)(2,1)S(1)} all-to-all(bf16[16,10,128]{2,1,0:T(8,128)(2,1)S(1)} %shard_map.117), channel_id=1, replica_groups=mesh['y'=4,'l'=8,'x'=4,'h'=2,'k'=2] {'x','h','k'}, dimensions={0} | all-to-all | bytes 81920 | tf_op jit(solution)/shard_map/all_to_all | solution.py:385
  155.3 0.1 reshape.26
  155.5 0.8 reshape.27
  (3 shorter events, 0.1 us)
Async XLA Ops:
  6.5 90.0 %all-gather.2.cloned.1.call-start = ((), (), s32[]{:S(2)}) async-start(), calls=%async_computation.5 | async-start | bytes 1392640 | tf_op jit(solution)/shard_map/all_gather | solution.py:343
  6.5 49.5 %copy-start.2 = (bf16[1,1,160,32]{2,3,1,0:T(8,128)(2,1)S(1)}, bf16[1,1,160,32]{2,3,1,0:T(8,128)(2,1)}, u32[]{:S(2)}) copy-start(bf16[1,1,160,32]{2,3,1,0:T(8,128)(2,1)} %param.11) | copy-start | bytes 30724
  9.8 46.3 %copy-start.1 = (f32[32,3]{1,0:T(8,128)S(1)}, f32[32,3]{1,0:T(8,128)}, u32[]{:S(2)}) copy-start(f32[32,3]{1,0:T(8,128)} %get-tuple-element.18.refs_4_.refs_2_) | copy-start | bytes 1156
  9.8 27.5 %all-to-all-start = ((f32[32,1,128]{2,1,0:T(1,128)}), f32[32,1,128]{2,1,0:T(1,128)S(1)}, u32[]{:S(2)}, u32[]{:S(2)}) async-start(f32[32,1,128]{2,1,0:T(1,128)} %get-tuple-element.16), calls=%async_computation | async-start | bytes 32768 | tf_op jit(solution)/shard_map/all_to_all | solution.py:325
  26.0 4.6 %collective-permute-start = (bf16[3,32,160]{2,1,0:T(8,128)(2,1)}, bf16[3,32,160]{2,1,0:T(8,128)(2,1)S(1)}, u32[]{:S(2)}, u32[]{:S(2)}) collective-permute-start(bf16[3,32,160]{2,1,0:T(8,128)(2,1)} %get-tuple-element.17.refs_1_), channel_id=1, source_target_pairs={{0,16},{16,32},{32,48},{48,64},{64,80},{80,96},{96,112},{112,128},... | collective-permute-start | bytes 92168 | tf_op jit(solution)/shard_map/ppermute | solution.py:328
  29.2 5.4 %collective-permute-start.1 = (bf16[3,32,160]{2,1,0:T(8,128)(2,1)}, bf16[3,32,160]{2,1,0:T(8,128)(2,1)S(1)}, u32[]{:S(2)}, u32[]{:S(2)}) collective-permute-start(bf16[3,32,160]{2,1,0:T(8,128)(2,1)} %get-tuple-element.17.refs_1_), channel_id=1, source_target_pairs={{16,0},{32,16},{48,32},{64,48},{80,64},{96,80},{112,96},{128,112},... | collective-permute-start | bytes 92168 | tf_op jit(solution)/shard_map/ppermute | solution.py:329
  30.6 6.7 %copy-start.7 = (bf16[3,32,160]{2,1,0:T(8,128)(2,1)}, bf16[3,32,160]{2,1,0:T(8,128)(2,1)S(1)}, u32[]{:S(2)}) copy-start(bf16[3,32,160]{2,1,0:T(8,128)(2,1)S(1)} %collective-permute-done.refs_2_) | copy-start | bytes 92164
  34.5 2.8 %copy-start.8 = (bf16[3,32,160]{2,1,0:T(8,128)(2,1)}, bf16[3,32,160]{2,1,0:T(8,128)(2,1)S(1)}, u32[]{:S(2)}) copy-start(bf16[3,32,160]{2,1,0:T(8,128)(2,1)S(1)} %collective-permute-done.1.refs_3_) | copy-start | bytes 92164
  37.3 0.6 copy-start.6
  56.2 13.6 %collective-permute-start.2 = (f32[80,128]{1,0:T(8,128)S(1)}, f32[80,128]{1,0:T(8,128)S(1)}, u32[]{:S(2)}, u32[]{:S(2)}) collective-permute-start(f32[80,128]{1,0:T(8,128)S(1)} %shard_map.111.refs_0_), channel_id=1, source_target_pairs={{0,2},{2,0},{1,3},{3,1},{4,6},{6,4},{5,7},{7,5},{8,10},{10,8},{9,1... | collective-permute-start | bytes 122888 | tf_op jit(solution)/shard_map/ppermute | solution.py:339
  70.5 31.4 %all-to-all-start.2 = ((bf16[8,80,128]{2,1,0:T(8,128)(2,1)}), bf16[8,80,128]{2,1,0:T(8,128)(2,1)S(1)}, u32[]{:S(2)}, u32[]{:S(2)}) async-start(bf16[8,80,128]{2,1,0:T(8,128)(2,1)} %shard_map.112), calls=%async_computation.2 | async-start | bytes 327680 | tf_op jit(solution)/shard_map/all_to_all | solution.py:341
  99.9 1.2 copy-start
  101.1 17.9 %copy-start.3 = (f32[512]{0:T(512)S(1)}, f32[512]{0:T(512)}, u32[]{:S(2)}) copy-start(f32[512]{0:T(512)} %param.18) | copy-start | bytes 6148
  101.1 17.9 %copy-start.4 = (f32[512]{0:T(512)S(1)}, f32[512]{0:T(512)}, u32[]{:S(2)}) copy-start(f32[512]{0:T(512)} %param.19) | copy-start | bytes 6148
  101.1 18.0 %copy-start.5 = (f32[512]{0:T(512)S(1)}, f32[512]{0:T(512)}, u32[]{:S(2)}) copy-start(f32[512]{0:T(512)} %param.21) | copy-start | bytes 6148
  103.0 27.3 %collective-permute-start.3 = (bf16[10,80,128]{2,1,0:T(8,128)(2,1)S(1)}, bf16[10,80,128]{2,1,0:T(8,128)(2,1)S(1)}, u32[]{:S(2)}, u32[]{:S(2)}) collective-permute-start(bf16[10,80,128]{2,1,0:T(8,128)(2,1)S(1)} %get-tuple-element.22), channel_id=1, source_target_pairs={{0,16},{16,32},{32,48},{48,64},{64,80},{80,96},{96,112},{112,128},... | collective-permute-start | bytes 614408 | tf_op jit(solution)/shard_map/ppermute | solution.py:361
  104.3 26.0 %collective-permute-start.4 = (bf16[10,80,128]{2,1,0:T(8,128)(2,1)S(1)}, bf16[10,80,128]{2,1,0:T(8,128)(2,1)S(1)}, u32[]{:S(2)}, u32[]{:S(2)}) collective-permute-start(bf16[10,80,128]{2,1,0:T(8,128)(2,1)S(1)} %get-tuple-element.23), channel_id=1, source_target_pairs={{16,0},{32,16},{48,32},{64,48},{80,64},{96,80},{112,96},{128,112},... | collective-permute-start | bytes 614408 | tf_op jit(solution)/shard_map/ppermute | solution.py:362
  105.6 24.7 %all-to-all-start.3 = ((f32[32,1,128]{2,1,0:T(1,128)}), f32[32,1,128]{2,1,0:T(1,128)S(1)}, u32[]{:S(2)}, u32[]{:S(2)}) async-start(f32[32,1,128]{2,1,0:T(1,128)} %get-tuple-element.21), calls=%async_computation.3 | async-start | bytes 32768 | tf_op jit(solution)/shard_map/all_to_all | solution.py:363
Sparse Core Ops, SparseCore 0:
  10.6 85.8 all-gather.1

commit v6 on v5

--- a/solution.py
+++ b/solution.py
@@ -314,6 +314,7 @@
     peers = n_y * n_l
     cols, chans = latent.shape[2], latent.shape[3]
     sizes = (n_y, n_l)
+    hi = lax.axis_index("h")
     space = ("y", "l")
     own = latent[0, 0].T
     stats, raw, affine = run(
@@ -339,11 +340,14 @@
     other = lax.ppermute(mine, "h", [(0, 1), (1, 0)])
     gathered = run(merge, ((8, 80, 128), BF16), (mine, other))
     gathered = lax.all_to_all(gathered, ("x", "k"), 0, 0, tiled=True)
-    tile = cache_up.reshape(2, 2, 10, 2, 512).transpose(0, 1, 3, 2, 4).reshape(80, 512)
-    spread = lax.all_gather(tile, ("x", "h", "k"))
+    tile = cache_up.reshape(2, 2, 10, 2, 512).transpose(0, 1, 3, 2, 4)
+    swapped = lax.ppermute(tile, "h", [(0, 1), (1, 0)])
+    pair = jnp.where(hi == 0, jnp.stack([tile, swapped]), jnp.stack([swapped, tile]))
+    copies = jnp.broadcast_to(pair[None], (8,) + pair.shape)
+    spread = lax.all_to_all(copies, ("x", "k"), 0, 0, tiled=True)
     images = (
-        spread.reshape(16, 2, 2, 2, 10, 512)
-        .transpose(1, 2, 3, 0, 4, 5)
+        spread.reshape(4, 2, 2, 2, 2, 2, 10, 512)
+        .transpose(3, 4, 5, 0, 2, 1, 6, 7)
         .reshape(2, 2, 2, cols, 512)
     )
     kernel2 = conv2_weight.transpose(0, 1, 2, 4, 3).reshape(27 * 32, 512)

time: 164 us -> 155 us (0.945)
  starting transfers between devices: 49.2 us -> 80.6 us
  blocking collectives: 37.7 us -> 23.5 us
  between operations: 13.6 us -> 0.21 us
  waiting for transfers between devices: 44.9 us -> 33.3 us
    all_gather x1 -> x0, waiting for transfers between devices: 20.8 us -> none  [on_device(): spread = lax.all_gather(tile, ('x', 'h', 'k'))]
    all_to_all x1 -> x0, blocking collectives: 14.4 us -> none  [on_device(): partial = lax.all_to_all(partial, ('x', 'k'), 0, 0, tiled=True)]
    all_to_all x0 -> x2, starting transfers between devices: none -> 12.1 us  [the longest x1 6.41 us: on_device(): partial = lax.all_to_all(partial, ('x', 'k'), 0, 0, tiled=True)]
    all_to_all x1, starting transfers between devices: 13.4 us -> 21.9 us  [on_device(): stats2 = lax.all_to_all(stats2, space, 0, 0, tiled=True)]
    ppermute x0 -> x1, starting transfers between devices: none -> 7.93 us  [on_device(): swapped = lax.ppermute(tile, 'h', [(0, 1), (1, 0)])]
    ppermute x0 -> x1, waiting for transfers between devices: none -> 6.69 us  [on_device(): swapped = lax.ppermute(tile, 'h', [(0, 1), (1, 0)])]
    all_to_all x0 -> x2, waiting for transfers between devices: none -> 3.49 us  [the longest x1 3.49 us: on_device(): spread = lax.all_to_all(copies, ('x', 'k'), 0, 0, tiled=True)]
    ppermute x1, waiting for transfers between devices: 6.21 us -> 3.01 us  [on_device(): other = lax.ppermute(mine, 'h', [(0, 1), (1, 0)])]
  transfers between devices with their start and end apart: 9 -> 11, of which waited for: 6 -> 8; matrix products, arithmetic and copies ran while one was open for 2% -> 1% of each run, Pallas kernels for 5% -> 1%
where the time goes in v6:
time: 155 us; the launch traced here: 154 us
  starting transfers between devices  80.6 us (52%)
  waiting for transfers between devices  33.3 us (21%)
  blocking collectives  23.5 us (15%)
  Pallas kernels  10.1 us (7%)
  local copies, waits for them, and re-layouts  6.15 us (4%)
    all_to_all x1, blocking collectives, on_device(): out = lax.all_to_all(out, ('x', 'h', 'k'), 0, 0, tiled=True)  23.5 us
    all_to_all x1, starting transfers between devices, on_device(): stats2 = lax.all_to_all(stats2, space, 0, 0, tiled=True)  21.9 us
    all_to_all x1, starting transfers between devices, on_device(): stats = lax.all_to_all(stats, space, 0, 0, tiled=True)  16.1 us
    all_to_all x1, waiting for transfers between devices, on_device(): stats2 = lax.all_to_all(stats2, space, 0, 0, tiled=True)  10.9 us
    ppermute x1, starting transfers between devices, on_device(): other = lax.ppermute(mine, 'h', [(0, 1), (1, 0)])  10.4 us
    pallas_call x9, Pallas kernels, run(): pl.pallas_call(body, out_shape=[jax.ShapeDtypeStruct(s, d) for s, d in sh...  10.1 us
    ppermute x1, starting transfers between devices, on_device(): swapped = lax.ppermute(tile, 'h', [(0, 1), (1, 0)])  7.93 us
    ppermute x1, waiting for transfers between devices, on_device(): swapped = lax.ppermute(tile, 'h', [(0, 1), (1, 0)])  6.69 us
  transfers between devices with their start and end apart: 11, of which 8 were waited for; matrix products, arithmetic and copies ran while one was open for 1% of the time, Pallas kernels for 1%

profile of v6, /device:TPU:1, one launch (start us, length us, event | category | flops | bytes accessed | tf_op | source)
XLA Modules:
  0.0 154.1 jit_solution(7807536266834189313)
XLA Ops:
  0.0 0.0 copy-start.6
  0.0 1.7 %shard_map.109 = (f32[32,1,128]{2,1,0:T(1,128)}, bf16[3,32,160]{2,1,0:T(8,128)(2,1)}, f32[32,3]{1,0:T(8,128)}) custom-call(bf16[32,160]{1,0:T(8,128)(2,1)} %bitcast.35, bf16[2,32,160]{2,1,0:T(8,128)(2,1)} %bitcast.47, f32[1,32]{1,0:T(1,128)} %bitcast.48, f32[1,32]{1,0:T(1,128)} %bitcast.49, f32[1,32]{1,0:T(1,128)} %bitcast.50), custom_call_target="tpu_custom_call" | custom-call | tf_op jit(solution)/shard_map/pallas_call | solution.py:49
  1.7 16.1 %all-to-all-start = ((f32[32,1,128]{2,1,0:T(1,128)}), f32[32,1,128]{2,1,0:T(1,128)S(1)}, u32[]{:S(2)}, u32[]{:S(2)}) async-start(f32[32,1,128]{2,1,0:T(1,128)} %get-tuple-element.16), calls=%async_computation | async-start | bytes 32768 | tf_op jit(solution)/shard_map/all_to_all | solution.py:326
  17.8 3.1 %collective-permute-start = (bf16[3,32,160]{2,1,0:T(8,128)(2,1)}, bf16[3,32,160]{2,1,0:T(8,128)(2,1)S(1)}, u32[]{:S(2)}, u32[]{:S(2)}) collective-permute-start(bf16[3,32,160]{2,1,0:T(8,128)(2,1)} %get-tuple-element.17.refs_1_), channel_id=1, source_target_pairs={{0,16},{16,32},{32,48},{48,64},{64,80},{80,96},{96,112},{112,128},... | collective-permute-start | bytes 92168 | tf_op jit(solution)/shard_map/ppermute | solution.py:329
  20.9 1.3 collective-permute-start.1
  22.2 0.2 collective-permute-done.refs_2_
  22.4 0.0 copy-start.8
  22.4 3.9 %collective-permute-done.1.refs_3_ = bf16[3,32,160]{2,1,0:T(8,128)(2,1)S(1)} collective-permute-done((bf16[3,32,160]{2,1,0:T(8,128)(2,1)}, bf16[3,32,160]{2,1,0:T(8,128)(2,1)S(1)}, u32[]{:S(2)}, u32[]{:S(2)}) %collective-permute-start.1) | collective-permute-done | bytes 30752 | tf_op jit(solution)/shard_map/ppermute | solution.py:330
  26.3 0.0 copy-start.9
  26.3 2.8 %all-to-all-done.refs_0_ = f32[32,1,128]{2,1,0:T(1,128)S(1)} async-done(((f32[32,1,128]{2,1,0:T(1,128)}), f32[32,1,128]{2,1,0:T(1,128)S(1)}, u32[]{:S(2)}, u32[]{:S(2)}) %all-to-all-start) | async-done | bytes 16416 | tf_op jit(solution)/shard_map/all_to_all | solution.py:326
  29.1 0.0 copy-start.7
  29.1 0.0 copy-done.8
  29.1 0.0 copy-done.9
  29.1 0.6 copy-done.7
  29.7 3.7 %shard_map.110 = f32[8,80,128]{2,1,0:T(8,128)} custom-call(f32[32,1,128]{2,1,0:T(1,128)} %copy-done.7, bf16[3,32,160]{2,1,0:T(8,128)(2,1)} %get-tuple-element.17.refs_1_, bf16[3,32,160]{2,1,0:T(8,128)(2,1)} %copy-done.8, bf16[3,32,160]{2,1,0:T(8,128)(2,1)} %copy-done.9, f32[32,3]{1,0:T(8,128)} %get-tuple-element.18.refs_4_.refs_2_, bf16[864,512]{1,0:T(8,128)(2,1)} %bitcast.42), custom_call_target="tpu_custom_call" | custom-call | tf_op jit(solution)/shard_map/pallas_call | solution.py:49
  33.4 6.4 %all-to-all-start.1 = ((f32[8,80,128]{2,1,0:T(8,128)}), f32[8,80,128]{2,1,0:T(8,128)S(1)}, u32[]{:S(2)}, u32[]{:S(2)}) async-start(f32[8,80,128]{2,1,0:T(8,128)} %shard_map.110), calls=%async_computation.1 | async-start | bytes 655360 | tf_op jit(solution)/shard_map/all_to_all | solution.py:338
  39.8 0.0 copy-done.6
  39.8 7.9 %collective-permute-start.3 = (bf16[2,2,2,10,512]{4,1,2,3,0:T(2,128)(2,1)S(1)}, bf16[2,2,2,10,512]{4,1,2,3,0:T(2,128)(2,1)S(1)}, u32[]{:S(2)}, u32[]{:S(2)}) collective-permute-start(bf16[2,2,2,10,512]{4,1,2,3,0:T(2,128)(2,1)S(1)} %bitcast.44), channel_id=1, source_target_pairs={{0,2},{2,0},{1,3},{3,1},{4,6},{6,4},{5,7},{7,5},{8,10},{10,8},{9,1... | collective-permute-start | bytes 245768 | tf_op jit(solution)/shard_map/ppermute | solution.py:344
  47.8 6.7 %collective-permute-done.3 = bf16[2,2,2,10,512]{4,1,2,3,0:T(2,128)(2,1)S(1)} collective-permute-done((bf16[2,2,2,10,512]{4,1,2,3,0:T(2,128)(2,1)S(1)}, bf16[2,2,2,10,512]{4,1,2,3,0:T(2,128)(2,1)S(1)}, u32[]{:S(2)}, u32[]{:S(2)}) %collective-permute-start.3) | collective-permute-done | bytes 81952 | tf_op jit(solution)/shard_map/ppermute | solution.py:344
  54.4 0.2 broadcast_select_fusion
  54.7 0.1 copy.18
  54.8 0.0 all-to-all-done.1.refs_0_
  54.8 2.1 %broadcast_in_dim.27 = bf16[8,2,2,2,2,10,512]{6,4,5,3,2,1,0:T(2,128)(2,1)} broadcast(bf16[2,2,2,2,10,512]{5,3,4,2,1,0:T(2,128)(2,1)S(1)} %copy.18), dimensions={1,2,3,4,5,6} | broadcast | bytes 1474560 | tf_op jit(solution)/shard_map/broadcast_in_dim | solution.py:346
  56.9 0.0 copy-start.1
  56.9 0.0 copy-start.2
  56.9 5.7 %all-to-all-start.3 = ((bf16[8,2,2,2,2,10,512]{6,4,5,3,2,1,0:T(2,128)(2,1)}), bf16[8,2,2,2,2,10,512]{6,4,5,3,2,1,0:T(2,128)(2,1)S(1)}, u32[]{:S(2)}, u32[]{:S(2)}) async-start(bf16[8,2,2,2,2,10,512]{6,4,5,3,2,1,0:T(2,128)(2,1)} %broadcast_in_dim.27), calls=%async_computation.3 | async-start | bytes 2621440 | tf_op jit(solution)/shard_map/all_to_all | solution.py:347
  62.6 0.0 copy-done.1
  62.6 0.0 copy-done.2
  62.7 0.2 shard_map.111.refs_0_
  62.8 10.4 %collective-permute-start.2 = (f32[80,128]{1,0:T(8,128)S(1)}, f32[80,128]{1,0:T(8,128)S(1)}, u32[]{:S(2)}, u32[]{:S(2)}) collective-permute-start(f32[80,128]{1,0:T(8,128)S(1)} %shard_map.111.refs_0_), channel_id=1, source_target_pairs={{0,2},{2,0},{1,3},{3,1},{4,6},{6,4},{5,7},{7,5},{8,10},{10,8},{9,1... | collective-permute-start | bytes 122888 | tf_op jit(solution)/shard_map/ppermute | solution.py:340
  73.3 3.0 %collective-permute-done.2.refs_1_ = f32[80,128]{1,0:T(8,128)S(1)} collective-permute-done((f32[80,128]{1,0:T(8,128)S(1)}, f32[80,128]{1,0:T(8,128)S(1)}, u32[]{:S(2)}, u32[]{:S(2)}) %collective-permute-start.2) | collective-permute-done | bytes 40992 | tf_op jit(solution)/shard_map/ppermute | solution.py:340
  76.3 0.7 shard_map.112
  76.9 3.5 %all-to-all-done.3 = bf16[8,2,2,2,2,10,512]{6,4,5,3,2,1,0:T(2,128)(2,1)S(1)} async-done(((bf16[8,2,2,2,2,10,512]{6,4,5,3,2,1,0:T(2,128)(2,1)}), bf16[8,2,2,2,2,10,512]{6,4,5,3,2,1,0:T(2,128)(2,1)S(1)}, u32[]{:S(2)}, u32[]{:S(2)}) %all-to-all-start.3) | async-done | bytes 1310752 | tf_op jit(solution)/shard_map/all_to_all | solution.py:347
  80.4 4.3 %all-to-all-start.2 = ((bf16[8,80,128]{2,1,0:T(8,128)(2,1)}), bf16[8,80,128]{2,1,0:T(8,128)(2,1)S(1)}, u32[]{:S(2)}, u32[]{:S(2)}) async-start(bf16[8,80,128]{2,1,0:T(8,128)(2,1)} %shard_map.112), calls=%async_computation.2 | async-start | bytes 327680 | tf_op jit(solution)/shard_map/all_to_all | solution.py:342
  84.7 1.2 copy.19
  85.9 0.0 copy-start
  85.9 0.2 copy.20.refs_0_
  86.1 0.9 copy-done
  87.1 0.0 copy-start.3
  87.1 0.0 copy-start.4
  87.1 0.0 copy-start.5
  87.1 0.9 shard_map.113
  87.9 2.3 %all-to-all-done.2.refs_0_.refs_1_ = bf16[8,80,128]{2,1,0:T(8,128)(2,1)S(1)} async-done(((bf16[8,80,128]{2,1,0:T(8,128)(2,1)}), bf16[8,80,128]{2,1,0:T(8,128)(2,1)S(1)}, u32[]{:S(2)}, u32[]{:S(2)}) %all-to-all-start.2) | async-done | bytes 163872 | tf_op jit(solution)/shard_map/all_to_all | solution.py:342
  90.3 1.1 shard_map.114
  91.3 2.1 %collective-permute-start.4 = (bf16[10,80,128]{2,1,0:T(8,128)(2,1)S(1)}, bf16[10,80,128]{2,1,0:T(8,128)(2,1)S(1)}, u32[]{:S(2)}, u32[]{:S(2)}) collective-permute-start(bf16[10,80,128]{2,1,0:T(8,128)(2,1)S(1)} %get-tuple-element.22), channel_id=1, source_target_pairs={{0,16},{16,32},{32,48},{48,64},{64,80},{80,96},{96,112},{112,128},... | collective-permute-start | bytes 614408 | tf_op jit(solution)/shard_map/ppermute | solution.py:365
  93.4 1.3 collective-permute-start.5
  94.7 21.9 %all-to-all-start.4 = ((f32[32,1,128]{2,1,0:T(1,128)}), f32[32,1,128]{2,1,0:T(1,128)S(1)}, u32[]{:S(2)}, u32[]{:S(2)}) async-start(f32[32,1,128]{2,1,0:T(1,128)} %get-tuple-element.21), calls=%async_computation.4 | async-start | bytes 32768 | tf_op jit(solution)/shard_map/all_to_all | solution.py:367
  116.7 0.0 copy-done.3
  116.7 0.0 copy-done.4
  116.7 0.0 copy-done.5
  116.7 0.3 shard_map.115
  117.0 10.9 %all-to-all-done.4.refs_0_ = f32[32,1,128]{2,1,0:T(1,128)S(1)} async-done(((f32[32,1,128]{2,1,0:T(1,128)}), f32[32,1,128]{2,1,0:T(1,128)S(1)}, u32[]{:S(2)}, u32[]{:S(2)}) %all-to-all-start.4) | async-done | bytes 16416 | tf_op jit(solution)/shard_map/all_to_all | solution.py:367
  127.9 0.0 collective-permute-done.4.refs_2_
  127.9 0.0 collective-permute-done.5.refs_3_
  127.9 1.7 %shard_map.117 = bf16[16,10,128]{2,1,0:T(8,128)(2,1)S(1)} custom-call(f32[32,1,128]{2,1,0:T(1,128)S(1)} %all-to-all-done.4.refs_0_, bf16[8,80,128]{2,1,0:T(8,128)(2,1)S(1)} %all-to-all-done.2.refs_0_.refs_1_, bf16[10,80,128]{2,1,0:T(8,128)(2,1)S(1)} %collective-permute-done.4.refs_2_, bf16[10,80,128]{2,1,0:T(8,128)(2,1)S(1)} %collective-permute-done.5.refs_3_, ...), custom_call_target="tpu_custom_call" | custom-call | tf_op jit(solution)/shard_map/pallas_call | solution.py:49
  129.6 23.5 %all_to_all.30 = bf16[16,10,128]{2,1,0:T(8,128)(2,1)S(1)} all-to-all(bf16[16,10,128]{2,1,0:T(8,128)(2,1)S(1)} %shard_map.117), channel_id=1, replica_groups=mesh['y'=4,'l'=8,'x'=4,'h'=2,'k'=2] {'x','h','k'}, dimensions={0} | all-to-all | bytes 81920 | tf_op jit(solution)/shard_map/all_to_all | solution.py:389
  153.2 0.1 reshape.59
  153.3 0.8 reshape.60
  (3 shorter events, 0.1 us)
Async XLA Ops:
  0.0 39.8 %copy-start.6 = (bf16[2,2,20,512]{3,1,2,0:T(2,128)(2,1)S(1)}, bf16[2,2,20,512]{3,1,2,0:T(2,128)(2,1)}, u32[]{:S(2)}) copy-start(bf16[2,2,20,512]{3,1,2,0:T(2,128)(2,1)} %param.17) | copy-start | bytes 245764
  1.7 27.4 %all-to-all-start = ((f32[32,1,128]{2,1,0:T(1,128)}), f32[32,1,128]{2,1,0:T(1,128)S(1)}, u32[]{:S(2)}, u32[]{:S(2)}) async-start(f32[32,1,128]{2,1,0:T(1,128)} %get-tuple-element.16), calls=%async_computation | async-start | bytes 32768 | tf_op jit(solution)/shard_map/all_to_all | solution.py:326
  17.8 4.6 %collective-permute-start = (bf16[3,32,160]{2,1,0:T(8,128)(2,1)}, bf16[3,32,160]{2,1,0:T(8,128)(2,1)S(1)}, u32[]{:S(2)}, u32[]{:S(2)}) collective-permute-start(bf16[3,32,160]{2,1,0:T(8,128)(2,1)} %get-tuple-element.17.refs_1_), channel_id=1, source_target_pairs={{0,16},{16,32},{32,48},{48,64},{64,80},{80,96},{96,112},{112,128},... | collective-permute-start | bytes 92168 | tf_op jit(solution)/shard_map/ppermute | solution.py:329
  20.9 5.4 %collective-permute-start.1 = (bf16[3,32,160]{2,1,0:T(8,128)(2,1)}, bf16[3,32,160]{2,1,0:T(8,128)(2,1)S(1)}, u32[]{:S(2)}, u32[]{:S(2)}) collective-permute-start(bf16[3,32,160]{2,1,0:T(8,128)(2,1)} %get-tuple-element.17.refs_1_), channel_id=1, source_target_pairs={{16,0},{32,16},{48,32},{64,48},{80,64},{96,80},{112,96},{128,112},... | collective-permute-start | bytes 92168 | tf_op jit(solution)/shard_map/ppermute | solution.py:330
  22.4 6.7 %copy-start.8 = (bf16[3,32,160]{2,1,0:T(8,128)(2,1)}, bf16[3,32,160]{2,1,0:T(8,128)(2,1)S(1)}, u32[]{:S(2)}) copy-start(bf16[3,32,160]{2,1,0:T(8,128)(2,1)S(1)} %collective-permute-done.refs_2_) | copy-start | bytes 92164
  26.3 2.8 %copy-start.9 = (bf16[3,32,160]{2,1,0:T(8,128)(2,1)}, bf16[3,32,160]{2,1,0:T(8,128)(2,1)S(1)}, u32[]{:S(2)}) copy-start(bf16[3,32,160]{2,1,0:T(8,128)(2,1)S(1)} %collective-permute-done.1.refs_3_) | copy-start | bytes 92164
  29.1 0.6 copy-start.7
  33.4 21.4 %all-to-all-start.1 = ((f32[8,80,128]{2,1,0:T(8,128)}), f32[8,80,128]{2,1,0:T(8,128)S(1)}, u32[]{:S(2)}, u32[]{:S(2)}) async-start(f32[8,80,128]{2,1,0:T(8,128)} %shard_map.110), calls=%async_computation.1 | async-start | bytes 655360 | tf_op jit(solution)/shard_map/all_to_all | solution.py:338
  39.8 14.6 %collective-permute-start.3 = (bf16[2,2,2,10,512]{4,1,2,3,0:T(2,128)(2,1)S(1)}, bf16[2,2,2,10,512]{4,1,2,3,0:T(2,128)(2,1)S(1)}, u32[]{:S(2)}, u32[]{:S(2)}) collective-permute-start(bf16[2,2,2,10,512]{4,1,2,3,0:T(2,128)(2,1)S(1)} %bitcast.44), channel_id=1, source_target_pairs={{0,2},{2,0},{1,3},{3,1},{4,6},{6,4},{5,7},{7,5},{8,10},{10,8},{9,1... | collective-permute-start | bytes 245768 | tf_op jit(solution)/shard_map/ppermute | solution.py:344
  56.9 5.7 %copy-start.1 = (f32[32,3]{1,0:T(8,128)S(1)}, f32[32,3]{1,0:T(8,128)}, u32[]{:S(2)}) copy-start(f32[32,3]{1,0:T(8,128)} %get-tuple-element.18.refs_4_.refs_2_) | copy-start | bytes 1156
  56.9 5.7 %copy-start.2 = (bf16[1,1,160,32]{2,3,1,0:T(8,128)(2,1)S(1)}, bf16[1,1,160,32]{2,3,1,0:T(8,128)(2,1)}, u32[]{:S(2)}) copy-start(bf16[1,1,160,32]{2,3,1,0:T(8,128)(2,1)} %param.11) | copy-start | bytes 30724
  56.9 23.5 %all-to-all-start.3 = ((bf16[8,2,2,2,2,10,512]{6,4,5,3,2,1,0:T(2,128)(2,1)}), bf16[8,2,2,2,2,10,512]{6,4,5,3,2,1,0:T(2,128)(2,1)S(1)}, u32[]{:S(2)}, u32[]{:S(2)}) async-start(bf16[8,2,2,2,2,10,512]{6,4,5,3,2,1,0:T(2,128)(2,1)} %broadcast_in_dim.27), calls=%async_computation.3 | async-start | bytes 2621440 | tf_op jit(solution)/shard_map/all_to_all | solution.py:347
  62.8 13.5 %collective-permute-start.2 = (f32[80,128]{1,0:T(8,128)S(1)}, f32[80,128]{1,0:T(8,128)S(1)}, u32[]{:S(2)}, u32[]{:S(2)}) collective-permute-start(f32[80,128]{1,0:T(8,128)S(1)} %shard_map.111.refs_0_), channel_id=1, source_target_pairs={{0,2},{2,0},{1,3},{3,1},{4,6},{6,4},{5,7},{7,5},{8,10},{10,8},{9,1... | collective-permute-start | bytes 122888 | tf_op jit(solution)/shard_map/ppermute | solution.py:340
  80.4 9.8 %all-to-all-start.2 = ((bf16[8,80,128]{2,1,0:T(8,128)(2,1)}), bf16[8,80,128]{2,1,0:T(8,128)(2,1)S(1)}, u32[]{:S(2)}, u32[]{:S(2)}) async-start(bf16[8,80,128]{2,1,0:T(8,128)(2,1)} %shard_map.112), calls=%async_computation.2 | async-start | bytes 327680 | tf_op jit(solution)/shard_map/all_to_all | solution.py:342
  85.9 1.2 copy-start
  87.1 29.6 %copy-start.3 = (f32[512]{0:T(512)S(1)}, f32[512]{0:T(512)}, u32[]{:S(2)}) copy-start(f32[512]{0:T(512)} %param.18) | copy-start | bytes 6148
  87.1 29.6 %copy-start.4 = (f32[512]{0:T(512)S(1)}, f32[512]{0:T(512)}, u32[]{:S(2)}) copy-start(f32[512]{0:T(512)} %param.19) | copy-start | bytes 6148
  87.1 29.6 %copy-start.5 = (f32[512]{0:T(512)S(1)}, f32[512]{0:T(512)}, u32[]{:S(2)}) copy-start(f32[512]{0:T(512)} %param.21) | copy-start | bytes 6148
  91.3 36.6 %collective-permute-start.4 = (bf16[10,80,128]{2,1,0:T(8,128)(2,1)S(1)}, bf16[10,80,128]{2,1,0:T(8,128)(2,1)S(1)}, u32[]{:S(2)}, u32[]{:S(2)}) collective-permute-start(bf16[10,80,128]{2,1,0:T(8,128)(2,1)S(1)} %get-tuple-element.22), channel_id=1, source_target_pairs={{0,16},{16,32},{32,48},{48,64},{64,80},{80,96},{96,112},{112,128},... | collective-permute-start | bytes 614408 | tf_op jit(solution)/shard_map/ppermute | solution.py:365
  93.4 34.5 %collective-permute-start.5 = (bf16[10,80,128]{2,1,0:T(8,128)(2,1)S(1)}, bf16[10,80,128]{2,1,0:T(8,128)(2,1)S(1)}, u32[]{:S(2)}, u32[]{:S(2)}) collective-permute-start(bf16[10,80,128]{2,1,0:T(8,128)(2,1)S(1)} %get-tuple-element.23), channel_id=1, source_target_pairs={{16,0},{32,16},{48,32},{64,48},{80,64},{96,80},{112,96},{128,112},... | collective-permute-start | bytes 614408 | tf_op jit(solution)/shard_map/ppermute | solution.py:366
  94.7 33.2 %all-to-all-start.4 = ((f32[32,1,128]{2,1,0:T(1,128)}), f32[32,1,128]{2,1,0:T(1,128)S(1)}, u32[]{:S(2)}, u32[]{:S(2)}) async-start(f32[32,1,128]{2,1,0:T(1,128)} %get-tuple-element.21), calls=%async_computation.4 | async-start | bytes 32768 | tf_op jit(solution)/shard_map/all_to_all | solution.py:367

commit v7 on v6

--- a/solution.py
+++ b/solution.py
@@ -17,44 +17,39 @@
 FIRST_GRANT = 56
 
 
-def run(fn, out_shapes, args, grant=8, late=()):
+def run(fn, out_shapes, args, grant=8):
     if not USE_KERNELS:
-        return fn(*[(lambda a=a: a) if i in late else a for i, a in enumerate(args)])
+        return fn(*args)
     n_a, single = len(args), isinstance(out_shapes, tuple)
     shapes = [out_shapes] if single else list(out_shapes)
-    n_o = len(shapes)
 
     def body(*refs):
-        held = refs[n_a + n_o :]
-        ins = [None if i in late else r[...] for i, r in enumerate(refs[:n_a])]
-        for spot, i in enumerate(late):
-            copy = pltpu.make_async_copy(refs[i], held[2 * spot], held[2 * spot + 1])
-            copy.start()
-
-            def ready(copy=copy, buffer=held[2 * spot]):
-                copy.wait()
-                return buffer[...]
-
-            ins[i] = ready
-        outs = fn(*ins)
+        outs = fn(*[r[...] for r in refs[:n_a]])
         outs = [outs] if single else outs
-        for ref, value in zip(refs[n_a : n_a + n_o], outs):
+        for ref, value in zip(refs[n_a:], outs):
             ref[...] = value
 
     vmem = pl.BlockSpec(memory_space=pltpu.VMEM)
-    far = pl.BlockSpec(memory_space=pltpu.HBM)
-    scratch = []
-    for i in late:
-        scratch += [pltpu.VMEM(args[i].shape, args[i].dtype), pltpu.SemaphoreType.DMA]
     res = pl.pallas_call(
         body,
         out_shape=[jax.ShapeDtypeStruct(s, d) for s, d in shapes],
-        in_specs=[far if i in late else vmem for i in range(n_a)],
-        out_specs=[vmem] * n_o,
-        scratch_shapes=scratch,
+        in_specs=[vmem] * n_a,
+        out_specs=[vmem] * len(shapes),
         compiler_params=pltpu.CompilerParams(vmem_limit_bytes=grant << 20),
     )(*args)
     return res[0] if single else res
+
+
+def preload(array):
+    if not USE_KERNELS:
+        return array
+    return pl.pallas_call(
+        lambda source, target: pltpu.sync_copy(source, target),
+        out_shape=jax.ShapeDtypeStruct(array.shape, array.dtype),
+        in_specs=[pl.BlockSpec(memory_space=pltpu.HBM)],
+        out_specs=pl.BlockSpec(memory_space=pltpu.VMEM),
+        compiler_params=pltpu.CompilerParams(vmem_limit_bytes=4 << 20),
+    )(array)
 
 
 def to_row(col):
@@ -154,7 +149,7 @@
                     x = jnp.where(has[0 if dy == 0 else 1], x, 0.0)
             pieces += [right(x).astype(BF16), x.astype(BF16), left(x).astype(BF16)]
     columns = jnp.concatenate(pieces, axis=0)
-    out = jnp.dot(columns.T, kernel(), preferred_element_type=F32).T
+    out = jnp.dot(columns.T, kernel, preferred_element_type=F32).T
     blocks = []
     for x in range(4):
         for k in range(2):
@@ -331,9 +326,7 @@
     partial = run(
         functools.partial(mid_conv, sizes=sizes),
         ((8, 80, 128), F32),
-        (stats, raw, above, below, affine, conv1_weight.reshape(27 * chans, 512)),
-        FIRST_GRANT,
-        late=(5,),
+        (stats, raw, above, below, affine, preload(conv1_weight.reshape(27 * chans, 512))),
     )
     partial = lax.all_to_all(partial, ("x", "k"), 0, 0, tiled=True)
     mine = run(fold, ((80, 128), F32), (partial, own, affine))

time: 155 us -> 152 us (0.981)
  Pallas kernels: 10.1 us -> 8.24 us
    pallas_call x9, Pallas kernels: 10.1 us -> 8.06 us  [run(): pl.pallas_call(body, out_shape=[jax.ShapeDtypeStruct(s, d) for s, d in sh...]
  transfers between devices with their start and end apart: 11 -> 11, of which waited for: 8 -> 7; matrix products, arithmetic and copies ran while one was open for 1% -> 1% of each run, Pallas kernels for 1% -> 1%
where the time goes in v7:
time: 152 us
  starting transfers between devices  80.7 us (53%)
  waiting for transfers between devices  31.9 us (21%)
  blocking collectives  23.5 us (15%)
  Pallas kernels  8.24 us (5%)
  local copies, waits for them, and re-layouts  6.72 us (4%)
    all_to_all x1, blocking collectives, on_device(): out = lax.all_to_all(out, ('x', 'h', 'k'), 0, 0, tiled=True)  23.5 us
    all_to_all x1, starting transfers between devices, on_device(): stats2 = lax.all_to_all(stats2, space, 0, 0, tiled=True)  21.9 us
    all_to_all x1, starting transfers between devices, on_device(): stats = lax.all_to_all(stats, space, 0, 0, tiled=True)  16.2 us
    all_to_all x1, waiting for transfers between devices, on_device(): stats2 = lax.all_to_all(stats2, space, 0, 0, tiled=True)  10.9 us
    ppermute x1, starting transfers between devices, on_device(): other = lax.ppermute(mine, 'h', [(0, 1), (1, 0)])  10.5 us
    pallas_call x9, Pallas kernels, run(): pl.pallas_call(body, out_shape=[jax.ShapeDtypeStruct(s, d) for s, d in sh...  8.06 us
    ppermute x1, starting transfers between devices, on_device(): swapped = lax.ppermute(tile, 'h', [(0, 1), (1, 0)])  7.93 us
    ppermute x1, waiting for transfers between devices, on_device(): swapped = lax.ppermute(tile, 'h', [(0, 1), (1, 0)])  6.69 us
  transfers between devices with their start and end apart: 11, of which 7 were waited for; matrix products, arithmetic and copies ran while one was open for 1% of the time, Pallas kernels for 1%

profile of v7, /device:TPU:1, one launch (start us, length us, event | category | flops | bytes accessed | tf_op | source)
XLA Modules:
  0.0 151.6 jit_solution(18143899624192948001)
XLA Ops:
  0.0 1.6 %shard_map.109 = (f32[32,1,128]{2,1,0:T(1,128)}, bf16[3,32,160]{2,1,0:T(8,128)(2,1)}, f32[32,3]{1,0:T(8,128)}) custom-call(bf16[32,160]{1,0:T(8,128)(2,1)} %bitcast.36, bf16[2,32,160]{2,1,0:T(8,128)(2,1)} %bitcast.47, f32[1,32]{1,0:T(1,128)} %bitcast.48, f32[1,32]{1,0:T(1,128)} %bitcast.49, f32[1,32]{1,0:T(1,128)} %bitcast.50), custom_call_target="tpu_custom_call" | custom-call | tf_op jit(solution)/shard_map/pallas_call | solution.py:33
  1.6 0.0 copy-start.2
  1.6 16.2 %all-to-all-start = ((f32[32,1,128]{2,1,0:T(1,128)}), f32[32,1,128]{2,1,0:T(1,128)S(1)}, u32[]{:S(2)}, u32[]{:S(2)}) async-start(f32[32,1,128]{2,1,0:T(1,128)} %get-tuple-element.16), calls=%async_computation | async-start | bytes 32768 | tf_op jit(solution)/shard_map/all_to_all | solution.py:321
  17.9 3.1 %collective-permute-start = (bf16[3,32,160]{2,1,0:T(8,128)(2,1)}, bf16[3,32,160]{2,1,0:T(8,128)(2,1)S(1)}, u32[]{:S(2)}, u32[]{:S(2)}) collective-permute-start(bf16[3,32,160]{2,1,0:T(8,128)(2,1)} %get-tuple-element.17.refs_1_), channel_id=1, source_target_pairs={{0,16},{16,32},{32,48},{48,64},{64,80},{80,96},{96,112},{112,128},... | collective-permute-start | bytes 92168 | tf_op jit(solution)/shard_map/ppermute | solution.py:324
  21.0 1.3 collective-permute-start.1
  22.3 0.0 copy-start.1
  22.3 1.2 copy-done.1
  23.5 0.0 copy-start.4
  23.5 0.2 shard_map.110.refs_5_
  23.7 0.0 copy-start.8
  23.7 0.0 collective-permute-done.refs_2_
  23.7 2.7 %collective-permute-done.1.refs_3_ = bf16[3,32,160]{2,1,0:T(8,128)(2,1)S(1)} collective-permute-done((bf16[3,32,160]{2,1,0:T(8,128)(2,1)}, bf16[3,32,160]{2,1,0:T(8,128)(2,1)S(1)}, u32[]{:S(2)}, u32[]{:S(2)}) %collective-permute-start.1) | collective-permute-done | bytes 30752 | tf_op jit(solution)/shard_map/ppermute | solution.py:325
  26.4 2.8 %all-to-all-done.refs_0_ = f32[32,1,128]{2,1,0:T(1,128)S(1)} async-done(((f32[32,1,128]{2,1,0:T(1,128)}), f32[32,1,128]{2,1,0:T(1,128)S(1)}, u32[]{:S(2)}, u32[]{:S(2)}) %all-to-all-start) | async-done | bytes 16416 | tf_op jit(solution)/shard_map/all_to_all | solution.py:321
  29.1 0.0 copy-done.2
  29.1 0.0 copy-done.4
  29.2 1.7 %shard_map.111 = f32[8,80,128]{2,1,0:T(8,128)} custom-call(f32[32,1,128]{2,1,0:T(1,128)S(1)} %all-to-all-done.refs_0_, bf16[3,32,160]{2,1,0:T(8,128)(2,1)S(1)} %copy-done.4, bf16[3,32,160]{2,1,0:T(8,128)(2,1)S(1)} %collective-permute-done.refs_2_, bf16[3,32,160]{2,1,0:T(8,128)(2,1)S(1)} %collective-permute-done.1.refs_3_, f32[32,3]{1,0:T(8,128)S(1)} %copy-done.2, ...), custom_call_target="tpu_custom_call" | custom-call | tf_op jit(solution)/shard_map/pallas_call | solution.py:33
  30.9 6.4 %all-to-all-start.1 = ((f32[8,80,128]{2,1,0:T(8,128)}), f32[8,80,128]{2,1,0:T(8,128)S(1)}, u32[]{:S(2)}, u32[]{:S(2)}) async-start(f32[8,80,128]{2,1,0:T(8,128)} %shard_map.111), calls=%async_computation.1 | async-start | bytes 655360 | tf_op jit(solution)/shard_map/all_to_all | solution.py:331
  37.3 0.0 copy-done.8
  37.3 7.9 %collective-permute-start.3 = (bf16[2,2,2,10,512]{4,1,2,3,0:T(2,128)(2,1)S(1)}, bf16[2,2,2,10,512]{4,1,2,3,0:T(2,128)(2,1)S(1)}, u32[]{:S(2)}, u32[]{:S(2)}) collective-permute-start(bf16[2,2,2,10,512]{4,1,2,3,0:T(2,128)(2,1)S(1)} %bitcast.44), channel_id=1, source_target_pairs={{0,2},{2,0},{1,3},{3,1},{4,6},{6,4},{5,7},{7,5},{8,10},{10,8},{9,1... | collective-permute-start | bytes 245768 | tf_op jit(solution)/shard_map/ppermute | solution.py:337
  45.2 6.7 %collective-permute-done.3 = bf16[2,2,2,10,512]{4,1,2,3,0:T(2,128)(2,1)S(1)} collective-permute-done((bf16[2,2,2,10,512]{4,1,2,3,0:T(2,128)(2,1)S(1)}, bf16[2,2,2,10,512]{4,1,2,3,0:T(2,128)(2,1)S(1)}, u32[]{:S(2)}, u32[]{:S(2)}) %collective-permute-start.3) | collective-permute-done | bytes 81952 | tf_op jit(solution)/shard_map/ppermute | solution.py:337
  51.9 0.2 broadcast_select_fusion
  52.1 0.1 copy.18
  52.3 0.0 all-to-all-done.1.refs_0_
  52.3 2.1 %broadcast_in_dim.27 = bf16[8,2,2,2,2,10,512]{6,4,5,3,2,1,0:T(2,128)(2,1)} broadcast(bf16[2,2,2,2,10,512]{5,3,4,2,1,0:T(2,128)(2,1)S(1)} %copy.18), dimensions={1,2,3,4,5,6} | broadcast | bytes 1474560 | tf_op jit(solution)/shard_map/broadcast_in_dim | solution.py:339
  54.4 0.0 copy-start.3
  54.4 5.7 %all-to-all-start.3 = ((bf16[8,2,2,2,2,10,512]{6,4,5,3,2,1,0:T(2,128)(2,1)}), bf16[8,2,2,2,2,10,512]{6,4,5,3,2,1,0:T(2,128)(2,1)S(1)}, u32[]{:S(2)}, u32[]{:S(2)}) async-start(bf16[8,2,2,2,2,10,512]{6,4,5,3,2,1,0:T(2,128)(2,1)} %broadcast_in_dim.27), calls=%async_computation.3 | async-start | bytes 2621440 | tf_op jit(solution)/shard_map/all_to_all | solution.py:340
  60.1 0.0 copy-done.3
  60.1 0.2 shard_map.112.refs_0_
  60.2 10.5 %collective-permute-start.2 = (f32[80,128]{1,0:T(8,128)S(1)}, f32[80,128]{1,0:T(8,128)S(1)}, u32[]{:S(2)}, u32[]{:S(2)}) collective-permute-start(f32[80,128]{1,0:T(8,128)S(1)} %shard_map.112.refs_0_), channel_id=1, source_target_pairs={{0,2},{2,0},{1,3},{3,1},{4,6},{6,4},{5,7},{7,5},{8,10},{10,8},{9,1... | collective-permute-start | bytes 122888 | tf_op jit(solution)/shard_map/ppermute | solution.py:333
  70.7 3.0 %collective-permute-done.2.refs_1_ = f32[80,128]{1,0:T(8,128)S(1)} collective-permute-done((f32[80,128]{1,0:T(8,128)S(1)}, f32[80,128]{1,0:T(8,128)S(1)}, u32[]{:S(2)}, u32[]{:S(2)}) %collective-permute-start.2) | collective-permute-done | bytes 40992 | tf_op jit(solution)/shard_map/ppermute | solution.py:333
  73.7 0.7 shard_map.113
  74.4 3.5 %all-to-all-done.3 = bf16[8,2,2,2,2,10,512]{6,4,5,3,2,1,0:T(2,128)(2,1)S(1)} async-done(((bf16[8,2,2,2,2,10,512]{6,4,5,3,2,1,0:T(2,128)(2,1)}), bf16[8,2,2,2,2,10,512]{6,4,5,3,2,1,0:T(2,128)(2,1)S(1)}, u32[]{:S(2)}, u32[]{:S(2)}) %all-to-all-start.3) | async-done | bytes 1310752 | tf_op jit(solution)/shard_map/all_to_all | solution.py:340
  77.9 4.3 %all-to-all-start.2 = ((bf16[8,80,128]{2,1,0:T(8,128)(2,1)}), bf16[8,80,128]{2,1,0:T(8,128)(2,1)S(1)}, u32[]{:S(2)}, u32[]{:S(2)}) async-start(bf16[8,80,128]{2,1,0:T(8,128)(2,1)} %shard_map.113), calls=%async_computation.2 | async-start | bytes 327680 | tf_op jit(solution)/shard_map/all_to_all | solution.py:335
  82.1 1.2 copy.19
  83.3 0.0 copy-start
  83.3 0.2 copy.20.refs_0_
  83.6 0.9 copy-done
  84.5 0.0 copy-start.5
  84.5 0.0 copy-start.6
  84.5 0.0 copy-start.7
  84.5 0.9 shard_map.114
  85.4 2.3 %all-to-all-done.2.refs_0_.refs_1_ = bf16[8,80,128]{2,1,0:T(8,128)(2,1)S(1)} async-done(((bf16[8,80,128]{2,1,0:T(8,128)(2,1)}), bf16[8,80,128]{2,1,0:T(8,128)(2,1)S(1)}, u32[]{:S(2)}, u32[]{:S(2)}) %all-to-all-start.2) | async-done | bytes 163872 | tf_op jit(solution)/shard_map/all_to_all | solution.py:335
  87.7 1.1 shard_map.115
  88.8 2.1 %collective-permute-start.4 = (bf16[10,80,128]{2,1,0:T(8,128)(2,1)S(1)}, bf16[10,80,128]{2,1,0:T(8,128)(2,1)S(1)}, u32[]{:S(2)}, u32[]{:S(2)}) collective-permute-start(bf16[10,80,128]{2,1,0:T(8,128)(2,1)S(1)} %get-tuple-element.22), channel_id=1, source_target_pairs={{0,16},{16,32},{32,48},{48,64},{64,80},{80,96},{96,112},{112,128},... | collective-permute-start | bytes 614408 | tf_op jit(solution)/shard_map/ppermute | solution.py:358
  90.9 1.3 collective-permute-start.5
  92.2 21.9 %all-to-all-start.4 = ((f32[32,1,128]{2,1,0:T(1,128)}), f32[32,1,128]{2,1,0:T(1,128)S(1)}, u32[]{:S(2)}, u32[]{:S(2)}) async-start(f32[32,1,128]{2,1,0:T(1,128)} %get-tuple-element.21), calls=%async_computation.4 | async-start | bytes 32768 | tf_op jit(solution)/shard_map/all_to_all | solution.py:360
  114.1 0.0 copy-done.5
  114.1 0.0 copy-done.6
  114.1 0.0 copy-done.7
  114.1 0.3 shard_map.116
  114.4 10.9 %all-to-all-done.4.refs_0_ = f32[32,1,128]{2,1,0:T(1,128)S(1)} async-done(((f32[32,1,128]{2,1,0:T(1,128)}), f32[32,1,128]{2,1,0:T(1,128)S(1)}, u32[]{:S(2)}, u32[]{:S(2)}) %all-to-all-start.4) | async-done | bytes 16416 | tf_op jit(solution)/shard_map/all_to_all | solution.py:360
  125.4 0.0 collective-permute-done.4.refs_2_
  125.4 0.0 collective-permute-done.5.refs_3_
  125.4 1.7 %shard_map.118 = bf16[16,10,128]{2,1,0:T(8,128)(2,1)S(1)} custom-call(f32[32,1,128]{2,1,0:T(1,128)S(1)} %all-to-all-done.4.refs_0_, bf16[8,80,128]{2,1,0:T(8,128)(2,1)S(1)} %all-to-all-done.2.refs_0_.refs_1_, bf16[10,80,128]{2,1,0:T(8,128)(2,1)S(1)} %collective-permute-done.4.refs_2_, bf16[10,80,128]{2,1,0:T(8,128)(2,1)S(1)} %collective-permute-done.5.refs_3_, ...), custom_call_target="tpu_custom_call" | custom-call | tf_op jit(solution)/shard_map/pallas_call | solution.py:33
  127.1 23.5 %all_to_all.30 = bf16[16,10,128]{2,1,0:T(8,128)(2,1)S(1)} all-to-all(bf16[16,10,128]{2,1,0:T(8,128)(2,1)S(1)} %shard_map.118), channel_id=1, replica_groups=mesh['y'=4,'l'=8,'x'=4,'h'=2,'k'=2] {'x','h','k'}, dimensions={0} | all-to-all | bytes 81920 | tf_op jit(solution)/shard_map/all_to_all | solution.py:382
  150.6 0.1 reshape.59
  150.8 0.8 reshape.60
  (3 shorter events, 0.1 us)
Async XLA Ops:
  1.6 27.5 %copy-start.2 = (f32[32,3]{1,0:T(8,128)S(1)}, f32[32,3]{1,0:T(8,128)}, u32[]{:S(2)}) copy-start(f32[32,3]{1,0:T(8,128)} %get-tuple-element.18.refs_4_.refs_2_) | copy-start | bytes 1156
  1.6 27.5 %all-to-all-start = ((f32[32,1,128]{2,1,0:T(1,128)}), f32[32,1,128]{2,1,0:T(1,128)S(1)}, u32[]{:S(2)}, u32[]{:S(2)}) async-start(f32[32,1,128]{2,1,0:T(1,128)} %get-tuple-element.16), calls=%async_computation | async-start | bytes 32768 | tf_op jit(solution)/shard_map/all_to_all | solution.py:321
  17.9 5.8 %collective-permute-start = (bf16[3,32,160]{2,1,0:T(8,128)(2,1)}, bf16[3,32,160]{2,1,0:T(8,128)(2,1)S(1)}, u32[]{:S(2)}, u32[]{:S(2)}) collective-permute-start(bf16[3,32,160]{2,1,0:T(8,128)(2,1)} %get-tuple-element.17.refs_1_), channel_id=1, source_target_pairs={{0,16},{16,32},{32,48},{48,64},{64,80},{80,96},{96,112},{112,128},... | collective-permute-start | bytes 92168 | tf_op jit(solution)/shard_map/ppermute | solution.py:324
  21.0 5.4 %collective-permute-start.1 = (bf16[3,32,160]{2,1,0:T(8,128)(2,1)}, bf16[3,32,160]{2,1,0:T(8,128)(2,1)S(1)}, u32[]{:S(2)}, u32[]{:S(2)}) collective-permute-start(bf16[3,32,160]{2,1,0:T(8,128)(2,1)} %get-tuple-element.17.refs_1_), channel_id=1, source_target_pairs={{16,0},{32,16},{48,32},{64,48},{80,64},{96,80},{112,96},{128,112},... | collective-permute-start | bytes 92168 | tf_op jit(solution)/shard_map/ppermute | solution.py:325
  22.3 1.2 copy-start.1
  23.5 5.7 %copy-start.4 = (bf16[3,32,160]{2,1,0:T(8,128)(2,1)S(1)}, bf16[3,32,160]{2,1,0:T(8,128)(2,1)}, u32[]{:S(2)}) copy-start(bf16[3,32,160]{2,1,0:T(8,128)(2,1)} %get-tuple-element.17.refs_1_) | copy-start | bytes 92164
  23.7 13.6 %copy-start.8 = (bf16[2,2,20,512]{3,1,2,0:T(2,128)(2,1)S(1)}, bf16[2,2,20,512]{3,1,2,0:T(2,128)(2,1)}, u32[]{:S(2)}) copy-start(bf16[2,2,20,512]{3,1,2,0:T(2,128)(2,1)} %param.17) | copy-start | bytes 245764
  30.9 21.4 %all-to-all-start.1 = ((f32[8,80,128]{2,1,0:T(8,128)}), f32[8,80,128]{2,1,0:T(8,128)S(1)}, u32[]{:S(2)}, u32[]{:S(2)}) async-start(f32[8,80,128]{2,1,0:T(8,128)} %shard_map.111), calls=%async_computation.1 | async-start | bytes 655360 | tf_op jit(solution)/shard_map/all_to_all | solution.py:331
  37.3 14.6 %collective-permute-start.3 = (bf16[2,2,2,10,512]{4,1,2,3,0:T(2,128)(2,1)S(1)}, bf16[2,2,2,10,512]{4,1,2,3,0:T(2,128)(2,1)S(1)}, u32[]{:S(2)}, u32[]{:S(2)}) collective-permute-start(bf16[2,2,2,10,512]{4,1,2,3,0:T(2,128)(2,1)S(1)} %bitcast.44), channel_id=1, source_target_pairs={{0,2},{2,0},{1,3},{3,1},{4,6},{6,4},{5,7},{7,5},{8,10},{10,8},{9,1... | collective-permute-start | bytes 245768 | tf_op jit(solution)/shard_map/ppermute | solution.py:337
  54.4 5.7 %copy-start.3 = (bf16[1,1,160,32]{2,3,1,0:T(8,128)(2,1)S(1)}, bf16[1,1,160,32]{2,3,1,0:T(8,128)(2,1)}, u32[]{:S(2)}) copy-start(bf16[1,1,160,32]{2,3,1,0:T(8,128)(2,1)} %param.11) | copy-start | bytes 30724
  54.4 23.5 %all-to-all-start.3 = ((bf16[8,2,2,2,2,10,512]{6,4,5,3,2,1,0:T(2,128)(2,1)}), bf16[8,2,2,2,2,10,512]{6,4,5,3,2,1,0:T(2,128)(2,1)S(1)}, u32[]{:S(2)}, u32[]{:S(2)}) async-start(bf16[8,2,2,2,2,10,512]{6,4,5,3,2,1,0:T(2,128)(2,1)} %broadcast_in_dim.27), calls=%async_computation.3 | async-start | bytes 2621440 | tf_op jit(solution)/shard_map/all_to_all | solution.py:340
  60.2 13.5 %collective-permute-start.2 = (f32[80,128]{1,0:T(8,128)S(1)}, f32[80,128]{1,0:T(8,128)S(1)}, u32[]{:S(2)}, u32[]{:S(2)}) collective-permute-start(f32[80,128]{1,0:T(8,128)S(1)} %shard_map.112.refs_0_), channel_id=1, source_target_pairs={{0,2},{2,0},{1,3},{3,1},{4,6},{6,4},{5,7},{7,5},{8,10},{10,8},{9,1... | collective-permute-start | bytes 122888 | tf_op jit(solution)/shard_map/ppermute | solution.py:333
  77.9 9.8 %all-to-all-start.2 = ((bf16[8,80,128]{2,1,0:T(8,128)(2,1)}), bf16[8,80,128]{2,1,0:T(8,128)(2,1)S(1)}, u32[]{:S(2)}, u32[]{:S(2)}) async-start(bf16[8,80,128]{2,1,0:T(8,128)(2,1)} %shard_map.113), calls=%async_computation.2 | async-start | bytes 327680 | tf_op jit(solution)/shard_map/all_to_all | solution.py:335
  83.3 1.2 copy-start
  84.5 29.6 %copy-start.5 = (f32[512]{0:T(512)S(1)}, f32[512]{0:T(512)}, u32[]{:S(2)}) copy-start(f32[512]{0:T(512)} %param.18) | copy-start | bytes 6148
  84.5 29.6 %copy-start.6 = (f32[512]{0:T(512)S(1)}, f32[512]{0:T(512)}, u32[]{:S(2)}) copy-start(f32[512]{0:T(512)} %param.19) | copy-start | bytes 6148
  84.5 29.6 %copy-start.7 = (f32[512]{0:T(512)S(1)}, f32[512]{0:T(512)}, u32[]{:S(2)}) copy-start(f32[512]{0:T(512)} %param.21) | copy-start | bytes 6148
  88.8 36.6 %collective-permute-start.4 = (bf16[10,80,128]{2,1,0:T(8,128)(2,1)S(1)}, bf16[10,80,128]{2,1,0:T(8,128)(2,1)S(1)}, u32[]{:S(2)}, u32[]{:S(2)}) collective-permute-start(bf16[10,80,128]{2,1,0:T(8,128)(2,1)S(1)} %get-tuple-element.22), channel_id=1, source_target_pairs={{0,16},{16,32},{32,48},{48,64},{64,80},{80,96},{96,112},{112,128},... | collective-permute-start | bytes 614408 | tf_op jit(solution)/shard_map/ppermute | solution.py:358
  90.9 34.5 %collective-permute-start.5 = (bf16[10,80,128]{2,1,0:T(8,128)(2,1)S(1)}, bf16[10,80,128]{2,1,0:T(8,128)(2,1)S(1)}, u32[]{:S(2)}, u32[]{:S(2)}) collective-permute-start(bf16[10,80,128]{2,1,0:T(8,128)(2,1)S(1)} %get-tuple-element.23), channel_id=1, source_target_pairs={{16,0},{32,16},{48,32},{64,48},{80,64},{96,80},{112,96},{128,112},... | collective-permute-start | bytes 614408 | tf_op jit(solution)/shard_map/ppermute | solution.py:359
  92.2 33.2 %all-to-all-start.4 = ((f32[32,1,128]{2,1,0:T(1,128)}), f32[32,1,128]{2,1,0:T(1,128)S(1)}, u32[]{:S(2)}, u32[]{:S(2)}) async-start(f32[32,1,128]{2,1,0:T(1,128)} %get-tuple-element.21), calls=%async_computation.4 | async-start | bytes 32768 | tf_op jit(solution)/shard_map/all_to_all | solution.py:360

commit v8 on v7

--- a/solution.py
+++ b/solution.py
@@ -187,63 +187,46 @@
     )
 
 
-def row_stats(gathered, to_above, to_below, peers):
-    return (
-        partial_stats(rows_of(gathered), peers),
-        jnp.concatenate([gathered, to_above], axis=0),
-        jnp.concatenate([gathered, to_below], axis=0),
-    )
-
-
-def halves(a):
-    a = pack(a)
-    high = a.astype(BF16)
-    return jnp.stack([high, (a - high.astype(F32)).astype(BF16)])
-
-
-def whole(blocks):
-    return unpack(blocks[0].astype(F32) + blocks[1].astype(F32))
-
-
-def taps(prod):
-    return [[prod[(dy * 3 + dx) * 32 : (dy * 3 + dx + 1) * 32] for dx in range(3)] for dy in range(3)]
-
-
-def cache_conv(images, kernel):
-    per = 9 * 32
-    sums = {}
-
-    def add(key, value):
-        sums[key] = sums[key] + value if key in sums else value
-
-    for t in range(2):
-        w = kernel[t * per : (t + 1) * per]
-        for r in range(2):
-            even, odd = (
-                taps(
-                    lax.dot_general(
-                        w, images[t, r, p], (((1,), (1,)), ((), ())), preferred_element_type=F32
-                    )
-                )
-                for p in range(2)
-            )
-            for dy in range(3):
-                o = r + 1 - dy
-                add((o, "m", 0), even[dy][1] + odd[dy][2])
-                add((o, "r", 0), odd[dy][0])
-                add((o, "m", 1), even[dy][0] + odd[dy][1])
-                add((o, "l", 1), even[dy][2])
-
-    def out(o):
-        return jnp.concatenate(
-            [
-                sums[(o, "m", 0)] + right(sums[(o, "r", 0)]),
-                sums[(o, "m", 1)] + left(sums[(o, "l", 1)]),
-            ],
-            axis=0,
-        )
-
-    return jnp.concatenate([out(0), out(1)], axis=0), halves(out(-1)), halves(out(2))
+def row_stats(gathered, peers):
+    return partial_stats(rows_of(gathered), peers)
+
+
+def product(w, image):
+    return lax.dot_general(w, image, (((1,), (1,)), ((), ())), preferred_element_type=F32)
+
+
+def phases(even, odd):
+    first = even[32:64] + odd[64:] + right(odd[:32])
+    second = even[:32] + odd[32:64] + left(even[64:])
+    return jnp.concatenate([first, second], axis=0)
+
+
+def cache_conv(first, second, kernel):
+    outs = []
+    for o in range(2):
+        sums = []
+        for p in range(2):
+            total = None
+            for t in range(2):
+                for r in range(2):
+                    row = (t * 3 + r - o + 1) * 96
+                    value = product(kernel[row : row + 96], (first, second)[r][t, p])
+                    total = value if total is None else total + value
+            sums.append(total)
+        outs.append(phases(*sums))
+    return jnp.concatenate(outs, axis=0)
+
+
+def edge_conv(above, below, kernel):
+    outs = []
+    for image, dy in ((above, 0), (below, 2)):
+        sums = [
+            product(kernel[dy * 96 : dy * 96 + 96], image[0, p])
+            + product(kernel[(3 + dy) * 96 : (4 + dy) * 96], image[1, p])
+            for p in range(2)
+        ]
+        outs.append(phases(*sums))
+    return jnp.concatenate(outs, axis=0)
 
 
 def up_columns(gain, bias, out_bias):
@@ -262,9 +245,8 @@
     )
 
 
-def up_conv(parts, row, above, below, affine, lhs, held, out_bias, sizes):
-    from_above, from_below = whole(above[8:]), whole(below[8:])
-    row, above, below = rows_of(row), rows_of(above[:8]), rows_of(below[:8])
+def up_conv(parts, row, above, below, affine, lhs, held, out_bias, old_above, old_below, kernel, sizes):
+    row, above, below = rows_of(row), rows_of(above), rows_of(below)
     chans, cols = row.shape
     groups = chans // GS
     mean, scale = merge_stats(parts, groups, GS * cols)
@@ -285,7 +267,7 @@
         cut = [prod[dx * 32 : (dx + 1) * 32] for dx in range(3)]
         outs += [right(cut[0]) + cut[1] + cut[2], cut[0] + cut[1] + left(cut[2])]
     total = jnp.concatenate(outs, axis=0) + held
-    total = total + jnp.concatenate([from_above, from_below], axis=0)
+    total = total + edge_conv(old_above, old_below, kernel)
     total = (total + out_bias).T
     part = cols // 16
     return jnp.stack([total[c * part : (c + 1) * part] for c in range(16)]).astype(BF16)
@@ -338,25 +320,31 @@
     pair = jnp.where(hi == 0, jnp.stack([tile, swapped]), jnp.stack([swapped, tile]))
     copies = jnp.broadcast_to(pair[None], (8,) + pair.shape)
     spread = lax.all_to_all(copies, ("x", "k"), 0, 0, tiled=True)
-    images = (
-        spread.reshape(4, 2, 2, 2, 2, 2, 10, 512)
-        .transpose(3, 4, 5, 0, 2, 1, 6, 7)
-        .reshape(2, 2, 2, cols, 512)
-    )
+    spread = spread.reshape(4, 2, 2, 2, 2, 2, 10, 512)
+    rows = [
+        spread[:, :, :, :, r].transpose(3, 4, 0, 2, 1, 5, 6).reshape(2, 2, cols, 512)
+        for r in range(2)
+    ]
     kernel2 = conv2_weight.transpose(0, 1, 2, 4, 3).reshape(27 * 32, 512)
-    held, to_above, to_below = run(
-        cache_conv,
-        [((128, cols), F32), ((2, 80, 128), BF16), ((2, 80, 128), BF16)],
-        (images, kernel2),
-        16,
-    )
-    stats2, going_up, going_down = run(
-        functools.partial(row_stats, peers=peers),
-        [((peers, 1, 128), F32), ((10, 80, 128), BF16), ((10, 80, 128), BF16)],
-        (gathered, to_above, to_below),
-    )
-    row_above = lax.ppermute(going_down, space, down)
-    row_below = lax.ppermute(going_up, space, up)
+    held = run(cache_conv, ((128, cols), F32), (*rows, kernel2), 16)
+    stats2 = run(functools.partial(row_stats, peers=peers), ((peers, 1, 128), F32), (gathered,))
+
+    def at(y, l, h):
+        return (y * n_l + l) * 2 + h
+
+    down_h = []
+    for y in range(n_y):
+        for l in range(n_l):
+            for h in range(2):
+                if l < n_l - 1:
+                    down_h.append((at(y, l, h), at(y, l + 1, h)))
+                elif y < n_y - 1:
+                    down_h.append((at(y, l, h), at(y + 1, 0, 1 - h)))
+    up_h = [pair[::-1] for pair in down_h]
+    old_above = lax.ppermute(rows[1], ("y", "l", "h"), down_h)
+    old_below = lax.ppermute(rows[0], ("y", "l", "h"), up_h)
+    row_above = lax.ppermute(gathered, ("y", "l", "h"), down_h)
+    row_below = lax.ppermute(gathered, ("y", "l", "h"), up_h)
     stats2 = lax.all_to_all(stats2, space, 0, 0, tiled=True)
     affine2, bias_here = run(
         up_columns,
@@ -376,6 +364,9 @@
             lhs,
             held,
             bias_here,
+            old_above,
+            old_below,
+            kernel2,
         ),
         16,
     )

time: 152 us -> 169 us (1.11)
  blocking collectives: 23.5 us -> 47.9 us
  starting transfers between devices: 80.7 us -> 72.8 us
    all_to_all x0 -> x2, blocking collectives: none -> 22.1 us  [the longest x1 12.2 us: on_device(): partial = lax.all_to_all(partial, ('x', 'k'), 0, 0, tiled=True)]
    all_to_all x2 -> x0, starting transfers between devices: 10.6 us -> none  [the longest x1 6.4 us: on_device(): partial = lax.all_to_all(partial, ('x', 'k'), 0, 0, tiled=True)]
    all_to_all x1, starting transfers between devices: 21.9 us -> 12.2 us  [on_device(): stats2 = lax.all_to_all(stats2, space, 0, 0, tiled=True)]
    ppermute x1, starting transfers between devices: 7.93 us -> 16.2 us  [on_device(): swapped = lax.ppermute(tile, 'h', [(0, 1), (1, 0)])]
    all_to_all x1, waiting for transfers between devices: 3.49 us -> 11.6 us  [on_device(): spread = lax.all_to_all(copies, ('x', 'k'), 0, 0, tiled=True)]
    ppermute x2 -> x4, starting transfers between devices: 3.41 us -> 9.76 us  [the longest x1 4.01 us: on_device(): old_above = lax.ppermute(rows[1], ('y', 'l', 'h'), down_h)]
    ppermute x1, waiting for transfers between devices: 6.69 us -> 2.32 us  [on_device(): swapped = lax.ppermute(tile, 'h', [(0, 1), (1, 0)])]
    ppermute x1, waiting for transfers between devices: 2.68 us -> 0.01 us  [on_device(): below = lax.ppermute(raw, space, up)]
  transfers between devices with their start and end apart: 11 -> 11, of which waited for: 7 -> 5; matrix products, arithmetic and copies ran while one was open for 1% -> 1% of each run, Pallas kernels for 1% -> 3%
where the time goes in v8:
time: 169 us; the launch traced here: 168 us
  starting transfers between devices  72.8 us (43%)
  blocking collectives  47.9 us (28%)
  waiting for transfers between devices  31.5 us (19%)
  Pallas kernels  8.86 us (5%)
  local copies, waits for them, and re-layouts  5.13 us (3%)
    all_to_all x1, blocking collectives, on_device(): out = lax.all_to_all(out, ('x', 'h', 'k'), 0, 0, tiled=True)  25.8 us
    ppermute x1, starting transfers between devices, on_device(): swapped = lax.ppermute(tile, 'h', [(0, 1), (1, 0)])  16.2 us
    all_to_all x1, starting transfers between devices, on_device(): stats = lax.all_to_all(stats, space, 0, 0, tiled=True)  13.6 us
    all_to_all x1, blocking collectives, on_device(): partial = lax.all_to_all(partial, ('x', 'k'), 0, 0, tiled=True)  12.2 us
    all_to_all x1, starting transfers between devices, on_device(): stats2 = lax.all_to_all(stats2, space, 0, 0, tiled=True)  12.2 us
    all_to_all x1, waiting for transfers between devices, on_device(): spread = lax.all_to_all(copies, ('x', 'k'), 0, 0, tiled=True)  11.6 us
    all_to_all x1, waiting for transfers between devices, on_device(): stats2 = lax.all_to_all(stats2, space, 0, 0, tiled=True)  9.91 us
    all_to_all x1, blocking collectives, on_device(): gathered = lax.all_to_all(gathered, ('x', 'k'), 0, 0, tiled=True)  9.83 us
  transfers between devices with their start and end apart: 11, of which 5 were waited for; matrix products, arithmetic and copies ran while one was open for 1% of the time, Pallas kernels for 3%

profile of v8, /device:TPU:1, one launch (start us, length us, event | category | flops | bytes accessed | tf_op | source)
XLA Modules:
  0.0 167.9 jit_solution(16993941306136840963)
XLA Ops:
  0.0 16.2 %collective-permute-start.5 = (bf16[2,2,2,10,512]{4,1,2,3,0:T(2,128)(2,1)}, bf16[2,2,2,10,512]{4,1,2,3,0:T(2,128)(2,1)S(1)}, u32[]{:S(2)}, u32[]{:S(2)}) collective-permute-start(bf16[2,2,2,10,512]{4,1,2,3,0:T(2,128)(2,1)} %bitcast.53), channel_id=1, source_target_pairs={{0,2},{2,0},{1,3},{3,1},{4,6},{6,4},{5,7},{7,5},{8,10},{10,8},{9,1... | collective-permute-start | bytes 245768 | tf_op jit(solution)/shard_map/ppermute | solution.py:319
  16.3 2.3 %collective-permute-done.5 = bf16[2,2,2,10,512]{4,1,2,3,0:T(2,128)(2,1)S(1)} collective-permute-done((bf16[2,2,2,10,512]{4,1,2,3,0:T(2,128)(2,1)}, bf16[2,2,2,10,512]{4,1,2,3,0:T(2,128)(2,1)S(1)}, u32[]{:S(2)}, u32[]{:S(2)}) %collective-permute-start.5) | collective-permute-done | bytes 81952 | tf_op jit(solution)/shard_map/ppermute | solution.py:319
  18.6 1.3 broadcast_select_fusion
  19.9 0.1 copy.22
  20.0 2.1 %broadcast_in_dim.30 = bf16[8,2,2,2,2,10,512]{6,4,5,3,2,1,0:T(2,128)(2,1)} broadcast(bf16[2,2,2,2,10,512]{5,3,4,2,1,0:T(2,128)(2,1)S(1)} %copy.22), dimensions={1,2,3,4,5,6} | broadcast | bytes 1474560 | tf_op jit(solution)/shard_map/broadcast_in_dim | solution.py:321
  22.1 7.0 %all-to-all-start.4 = ((bf16[8,2,2,2,2,10,512]{6,4,5,3,2,1,0:T(2,128)(2,1)}), bf16[8,2,2,2,2,10,512]{6,4,5,3,2,1,0:T(2,128)(2,1)S(1)}, u32[]{:S(2)}, u32[]{:S(2)}) async-start(bf16[8,2,2,2,2,10,512]{6,4,5,3,2,1,0:T(2,128)(2,1)} %broadcast_in_dim.30), calls=%async_computation.4 | async-start | bytes 2621440 | tf_op jit(solution)/shard_map/all_to_all | solution.py:322
  29.0 1.6 shard_map.109
  30.7 3.2 %collective-permute-start = (bf16[3,32,160]{2,1,0:T(8,128)(2,1)}, bf16[3,32,160]{2,1,0:T(8,128)(2,1)S(1)}, u32[]{:S(2)}, u32[]{:S(2)}) collective-permute-start(bf16[3,32,160]{2,1,0:T(8,128)(2,1)} %get-tuple-element.11.refs_1_), channel_id=1, source_target_pairs={{0,16},{16,32},{32,48},{48,64},{64,80},{80,96},{96,112},{112,128},... | collective-permute-start | bytes 92168 | tf_op jit(solution)/shard_map/ppermute | solution.py:306
  33.9 1.3 collective-permute-start.1
  35.2 11.6 %all-to-all-done.4 = bf16[8,2,2,2,2,10,512]{6,4,5,3,2,1,0:T(2,128)(2,1)S(1)} async-done(((bf16[8,2,2,2,2,10,512]{6,4,5,3,2,1,0:T(2,128)(2,1)}), bf16[8,2,2,2,2,10,512]{6,4,5,3,2,1,0:T(2,128)(2,1)S(1)}, u32[]{:S(2)}, u32[]{:S(2)}) %all-to-all-start.4) | async-done | bytes 1310752 | tf_op jit(solution)/shard_map/all_to_all | solution.py:322
  46.9 13.6 %all-to-all-start = ((f32[32,1,128]{2,1,0:T(1,128)}), f32[32,1,128]{2,1,0:T(1,128)S(1)}, u32[]{:S(2)}, u32[]{:S(2)}) async-start(f32[32,1,128]{2,1,0:T(1,128)} %get-tuple-element.10), calls=%async_computation | async-start | bytes 32768 | tf_op jit(solution)/shard_map/all_to_all | solution.py:303
  60.4 0.9 slice_bitcast_fusion
  61.3 0.5 copy.23
  61.8 0.1 copy.25.refs_0_
  61.9 0.0 copy-start.1
  61.9 0.5 copy.24
  62.3 0.0 copy-start.2
  62.4 0.0 copy-start.4
  62.4 0.1 copy.26.refs_1_
  62.4 4.0 %collective-permute-start.6 = (bf16[2,2,160,512]{3,2,1,0:T(8,128)(2,1)S(1)}, bf16[2,2,160,512]{3,2,1,0:T(8,128)(2,1)}, u32[]{:S(2)}, u32[]{:S(2)}) collective-permute-start(bf16[2,2,160,512]{3,2,1,0:T(8,128)(2,1)S(1)} %copy.26.refs_1_), channel_id=1, source_target_pairs={{0,16},{2,18},{16,32},{18,34},{32,48},{34,50},{48,64},{50,66},{64,... | collective-permute-start | bytes 1966088 | tf_op jit(solution)/shard_map/ppermute | solution.py:344
  66.4 1.3 collective-permute-start.7
  67.7 0.0 copy-done.1
  67.7 0.2 shard_map.110.refs_5_
  67.9 0.0 copy-start.3
  68.0 0.0 collective-permute-done.refs_2_
  68.0 0.0 collective-permute-done.1.refs_3_
  68.0 3.7 %all-to-all-done.refs_0_ = f32[32,1,128]{2,1,0:T(1,128)S(1)} async-done(((f32[32,1,128]{2,1,0:T(1,128)}), f32[32,1,128]{2,1,0:T(1,128)S(1)}, u32[]{:S(2)}, u32[]{:S(2)}) %all-to-all-start) | async-done | bytes 16416 | tf_op jit(solution)/shard_map/all_to_all | solution.py:303
  71.7 0.0 copy-done.2
  71.7 0.0 copy-done.4
  71.7 0.0 copy-start
  71.7 1.0 shard_map.111
  72.7 12.2 %all_to_all.30.refs_0_ = f32[8,80,128]{2,1,0:T(8,128)S(1)} all-to-all(f32[8,80,128]{2,1,0:T(8,128)S(1)} %shard_map.111), channel_id=1, replica_groups=mesh['y'=4,'l'=8,'x'=4,'h'=2,'k'=2] {'x','k'}, dimensions={0} | all-to-all | bytes 655360 | tf_op jit(solution)/shard_map/all_to_all | solution.py:313
  85.0 0.0 copy-done.3
  85.0 0.0 copy-start.5
  85.0 0.0 copy-start.6
  85.0 0.0 copy-start.7
  85.0 0.2 shard_map.112.refs_0_
  85.1 9.6 %collective-permute-start.2 = (f32[80,128]{1,0:T(8,128)S(1)}, f32[80,128]{1,0:T(8,128)S(1)}, u32[]{:S(2)}, u32[]{:S(2)}) collective-permute-start(f32[80,128]{1,0:T(8,128)S(1)} %shard_map.112.refs_0_), channel_id=1, source_target_pairs={{0,2},{2,0},{1,3},{3,1},{4,6},{6,4},{5,7},{7,5},{8,10},{10,8},{9,1... | collective-permute-start | bytes 122888 | tf_op jit(solution)/shard_map/ppermute | solution.py:315
  94.7 3.9 %collective-permute-done.2.refs_1_ = f32[80,128]{1,0:T(8,128)S(1)} collective-permute-done((f32[80,128]{1,0:T(8,128)S(1)}, f32[80,128]{1,0:T(8,128)S(1)}, u32[]{:S(2)}, u32[]{:S(2)}) %collective-permute-start.2) | collective-permute-done | bytes 40992 | tf_op jit(solution)/shard_map/ppermute | solution.py:315
  98.6 9.8 %all_to_all.31.refs_0_.refs_1_ = bf16[8,80,128]{2,1,0:T(8,128)(2,1)S(1)} all-to-all(bf16[8,80,128]{2,1,0:T(8,128)(2,1)S(1)} %shard_map.113), channel_id=1, replica_groups=mesh['y'=4,'l'=8,'x'=4,'h'=2,'k'=2] {'x','k'}, dimensions={0} | all-to-all | bytes 327680 | tf_op jit(solution)/shard_map/all_to_all | solution.py:317
  108.4 3.2 %collective-permute-start.3 = (bf16[8,80,128]{2,1,0:T(8,128)(2,1)S(1)}, bf16[8,80,128]{2,1,0:T(8,128)(2,1)S(1)}, u32[]{:S(2)}, u32[]{:S(2)}) collective-permute-start(bf16[8,80,128]{2,1,0:T(8,128)(2,1)S(1)} %all_to_all.31.refs_0_.refs_1_), channel_id=1, source_target_pairs={{0,16},{2,18},{16,32},{18,34},{32,48},{34,50},{48,64},{50,66},{64,... | collective-permute-start | bytes 491528 | tf_op jit(solution)/shard_map/ppermute | solution.py:346
  111.6 1.3 collective-permute-start.4
  112.9 1.0 shard_map.114
  114.0 12.2 %all-to-all-start.3 = ((f32[32,1,128]{2,1,0:T(1,128)}), f32[32,1,128]{2,1,0:T(1,128)S(1)}, u32[]{:S(2)}, u32[]{:S(2)}) async-start(f32[32,1,128]{2,1,0:T(1,128)} %shard_map.114), calls=%async_computation.3 | async-start | bytes 32768 | tf_op jit(solution)/shard_map/all_to_all | solution.py:348
  126.2 0.0 copy-done
  126.2 0.0 copy-done.5
  126.2 0.0 copy-done.6
  126.3 0.0 copy-done.7
  126.3 0.3 shard_map.115
  126.6 1.0 shard_map.117.refs_6_
  127.6 9.9 %all-to-all-done.3.refs_0_ = f32[32,1,128]{2,1,0:T(1,128)S(1)} async-done(((f32[32,1,128]{2,1,0:T(1,128)}), f32[32,1,128]{2,1,0:T(1,128)S(1)}, u32[]{:S(2)}, u32[]{:S(2)}) %all-to-all-start.3) | async-done | bytes 16416 | tf_op jit(solution)/shard_map/all_to_all | solution.py:348
  137.5 0.0 collective-permute-done.3.refs_2_
  137.5 0.0 collective-permute-done.4.refs_3_
  137.5 0.0 collective-permute-done.6.refs_8_
  137.5 0.0 collective-permute-done.7.refs_9_
  137.5 3.5 %shard_map.118 = bf16[16,10,128]{2,1,0:T(8,128)(2,1)S(1)} custom-call(f32[32,1,128]{2,1,0:T(1,128)S(1)} %all-to-all-done.3.refs_0_, bf16[8,80,128]{2,1,0:T(8,128)(2,1)S(1)} %all_to_all.31.refs_0_.refs_1_, bf16[8,80,128]{2,1,0:T(8,128)(2,1)S(1)} %collective-permute-done.3.refs_2_, bf16[8,80,128]{2,1,0:T(8,128)(2,1)S(1)} %collective-permute-done.4.refs_3_, ...), custom_call_target="tpu_custom_call" | custom-call | tf_op jit(solution)/shard_map/pallas_call | solution.py:33
  141.0 25.8 %all_to_all.32 = bf16[16,10,128]{2,1,0:T(8,128)(2,1)S(1)} all-to-all(bf16[16,10,128]{2,1,0:T(8,128)(2,1)S(1)} %shard_map.118), channel_id=1, replica_groups=mesh['y'=4,'l'=8,'x'=4,'h'=2,'k'=2] {'x','h','k'}, dimensions={0} | all-to-all | bytes 81920 | tf_op jit(solution)/shard_map/all_to_all | solution.py:373
  166.9 0.1 reshape.63
  167.1 0.8 reshape.64
  (4 shorter events, 0.1 us)
Async XLA Ops:
  0.0 18.6 %collective-permute-start.5 = (bf16[2,2,2,10,512]{4,1,2,3,0:T(2,128)(2,1)}, bf16[2,2,2,10,512]{4,1,2,3,0:T(2,128)(2,1)S(1)}, u32[]{:S(2)}, u32[]{:S(2)}) collective-permute-start(bf16[2,2,2,10,512]{4,1,2,3,0:T(2,128)(2,1)} %bitcast.53), channel_id=1, source_target_pairs={{0,2},{2,0},{1,3},{3,1},{4,6},{6,4},{5,7},{7,5},{8,10},{10,8},{9,1... | collective-permute-start | bytes 245768 | tf_op jit(solution)/shard_map/ppermute | solution.py:319
  22.1 24.8 %all-to-all-start.4 = ((bf16[8,2,2,2,2,10,512]{6,4,5,3,2,1,0:T(2,128)(2,1)}), bf16[8,2,2,2,2,10,512]{6,4,5,3,2,1,0:T(2,128)(2,1)S(1)}, u32[]{:S(2)}, u32[]{:S(2)}) async-start(bf16[8,2,2,2,2,10,512]{6,4,5,3,2,1,0:T(2,128)(2,1)} %broadcast_in_dim.30), calls=%async_computation.4 | async-start | bytes 2621440 | tf_op jit(solution)/shard_map/all_to_all | solution.py:322
  30.7 37.3 %collective-permute-start = (bf16[3,32,160]{2,1,0:T(8,128)(2,1)}, bf16[3,32,160]{2,1,0:T(8,128)(2,1)S(1)}, u32[]{:S(2)}, u32[]{:S(2)}) collective-permute-start(bf16[3,32,160]{2,1,0:T(8,128)(2,1)} %get-tuple-element.11.refs_1_), channel_id=1, source_target_pairs={{0,16},{16,32},{32,48},{48,64},{64,80},{80,96},{96,112},{112,128},... | collective-permute-start | bytes 92168 | tf_op jit(solution)/shard_map/ppermute | solution.py:306
  33.9 34.1 %collective-permute-start.1 = (bf16[3,32,160]{2,1,0:T(8,128)(2,1)}, bf16[3,32,160]{2,1,0:T(8,128)(2,1)S(1)}, u32[]{:S(2)}, u32[]{:S(2)}) collective-permute-start(bf16[3,32,160]{2,1,0:T(8,128)(2,1)} %get-tuple-element.11.refs_1_), channel_id=1, source_target_pairs={{16,0},{32,16},{48,32},{64,48},{80,64},{96,80},{112,96},{128,112},... | collective-permute-start | bytes 92168 | tf_op jit(solution)/shard_map/ppermute | solution.py:307
  46.9 24.9 %all-to-all-start = ((f32[32,1,128]{2,1,0:T(1,128)}), f32[32,1,128]{2,1,0:T(1,128)S(1)}, u32[]{:S(2)}, u32[]{:S(2)}) async-start(f32[32,1,128]{2,1,0:T(1,128)} %get-tuple-element.10), calls=%async_computation | async-start | bytes 32768 | tf_op jit(solution)/shard_map/all_to_all | solution.py:303
  61.9 5.9 %copy-start.1 = (bf16[3,3,3,32,512]{4,3,2,1,0:T(8,128)(2,1)S(1)}, bf16[3,3,3,32,512]{4,3,2,1,0:T(8,128)(2,1)}, u32[]{:S(2)}) copy-start(bf16[3,3,3,32,512]{4,3,2,1,0:T(8,128)(2,1)} %param.15) | copy-start | bytes 2654212
  62.3 9.4 %copy-start.2 = (f32[32,3]{1,0:T(8,128)S(1)}, f32[32,3]{1,0:T(8,128)}, u32[]{:S(2)}) copy-start(f32[32,3]{1,0:T(8,128)} %get-tuple-element.12.refs_4_.refs_2_) | copy-start | bytes 1156
  62.4 9.4 %copy-start.4 = (bf16[3,32,160]{2,1,0:T(8,128)(2,1)S(1)}, bf16[3,32,160]{2,1,0:T(8,128)(2,1)}, u32[]{:S(2)}) copy-start(bf16[3,32,160]{2,1,0:T(8,128)(2,1)} %get-tuple-element.11.refs_1_) | copy-start | bytes 92164
  62.4 75.0 %collective-permute-start.6 = (bf16[2,2,160,512]{3,2,1,0:T(8,128)(2,1)S(1)}, bf16[2,2,160,512]{3,2,1,0:T(8,128)(2,1)}, u32[]{:S(2)}, u32[]{:S(2)}) collective-permute-start(bf16[2,2,160,512]{3,2,1,0:T(8,128)(2,1)S(1)} %copy.26.refs_1_), channel_id=1, source_target_pairs={{0,16},{2,18},{16,32},{18,34},{32,48},{34,50},{48,64},{50,66},{64,... | collective-permute-start | bytes 1966088 | tf_op jit(solution)/shard_map/ppermute | solution.py:344
  66.4 71.0 %collective-permute-start.7 = (bf16[2,2,160,512]{3,2,1,0:T(8,128)(2,1)S(1)}, bf16[2,2,160,512]{3,2,1,0:T(8,128)(2,1)}, u32[]{:S(2)}, u32[]{:S(2)}) collective-permute-start(bf16[2,2,160,512]{3,2,1,0:T(8,128)(2,1)S(1)} %copy.25.refs_0_), channel_id=1, source_target_pairs={{16,0},{18,2},{32,16},{34,18},{48,32},{50,34},{64,48},{66,50},{80,... | collective-permute-start | bytes 1966088 | tf_op jit(solution)/shard_map/ppermute | solution.py:345
  67.9 17.0 %copy-start.3 = (bf16[1,1,160,32]{2,3,1,0:T(8,128)(2,1)S(1)}, bf16[1,1,160,32]{2,3,1,0:T(8,128)(2,1)}, u32[]{:S(2)}) copy-start(bf16[1,1,160,32]{2,3,1,0:T(8,128)(2,1)} %param.11) | copy-start | bytes 30724
  71.7 54.5 %copy-start = (bf16[3,3,3,512,32]{3,4,2,1,0:T(8,128)(2,1)S(1)}, bf16[3,3,3,512,32]{3,4,2,1,0:T(8,128)(2,1)}, u32[]{:S(2)}) copy-start(bf16[3,3,3,512,32]{3,4,2,1,0:T(8,128)(2,1)} %param.20) | copy-start | bytes 2654212
  85.0 41.3 %copy-start.5 = (f32[512]{0:T(512)S(1)}, f32[512]{0:T(512)}, u32[]{:S(2)}) copy-start(f32[512]{0:T(512)} %param.18) | copy-start | bytes 6148
  85.0 41.3 %copy-start.6 = (f32[512]{0:T(512)S(1)}, f32[512]{0:T(512)}, u32[]{:S(2)}) copy-start(f32[512]{0:T(512)} %param.19) | copy-start | bytes 6148
  85.0 41.3 %copy-start.7 = (f32[512]{0:T(512)S(1)}, f32[512]{0:T(512)}, u32[]{:S(2)}) copy-start(f32[512]{0:T(512)} %param.21) | copy-start | bytes 6148
  85.1 13.4 %collective-permute-start.2 = (f32[80,128]{1,0:T(8,128)S(1)}, f32[80,128]{1,0:T(8,128)S(1)}, u32[]{:S(2)}, u32[]{:S(2)}) collective-permute-start(f32[80,128]{1,0:T(8,128)S(1)} %shard_map.112.refs_0_), channel_id=1, source_target_pairs={{0,2},{2,0},{1,3},{3,1},{4,6},{6,4},{5,7},{7,5},{8,10},{10,8},{9,1... | collective-permute-start | bytes 122888 | tf_op jit(solution)/shard_map/ppermute | solution.py:315
  108.4 29.1 %collective-permute-start.3 = (bf16[8,80,128]{2,1,0:T(8,128)(2,1)S(1)}, bf16[8,80,128]{2,1,0:T(8,128)(2,1)S(1)}, u32[]{:S(2)}, u32[]{:S(2)}) collective-permute-start(bf16[8,80,128]{2,1,0:T(8,128)(2,1)S(1)} %all_to_all.31.refs_0_.refs_1_), channel_id=1, source_target_pairs={{0,16},{2,18},{16,32},{18,34},{32,48},{34,50},{48,64},{50,66},{64,... | collective-permute-start | bytes 491528 | tf_op jit(solution)/shard_map/ppermute | solution.py:346
  111.6 25.9 %collective-permute-start.4 = (bf16[8,80,128]{2,1,0:T(8,128)(2,1)S(1)}, bf16[8,80,128]{2,1,0:T(8,128)(2,1)S(1)}, u32[]{:S(2)}, u32[]{:S(2)}) collective-permute-start(bf16[8,80,128]{2,1,0:T(8,128)(2,1)S(1)} %all_to_all.31.refs_0_.refs_1_), channel_id=1, source_target_pairs={{16,0},{18,2},{32,16},{34,18},{48,32},{50,34},{64,48},{66,50},{80,... | collective-permute-start | bytes 491528 | tf_op jit(solution)/shard_map/ppermute | solution.py:347
  114.0 23.5 %all-to-all-start.3 = ((f32[32,1,128]{2,1,0:T(1,128)}), f32[32,1,128]{2,1,0:T(1,128)S(1)}, u32[]{:S(2)}, u32[]{:S(2)}) async-start(f32[32,1,128]{2,1,0:T(1,128)} %shard_map.114), calls=%async_computation.3 | async-start | bytes 32768 | tf_op jit(solution)/shard_map/all_to_all | solution.py:348

commit v9 on v8

--- a/solution.py
+++ b/solution.py
@@ -245,7 +245,7 @@
     )
 
 
-def up_conv(parts, row, above, below, affine, lhs, held, out_bias, old_above, old_below, kernel, sizes):
+def up_conv(parts, row, above, below, affine, lhs, held, edge, out_bias, sizes):
     row, above, below = rows_of(row), rows_of(above), rows_of(below)
     chans, cols = row.shape
     groups = chans // GS
@@ -267,7 +267,7 @@
         cut = [prod[dx * 32 : (dx + 1) * 32] for dx in range(3)]
         outs += [right(cut[0]) + cut[1] + cut[2], cut[0] + cut[1] + left(cut[2])]
     total = jnp.concatenate(outs, axis=0) + held
-    total = total + edge_conv(old_above, old_below, kernel)
+    total = total + edge
     total = (total + out_bias).T
     part = cols // 16
     return jnp.stack([total[c * part : (c + 1) * part] for c in range(16)]).astype(BF16)
@@ -326,7 +326,7 @@
         for r in range(2)
     ]
     kernel2 = conv2_weight.transpose(0, 1, 2, 4, 3).reshape(27 * 32, 512)
-    held = run(cache_conv, ((128, cols), F32), (*rows, kernel2), 16)
+    held = run(cache_conv, ((128, cols), F32), (*rows, kernel2))
     stats2 = run(functools.partial(row_stats, peers=peers), ((peers, 1, 128), F32), (gathered,))
 
     def at(y, l, h):
@@ -346,6 +346,7 @@
     row_above = lax.ppermute(gathered, ("y", "l", "h"), down_h)
     row_below = lax.ppermute(gathered, ("y", "l", "h"), up_h)
     stats2 = lax.all_to_all(stats2, space, 0, 0, tiled=True)
+    edge = run(edge_conv, ((128, cols), F32), (old_above, old_below, kernel2))
     affine2, bias_here = run(
         up_columns,
         [((512, 2), F32), ((128, 1), F32)],
@@ -363,12 +364,9 @@
             affine2,
             lhs,
             held,
+            edge,
             bias_here,
-            old_above,
-            old_below,
-            kernel2,
         ),
-        16,
     )
     out = lax.all_to_all(out, ("x", "h", "k"), 0, 0, tiled=True)
     out = out.reshape(16, 10, 2, 2, 32).transpose(2, 1, 3, 0, 4)

time: 169 us -> 167 us (0.988)
  waiting for transfers between devices: 31.5 us -> 28.9 us
    all_to_all x1, waiting for transfers between devices: 9.91 us -> 7.33 us  [on_device(): stats2 = lax.all_to_all(stats2, space, 0, 0, tiled=True)]
    pallas_call x9 -> x10, Pallas kernels: 8.67 us -> 8.71 us  [run(): pl.pallas_call(body, out_shape=[jax.ShapeDtypeStruct(s, d) for s, d in sh...]
  transfers between devices with their start and end apart: 11 -> 11, of which waited for: 5 -> 5; matrix products, arithmetic and copies ran while one was open for 1% -> 1% of each run, Pallas kernels for 3% -> 4%
where the time goes in v9:
time: 167 us; the launch traced here: 166 us
  starting transfers between devices  72.9 us (44%)
  blocking collectives  47.9 us (29%)
  waiting for transfers between devices  28.9 us (17%)
  Pallas kernels  8.89 us (5%)
  local copies, waits for them, and re-layouts  5.77 us (3%)
    all_to_all x1, blocking collectives, on_device(): out = lax.all_to_all(out, ('x', 'h', 'k'), 0, 0, tiled=True)  25.8 us
    ppermute x1, starting transfers between devices, on_device(): swapped = lax.ppermute(tile, 'h', [(0, 1), (1, 0)])  16.2 us
    all_to_all x1, starting transfers between devices, on_device(): stats = lax.all_to_all(stats, space, 0, 0, tiled=True)  13.6 us
    all_to_all x1, blocking collectives, on_device(): partial = lax.all_to_all(partial, ('x', 'k'), 0, 0, tiled=True)  12.2 us
    all_to_all x1, starting transfers between devices, on_device(): stats2 = lax.all_to_all(stats2, space, 0, 0, tiled=True)  12.2 us
    all_to_all x1, waiting for transfers between devices, on_device(): spread = lax.all_to_all(copies, ('x', 'k'), 0, 0, tiled=True)  11.6 us
    all_to_all x1, blocking collectives, on_device(): gathered = lax.all_to_all(gathered, ('x', 'k'), 0, 0, tiled=True)  9.83 us
    ppermute x1, starting transfers between devices, on_device(): other = lax.ppermute(mine, 'h', [(0, 1), (1, 0)])  9.58 us
  transfers between devices with their start and end apart: 11, of which 5 were waited for; matrix products, arithmetic and copies ran while one was open for 1% of the time, Pallas kernels for 4%

profile of v9, /device:TPU:1, one launch (start us, length us, event | category | flops | bytes accessed | tf_op | source)
XLA Modules:
  0.0 166.0 jit_solution(3358262769961007521)
XLA Ops:
  0.0 16.2 %collective-permute-start.5 = (bf16[2,2,2,10,512]{4,1,2,3,0:T(2,128)(2,1)}, bf16[2,2,2,10,512]{4,1,2,3,0:T(2,128)(2,1)S(1)}, u32[]{:S(2)}, u32[]{:S(2)}) collective-permute-start(bf16[2,2,2,10,512]{4,1,2,3,0:T(2,128)(2,1)} %bitcast.53), channel_id=1, source_target_pairs={{0,2},{2,0},{1,3},{3,1},{4,6},{6,4},{5,7},{7,5},{8,10},{10,8},{9,1... | collective-permute-start | bytes 245768 | tf_op jit(solution)/shard_map/ppermute | solution.py:319
  16.3 2.3 %collective-permute-done.5 = bf16[2,2,2,10,512]{4,1,2,3,0:T(2,128)(2,1)S(1)} collective-permute-done((bf16[2,2,2,10,512]{4,1,2,3,0:T(2,128)(2,1)}, bf16[2,2,2,10,512]{4,1,2,3,0:T(2,128)(2,1)S(1)}, u32[]{:S(2)}, u32[]{:S(2)}) %collective-permute-start.5) | collective-permute-done | bytes 81952 | tf_op jit(solution)/shard_map/ppermute | solution.py:319
  18.6 1.3 broadcast_select_fusion
  19.9 0.1 copy.22
  20.0 2.1 %broadcast_in_dim.30 = bf16[8,2,2,2,2,10,512]{6,4,5,3,2,1,0:T(2,128)(2,1)} broadcast(bf16[2,2,2,2,10,512]{5,3,4,2,1,0:T(2,128)(2,1)S(1)} %copy.22), dimensions={1,2,3,4,5,6} | broadcast | bytes 1474560 | tf_op jit(solution)/shard_map/broadcast_in_dim | solution.py:321
  22.1 7.0 %all-to-all-start.4 = ((bf16[8,2,2,2,2,10,512]{6,4,5,3,2,1,0:T(2,128)(2,1)}), bf16[8,2,2,2,2,10,512]{6,4,5,3,2,1,0:T(2,128)(2,1)S(1)}, u32[]{:S(2)}, u32[]{:S(2)}) async-start(bf16[8,2,2,2,2,10,512]{6,4,5,3,2,1,0:T(2,128)(2,1)} %broadcast_in_dim.30), calls=%async_computation.4 | async-start | bytes 2621440 | tf_op jit(solution)/shard_map/all_to_all | solution.py:322
  29.1 1.6 shard_map.109
  30.7 3.2 %collective-permute-start = (bf16[3,32,160]{2,1,0:T(8,128)(2,1)}, bf16[3,32,160]{2,1,0:T(8,128)(2,1)S(1)}, u32[]{:S(2)}, u32[]{:S(2)}) collective-permute-start(bf16[3,32,160]{2,1,0:T(8,128)(2,1)} %get-tuple-element.11.refs_1_), channel_id=1, source_target_pairs={{0,16},{16,32},{32,48},{48,64},{64,80},{80,96},{96,112},{112,128},... | collective-permute-start | bytes 92168 | tf_op jit(solution)/shard_map/ppermute | solution.py:306
  33.9 1.3 collective-permute-start.1
  35.2 11.6 %all-to-all-done.4 = bf16[8,2,2,2,2,10,512]{6,4,5,3,2,1,0:T(2,128)(2,1)S(1)} async-done(((bf16[8,2,2,2,2,10,512]{6,4,5,3,2,1,0:T(2,128)(2,1)}), bf16[8,2,2,2,2,10,512]{6,4,5,3,2,1,0:T(2,128)(2,1)S(1)}, u32[]{:S(2)}, u32[]{:S(2)}) %all-to-all-start.4) | async-done | bytes 1310752 | tf_op jit(solution)/shard_map/all_to_all | solution.py:322
  46.9 13.6 %all-to-all-start = ((f32[32,1,128]{2,1,0:T(1,128)}), f32[32,1,128]{2,1,0:T(1,128)S(1)}, u32[]{:S(2)}, u32[]{:S(2)}) async-start(f32[32,1,128]{2,1,0:T(1,128)} %get-tuple-element.10), calls=%async_computation | async-start | bytes 32768 | tf_op jit(solution)/shard_map/all_to_all | solution.py:303
  60.4 0.9 slice_bitcast_fusion
  61.3 0.5 copy.24
  61.8 0.1 copy.26.refs_1_
  61.9 4.0 %collective-permute-start.6 = (bf16[2,2,160,512]{3,2,1,0:T(8,128)(2,1)S(1)}, bf16[2,2,160,512]{3,2,1,0:T(8,128)(2,1)}, u32[]{:S(2)}, u32[]{:S(2)}) collective-permute-start(bf16[2,2,160,512]{3,2,1,0:T(8,128)(2,1)S(1)} %copy.26.refs_1_), channel_id=1, source_target_pairs={{0,16},{2,18},{16,32},{18,34},{32,48},{34,50},{48,64},{50,66},{64,... | collective-permute-start | bytes 1966088 | tf_op jit(solution)/shard_map/ppermute | solution.py:344
  65.9 0.0 copy-start.1
  65.9 0.5 copy.23
  66.3 0.0 copy-start.2
  66.4 0.0 copy-start.6
  66.4 0.1 copy.25.refs_0_
  66.4 1.3 collective-permute-start.7
  67.7 0.0 copy-done.1
  67.8 0.2 shard_map.110.refs_5_
  67.9 0.0 copy-start.5
  68.0 0.0 collective-permute-done.refs_2_
  68.0 0.0 collective-permute-done.1.refs_3_
  68.0 3.7 %all-to-all-done.refs_0_ = f32[32,1,128]{2,1,0:T(1,128)S(1)} async-done(((f32[32,1,128]{2,1,0:T(1,128)}), f32[32,1,128]{2,1,0:T(1,128)S(1)}, u32[]{:S(2)}, u32[]{:S(2)}) %all-to-all-start) | async-done | bytes 16416 | tf_op jit(solution)/shard_map/all_to_all | solution.py:303
  71.7 0.0 copy-done.2
  71.7 0.0 copy-done.6
  71.7 0.0 copy-start
  71.7 1.0 shard_map.111
  72.7 12.2 %all_to_all.30.refs_0_ = f32[8,80,128]{2,1,0:T(8,128)S(1)} all-to-all(f32[8,80,128]{2,1,0:T(8,128)S(1)} %shard_map.111), channel_id=1, replica_groups=mesh['y'=4,'l'=8,'x'=4,'h'=2,'k'=2] {'x','k'}, dimensions={0} | all-to-all | bytes 655360 | tf_op jit(solution)/shard_map/all_to_all | solution.py:313
  85.0 0.0 copy-done.5
  85.0 0.0 copy-start.7
  85.0 0.0 copy-start.8
  85.0 0.0 copy-start.9
  85.0 0.2 shard_map.112.refs_0_
  85.1 9.6 %collective-permute-start.2 = (f32[80,128]{1,0:T(8,128)S(1)}, f32[80,128]{1,0:T(8,128)S(1)}, u32[]{:S(2)}, u32[]{:S(2)}) collective-permute-start(f32[80,128]{1,0:T(8,128)S(1)} %shard_map.112.refs_0_), channel_id=1, source_target_pairs={{0,2},{2,0},{1,3},{3,1},{4,6},{6,4},{5,7},{7,5},{8,10},{10,8},{9,1... | collective-permute-start | bytes 122888 | tf_op jit(solution)/shard_map/ppermute | solution.py:315
  94.7 3.9 %collective-permute-done.2.refs_1_ = f32[80,128]{1,0:T(8,128)S(1)} collective-permute-done((f32[80,128]{1,0:T(8,128)S(1)}, f32[80,128]{1,0:T(8,128)S(1)}, u32[]{:S(2)}, u32[]{:S(2)}) %collective-permute-start.2) | collective-permute-done | bytes 40992 | tf_op jit(solution)/shard_map/ppermute | solution.py:315
  98.6 9.8 %all_to_all.31.refs_0_.refs_1_ = bf16[8,80,128]{2,1,0:T(8,128)(2,1)S(1)} all-to-all(bf16[8,80,128]{2,1,0:T(8,128)(2,1)S(1)} %shard_map.113), channel_id=1, replica_groups=mesh['y'=4,'l'=8,'x'=4,'h'=2,'k'=2] {'x','k'}, dimensions={0} | all-to-all | bytes 327680 | tf_op jit(solution)/shard_map/all_to_all | solution.py:317
  108.4 3.2 %collective-permute-start.3 = (bf16[8,80,128]{2,1,0:T(8,128)(2,1)S(1)}, bf16[8,80,128]{2,1,0:T(8,128)(2,1)S(1)}, u32[]{:S(2)}, u32[]{:S(2)}) collective-permute-start(bf16[8,80,128]{2,1,0:T(8,128)(2,1)S(1)} %all_to_all.31.refs_0_.refs_1_), channel_id=1, source_target_pairs={{0,16},{2,18},{16,32},{18,34},{32,48},{34,50},{48,64},{50,66},{64,... | collective-permute-start | bytes 491528 | tf_op jit(solution)/shard_map/ppermute | solution.py:346
  111.6 1.3 collective-permute-start.4
  112.9 1.0 shard_map.114
  114.0 12.2 %all-to-all-start.3 = ((f32[32,1,128]{2,1,0:T(1,128)}), f32[32,1,128]{2,1,0:T(1,128)S(1)}, u32[]{:S(2)}, u32[]{:S(2)}) async-start(f32[32,1,128]{2,1,0:T(1,128)} %shard_map.114), calls=%async_computation.3 | async-start | bytes 32768 | tf_op jit(solution)/shard_map/all_to_all | solution.py:348
  126.2 0.0 copy-done
  126.2 0.0 copy-done.7
  126.3 0.0 copy-done.8
  126.3 0.0 copy-done.9
  126.3 0.3 shard_map.115
  126.6 0.0 copy-start.3
  126.6 0.6 copy-done.3
  127.2 1.0 shard_map.117.refs_6_
  128.2 0.0 collective-permute-done.6.refs_0_
  128.2 0.0 copy-start.4
  128.2 0.0 collective-permute-done.7.refs_1_
  128.2 1.9 %shard_map.118.refs_7_ = f32[128,160]{1,0:T(8,128)S(1)} custom-call(bf16[2,2,160,512]{3,2,1,0:T(8,128)(2,1)} %collective-permute-done.6.refs_0_, bf16[2,2,160,512]{3,2,1,0:T(8,128)(2,1)} %collective-permute-done.7.refs_1_, bf16[864,512]{1,0:T(8,128)(2,1)S(1)} %bitcast.42), custom_call_target="tpu_custom_call" | custom-call | tf_op jit(solution)/shard_map/pallas_call | solution.py:33
  130.2 7.3 %all-to-all-done.3.refs_0_ = f32[32,1,128]{2,1,0:T(1,128)S(1)} async-done(((f32[32,1,128]{2,1,0:T(1,128)}), f32[32,1,128]{2,1,0:T(1,128)S(1)}, u32[]{:S(2)}, u32[]{:S(2)}) %all-to-all-start.3) | async-done | bytes 16416 | tf_op jit(solution)/shard_map/all_to_all | solution.py:348
  137.5 0.0 collective-permute-done.3.refs_2_
  137.5 0.0 collective-permute-done.4.refs_3_
  137.5 0.0 copy-done.4
  137.5 1.6 shard_map.119
  139.2 25.8 %all_to_all.32 = bf16[16,10,128]{2,1,0:T(8,128)(2,1)S(1)} all-to-all(bf16[16,10,128]{2,1,0:T(8,128)(2,1)S(1)} %shard_map.119), channel_id=1, replica_groups=mesh['y'=4,'l'=8,'x'=4,'h'=2,'k'=2] {'x','h','k'}, dimensions={0} | all-to-all | bytes 81920 | tf_op jit(solution)/shard_map/all_to_all | solution.py:371
  165.0 0.1 reshape.63
  165.2 0.8 reshape.64
  (4 shorter events, 0.1 us)
Async XLA Ops:
  0.0 18.6 %collective-permute-start.5 = (bf16[2,2,2,10,512]{4,1,2,3,0:T(2,128)(2,1)}, bf16[2,2,2,10,512]{4,1,2,3,0:T(2,128)(2,1)S(1)}, u32[]{:S(2)}, u32[]{:S(2)}) collective-permute-start(bf16[2,2,2,10,512]{4,1,2,3,0:T(2,128)(2,1)} %bitcast.53), channel_id=1, source_target_pairs={{0,2},{2,0},{1,3},{3,1},{4,6},{6,4},{5,7},{7,5},{8,10},{10,8},{9,1... | collective-permute-start | bytes 245768 | tf_op jit(solution)/shard_map/ppermute | solution.py:319
  22.1 24.8 %all-to-all-start.4 = ((bf16[8,2,2,2,2,10,512]{6,4,5,3,2,1,0:T(2,128)(2,1)}), bf16[8,2,2,2,2,10,512]{6,4,5,3,2,1,0:T(2,128)(2,1)S(1)}, u32[]{:S(2)}, u32[]{:S(2)}) async-start(bf16[8,2,2,2,2,10,512]{6,4,5,3,2,1,0:T(2,128)(2,1)} %broadcast_in_dim.30), calls=%async_computation.4 | async-start | bytes 2621440 | tf_op jit(solution)/shard_map/all_to_all | solution.py:322
  30.7 37.3 %collective-permute-start = (bf16[3,32,160]{2,1,0:T(8,128)(2,1)}, bf16[3,32,160]{2,1,0:T(8,128)(2,1)S(1)}, u32[]{:S(2)}, u32[]{:S(2)}) collective-permute-start(bf16[3,32,160]{2,1,0:T(8,128)(2,1)} %get-tuple-element.11.refs_1_), channel_id=1, source_target_pairs={{0,16},{16,32},{32,48},{48,64},{64,80},{80,96},{96,112},{112,128},... | collective-permute-start | bytes 92168 | tf_op jit(solution)/shard_map/ppermute | solution.py:306
  33.9 34.1 %collective-permute-start.1 = (bf16[3,32,160]{2,1,0:T(8,128)(2,1)}, bf16[3,32,160]{2,1,0:T(8,128)(2,1)S(1)}, u32[]{:S(2)}, u32[]{:S(2)}) collective-permute-start(bf16[3,32,160]{2,1,0:T(8,128)(2,1)} %get-tuple-element.11.refs_1_), channel_id=1, source_target_pairs={{16,0},{32,16},{48,32},{64,48},{80,64},{96,80},{112,96},{128,112},... | collective-permute-start | bytes 92168 | tf_op jit(solution)/shard_map/ppermute | solution.py:307
  46.9 24.9 %all-to-all-start = ((f32[32,1,128]{2,1,0:T(1,128)}), f32[32,1,128]{2,1,0:T(1,128)S(1)}, u32[]{:S(2)}, u32[]{:S(2)}) async-start(f32[32,1,128]{2,1,0:T(1,128)} %get-tuple-element.10), calls=%async_computation | async-start | bytes 32768 | tf_op jit(solution)/shard_map/all_to_all | solution.py:303
  61.9 66.3 %collective-permute-start.6 = (bf16[2,2,160,512]{3,2,1,0:T(8,128)(2,1)S(1)}, bf16[2,2,160,512]{3,2,1,0:T(8,128)(2,1)}, u32[]{:S(2)}, u32[]{:S(2)}) collective-permute-start(bf16[2,2,160,512]{3,2,1,0:T(8,128)(2,1)S(1)} %copy.26.refs_1_), channel_id=1, source_target_pairs={{0,16},{2,18},{16,32},{18,34},{32,48},{34,50},{48,64},{50,66},{64,... | collective-permute-start | bytes 1966088 | tf_op jit(solution)/shard_map/ppermute | solution.py:344
  65.9 1.9 %copy-start.1 = (bf16[3,3,3,32,512]{4,3,2,1,0:T(8,128)(2,1)S(1)}, bf16[3,3,3,32,512]{4,3,2,1,0:T(8,128)(2,1)}, u32[]{:S(2)}) copy-start(bf16[3,3,3,32,512]{4,3,2,1,0:T(8,128)(2,1)} %param.15) | copy-start | bytes 2654212
  66.3 5.4 %copy-start.2 = (f32[32,3]{1,0:T(8,128)S(1)}, f32[32,3]{1,0:T(8,128)}, u32[]{:S(2)}) copy-start(f32[32,3]{1,0:T(8,128)} %get-tuple-element.12.refs_4_.refs_2_) | copy-start | bytes 1156
  66.4 5.4 %copy-start.6 = (bf16[3,32,160]{2,1,0:T(8,128)(2,1)S(1)}, bf16[3,32,160]{2,1,0:T(8,128)(2,1)}, u32[]{:S(2)}) copy-start(bf16[3,32,160]{2,1,0:T(8,128)(2,1)} %get-tuple-element.11.refs_1_) | copy-start | bytes 92164
  66.4 61.8 %collective-permute-start.7 = (bf16[2,2,160,512]{3,2,1,0:T(8,128)(2,1)S(1)}, bf16[2,2,160,512]{3,2,1,0:T(8,128)(2,1)}, u32[]{:S(2)}, u32[]{:S(2)}) collective-permute-start(bf16[2,2,160,512]{3,2,1,0:T(8,128)(2,1)S(1)} %copy.25.refs_0_), channel_id=1, source_target_pairs={{16,0},{18,2},{32,16},{34,18},{48,32},{50,34},{64,48},{66,50},{80,... | collective-permute-start | bytes 1966088 | tf_op jit(solution)/shard_map/ppermute | solution.py:345
  67.9 17.0 %copy-start.5 = (bf16[1,1,160,32]{2,3,1,0:T(8,128)(2,1)S(1)}, bf16[1,1,160,32]{2,3,1,0:T(8,128)(2,1)}, u32[]{:S(2)}) copy-start(bf16[1,1,160,32]{2,3,1,0:T(8,128)(2,1)} %param.11) | copy-start | bytes 30724
  71.7 54.5 %copy-start = (bf16[3,3,3,512,32]{3,4,2,1,0:T(8,128)(2,1)S(1)}, bf16[3,3,3,512,32]{3,4,2,1,0:T(8,128)(2,1)}, u32[]{:S(2)}) copy-start(bf16[3,3,3,512,32]{3,4,2,1,0:T(8,128)(2,1)} %param.20) | copy-start | bytes 2654212
  85.0 41.3 %copy-start.7 = (f32[512]{0:T(512)S(1)}, f32[512]{0:T(512)}, u32[]{:S(2)}) copy-start(f32[512]{0:T(512)} %param.18) | copy-start | bytes 6148
  85.0 41.3 %copy-start.8 = (f32[512]{0:T(512)S(1)}, f32[512]{0:T(512)}, u32[]{:S(2)}) copy-start(f32[512]{0:T(512)} %param.19) | copy-start | bytes 6148
  85.0 41.3 %copy-start.9 = (f32[512]{0:T(512)S(1)}, f32[512]{0:T(512)}, u32[]{:S(2)}) copy-start(f32[512]{0:T(512)} %param.21) | copy-start | bytes 6148
  85.1 13.4 %collective-permute-start.2 = (f32[80,128]{1,0:T(8,128)S(1)}, f32[80,128]{1,0:T(8,128)S(1)}, u32[]{:S(2)}, u32[]{:S(2)}) collective-permute-start(f32[80,128]{1,0:T(8,128)S(1)} %shard_map.112.refs_0_), channel_id=1, source_target_pairs={{0,2},{2,0},{1,3},{3,1},{4,6},{6,4},{5,7},{7,5},{8,10},{10,8},{9,1... | collective-permute-start | bytes 122888 | tf_op jit(solution)/shard_map/ppermute | solution.py:315
  108.4 29.1 %collective-permute-start.3 = (bf16[8,80,128]{2,1,0:T(8,128)(2,1)S(1)}, bf16[8,80,128]{2,1,0:T(8,128)(2,1)S(1)}, u32[]{:S(2)}, u32[]{:S(2)}) collective-permute-start(bf16[8,80,128]{2,1,0:T(8,128)(2,1)S(1)} %all_to_all.31.refs_0_.refs_1_), channel_id=1, source_target_pairs={{0,16},{2,18},{16,32},{18,34},{32,48},{34,50},{48,64},{50,66},{64,... | collective-permute-start | bytes 491528 | tf_op jit(solution)/shard_map/ppermute | solution.py:346
  111.6 25.9 %collective-permute-start.4 = (bf16[8,80,128]{2,1,0:T(8,128)(2,1)S(1)}, bf16[8,80,128]{2,1,0:T(8,128)(2,1)S(1)}, u32[]{:S(2)}, u32[]{:S(2)}) collective-permute-start(bf16[8,80,128]{2,1,0:T(8,128)(2,1)S(1)} %all_to_all.31.refs_0_.refs_1_), channel_id=1, source_target_pairs={{16,0},{18,2},{32,16},{34,18},{48,32},{50,34},{64,48},{66,50},{80,... | collective-permute-start | bytes 491528 | tf_op jit(solution)/shard_map/ppermute | solution.py:347
  114.0 23.5 %all-to-all-start.3 = ((f32[32,1,128]{2,1,0:T(1,128)}), f32[32,1,128]{2,1,0:T(1,128)S(1)}, u32[]{:S(2)}, u32[]{:S(2)}) async-start(f32[32,1,128]{2,1,0:T(1,128)} %shard_map.114), calls=%async_computation.3 | async-start | bytes 32768 | tf_op jit(solution)/shard_map/all_to_all | solution.py:348
  126.6 0.6 copy-start.3
  128.2 9.3 %copy-start.4 = (f32[128,1]{1,0:T(8,128)S(1)}, f32[128,1]{1,0:T(8,128)}, u32[]{:S(2)}) copy-start(f32[128,1]{1,0:T(8,128)} %copy-done.3) | copy-start | bytes 1540

commit v10 on v7

--- a/solution.py
+++ b/solution.py
@@ -187,9 +187,12 @@
     )
 
 
-def row_stats(gathered, to_above, to_below, peers):
+def row_stats(gathered, peers):
+    return partial_stats(rows_of(gathered), peers)
+
+
+def join_rows(gathered, to_above, to_below):
     return (
-        partial_stats(rows_of(gathered), peers),
         jnp.concatenate([gathered, to_above], axis=0),
         jnp.concatenate([gathered, to_below], axis=0),
     )
@@ -350,10 +353,9 @@
         (images, kernel2),
         16,
     )
-    stats2, going_up, going_down = run(
-        functools.partial(row_stats, peers=peers),
-        [((peers, 1, 128), F32), ((10, 80, 128), BF16), ((10, 80, 128), BF16)],
-        (gathered, to_above, to_below),
+    stats2 = run(functools.partial(row_stats, peers=peers), ((peers, 1, 128), F32), (gathered,))
+    going_up, going_down = run(
+        join_rows, [((10, 80, 128), BF16), ((10, 80, 128), BF16)], (gathered, to_above, to_below)
     )
     row_above = lax.ppermute(going_down, space, down)
     row_below = lax.ppermute(going_up, space, up)

time: 152 us -> 152 us (level)
    pallas_call x9 -> x10, Pallas kernels: 8.06 us -> 8.09 us  [run(): pl.pallas_call(body, out_shape=[jax.ShapeDtypeStruct(s, d) for s, d in sh...]
  transfers between devices with their start and end apart: 11 -> 11, of which waited for: 7 -> 7; matrix products, arithmetic and copies ran while one was open for 1% -> 1% of each run, Pallas kernels for 1% -> 2%
where the time goes in v10:
time: 152 us
  starting transfers between devices  80.7 us (53%)
  waiting for transfers between devices  31.9 us (21%)
  blocking collectives  23.5 us (15%)
  Pallas kernels  8.27 us (5%)
  local copies, waits for them, and re-layouts  6.72 us (4%)
    all_to_all x1, blocking collectives, on_device(): out = lax.all_to_all(out, ('x', 'h', 'k'), 0, 0, tiled=True)  23.5 us
    all_to_all x1, starting transfers between devices, on_device(): stats2 = lax.all_to_all(stats2, space, 0, 0, tiled=True)  21.9 us
    all_to_all x1, starting transfers between devices, on_device(): stats = lax.all_to_all(stats, space, 0, 0, tiled=True)  16.2 us
    all_to_all x1, waiting for transfers between devices, on_device(): stats2 = lax.all_to_all(stats2, space, 0, 0, tiled=True)  10.9 us
    ppermute x1, starting transfers between devices, on_device(): other = lax.ppermute(mine, 'h', [(0, 1), (1, 0)])  10.5 us
    pallas_call x10, Pallas kernels, run(): pl.pallas_call(body, out_shape=[jax.ShapeDtypeStruct(s, d) for s, d in sh...  8.09 us
    ppermute x1, starting transfers between devices, on_device(): swapped = lax.ppermute(tile, 'h', [(0, 1), (1, 0)])  7.93 us
    ppermute x1, waiting for transfers between devices, on_device(): swapped = lax.ppermute(tile, 'h', [(0, 1), (1, 0)])  6.69 us
  transfers between devices with their start and end apart: 11, of which 7 were waited for; matrix products, arithmetic and copies ran while one was open for 1% of the time, Pallas kernels for 2%

profile of v10, /device:TPU:1, one launch (start us, length us, event | category | flops | bytes accessed | tf_op | source)
XLA Modules:
  0.0 151.6 jit_solution(14583207731490159716)
XLA Ops:
  0.0 1.6 %shard_map.109 = (f32[32,1,128]{2,1,0:T(1,128)}, bf16[3,32,160]{2,1,0:T(8,128)(2,1)}, f32[32,3]{1,0:T(8,128)}) custom-call(bf16[32,160]{1,0:T(8,128)(2,1)} %bitcast.36, bf16[2,32,160]{2,1,0:T(8,128)(2,1)} %bitcast.47, f32[1,32]{1,0:T(1,128)} %bitcast.48, f32[1,32]{1,0:T(1,128)} %bitcast.49, f32[1,32]{1,0:T(1,128)} %bitcast.50), custom_call_target="tpu_custom_call" | custom-call | tf_op jit(solution)/shard_map/pallas_call | solution.py:33
  1.6 0.0 copy-start.2
  1.6 16.2 %all-to-all-start = ((f32[32,1,128]{2,1,0:T(1,128)}), f32[32,1,128]{2,1,0:T(1,128)S(1)}, u32[]{:S(2)}, u32[]{:S(2)}) async-start(f32[32,1,128]{2,1,0:T(1,128)} %get-tuple-element.15), calls=%async_computation | async-start | bytes 32768 | tf_op jit(solution)/shard_map/all_to_all | solution.py:324
  17.9 3.1 %collective-permute-start = (bf16[3,32,160]{2,1,0:T(8,128)(2,1)}, bf16[3,32,160]{2,1,0:T(8,128)(2,1)S(1)}, u32[]{:S(2)}, u32[]{:S(2)}) collective-permute-start(bf16[3,32,160]{2,1,0:T(8,128)(2,1)} %get-tuple-element.16.refs_1_), channel_id=1, source_target_pairs={{0,16},{16,32},{32,48},{48,64},{64,80},{80,96},{96,112},{112,128},... | collective-permute-start | bytes 92168 | tf_op jit(solution)/shard_map/ppermute | solution.py:327
  21.0 1.3 collective-permute-start.1
  22.3 0.0 copy-start.1
  22.3 1.2 copy-done.1
  23.5 0.0 copy-start.4
  23.5 0.2 shard_map.110.refs_5_
  23.7 0.0 copy-start.8
  23.7 0.0 collective-permute-done.refs_2_
  23.7 2.7 %collective-permute-done.1.refs_3_ = bf16[3,32,160]{2,1,0:T(8,128)(2,1)S(1)} collective-permute-done((bf16[3,32,160]{2,1,0:T(8,128)(2,1)}, bf16[3,32,160]{2,1,0:T(8,128)(2,1)S(1)}, u32[]{:S(2)}, u32[]{:S(2)}) %collective-permute-start.1) | collective-permute-done | bytes 30752 | tf_op jit(solution)/shard_map/ppermute | solution.py:328
  26.4 2.8 %all-to-all-done.refs_0_ = f32[32,1,128]{2,1,0:T(1,128)S(1)} async-done(((f32[32,1,128]{2,1,0:T(1,128)}), f32[32,1,128]{2,1,0:T(1,128)S(1)}, u32[]{:S(2)}, u32[]{:S(2)}) %all-to-all-start) | async-done | bytes 16416 | tf_op jit(solution)/shard_map/all_to_all | solution.py:324
  29.1 0.0 copy-done.2
  29.1 0.0 copy-done.4
  29.2 1.7 %shard_map.111 = f32[8,80,128]{2,1,0:T(8,128)} custom-call(f32[32,1,128]{2,1,0:T(1,128)S(1)} %all-to-all-done.refs_0_, bf16[3,32,160]{2,1,0:T(8,128)(2,1)S(1)} %copy-done.4, bf16[3,32,160]{2,1,0:T(8,128)(2,1)S(1)} %collective-permute-done.refs_2_, bf16[3,32,160]{2,1,0:T(8,128)(2,1)S(1)} %collective-permute-done.1.refs_3_, f32[32,3]{1,0:T(8,128)S(1)} %copy-done.2, ...), custom_call_target="tpu_custom_call" | custom-call | tf_op jit(solution)/shard_map/pallas_call | solution.py:33
  30.9 6.4 %all-to-all-start.1 = ((f32[8,80,128]{2,1,0:T(8,128)}), f32[8,80,128]{2,1,0:T(8,128)S(1)}, u32[]{:S(2)}, u32[]{:S(2)}) async-start(f32[8,80,128]{2,1,0:T(8,128)} %shard_map.111), calls=%async_computation.1 | async-start | bytes 655360 | tf_op jit(solution)/shard_map/all_to_all | solution.py:334
  37.3 0.0 copy-done.8
  37.3 7.9 %collective-permute-start.3 = (bf16[2,2,2,10,512]{4,1,2,3,0:T(2,128)(2,1)S(1)}, bf16[2,2,2,10,512]{4,1,2,3,0:T(2,128)(2,1)S(1)}, u32[]{:S(2)}, u32[]{:S(2)}) collective-permute-start(bf16[2,2,2,10,512]{4,1,2,3,0:T(2,128)(2,1)S(1)} %bitcast.44), channel_id=1, source_target_pairs={{0,2},{2,0},{1,3},{3,1},{4,6},{6,4},{5,7},{7,5},{8,10},{10,8},{9,1... | collective-permute-start | bytes 245768 | tf_op jit(solution)/shard_map/ppermute | solution.py:340
  45.2 6.7 %collective-permute-done.3 = bf16[2,2,2,10,512]{4,1,2,3,0:T(2,128)(2,1)S(1)} collective-permute-done((bf16[2,2,2,10,512]{4,1,2,3,0:T(2,128)(2,1)S(1)}, bf16[2,2,2,10,512]{4,1,2,3,0:T(2,128)(2,1)S(1)}, u32[]{:S(2)}, u32[]{:S(2)}) %collective-permute-start.3) | collective-permute-done | bytes 81952 | tf_op jit(solution)/shard_map/ppermute | solution.py:340
  51.9 0.2 broadcast_select_fusion
  52.1 0.1 copy.18
  52.3 0.0 all-to-all-done.1.refs_0_
  52.3 2.1 %broadcast_in_dim.27 = bf16[8,2,2,2,2,10,512]{6,4,5,3,2,1,0:T(2,128)(2,1)} broadcast(bf16[2,2,2,2,10,512]{5,3,4,2,1,0:T(2,128)(2,1)S(1)} %copy.18), dimensions={1,2,3,4,5,6} | broadcast | bytes 1474560 | tf_op jit(solution)/shard_map/broadcast_in_dim | solution.py:342
  54.4 0.0 copy-start.3
  54.4 5.7 %all-to-all-start.4 = ((bf16[8,2,2,2,2,10,512]{6,4,5,3,2,1,0:T(2,128)(2,1)}), bf16[8,2,2,2,2,10,512]{6,4,5,3,2,1,0:T(2,128)(2,1)S(1)}, u32[]{:S(2)}, u32[]{:S(2)}) async-start(bf16[8,2,2,2,2,10,512]{6,4,5,3,2,1,0:T(2,128)(2,1)} %broadcast_in_dim.27), calls=%async_computation.4 | async-start | bytes 2621440 | tf_op jit(solution)/shard_map/all_to_all | solution.py:343
  60.1 0.0 copy-done.3
  60.1 0.2 shard_map.112.refs_0_
  60.2 10.5 %collective-permute-start.2 = (f32[80,128]{1,0:T(8,128)S(1)}, f32[80,128]{1,0:T(8,128)S(1)}, u32[]{:S(2)}, u32[]{:S(2)}) collective-permute-start(f32[80,128]{1,0:T(8,128)S(1)} %shard_map.112.refs_0_), channel_id=1, source_target_pairs={{0,2},{2,0},{1,3},{3,1},{4,6},{6,4},{5,7},{7,5},{8,10},{10,8},{9,1... | collective-permute-start | bytes 122888 | tf_op jit(solution)/shard_map/ppermute | solution.py:336
  70.7 3.0 %collective-permute-done.2.refs_1_ = f32[80,128]{1,0:T(8,128)S(1)} collective-permute-done((f32[80,128]{1,0:T(8,128)S(1)}, f32[80,128]{1,0:T(8,128)S(1)}, u32[]{:S(2)}, u32[]{:S(2)}) %collective-permute-start.2) | collective-permute-done | bytes 40992 | tf_op jit(solution)/shard_map/ppermute | solution.py:336
  73.7 0.7 shard_map.113
  74.4 3.5 %all-to-all-done.4 = bf16[8,2,2,2,2,10,512]{6,4,5,3,2,1,0:T(2,128)(2,1)S(1)} async-done(((bf16[8,2,2,2,2,10,512]{6,4,5,3,2,1,0:T(2,128)(2,1)}), bf16[8,2,2,2,2,10,512]{6,4,5,3,2,1,0:T(2,128)(2,1)S(1)}, u32[]{:S(2)}, u32[]{:S(2)}) %all-to-all-start.4) | async-done | bytes 1310752 | tf_op jit(solution)/shard_map/all_to_all | solution.py:343
  77.9 4.3 %all-to-all-start.2 = ((bf16[8,80,128]{2,1,0:T(8,128)(2,1)}), bf16[8,80,128]{2,1,0:T(8,128)(2,1)S(1)}, u32[]{:S(2)}, u32[]{:S(2)}) async-start(bf16[8,80,128]{2,1,0:T(8,128)(2,1)} %shard_map.113), calls=%async_computation.2 | async-start | bytes 327680 | tf_op jit(solution)/shard_map/all_to_all | solution.py:338
  82.1 1.2 copy.19
  83.3 0.0 copy-start
  83.3 0.2 copy.20.refs_0_
  83.6 0.9 copy-done
  84.5 0.9 shard_map.115
  85.4 0.0 copy-start.5
  85.4 0.0 copy-start.6
  85.4 0.0 copy-start.7
  85.4 2.3 %all-to-all-done.2.refs_0_.refs_1_ = bf16[8,80,128]{2,1,0:T(8,128)(2,1)S(1)} async-done(((bf16[8,80,128]{2,1,0:T(8,128)(2,1)}), bf16[8,80,128]{2,1,0:T(8,128)(2,1)S(1)}, u32[]{:S(2)}, u32[]{:S(2)}) %all-to-all-start.2) | async-done | bytes 163872 | tf_op jit(solution)/shard_map/all_to_all | solution.py:338
  87.8 2.1 %collective-permute-start.4 = (bf16[10,80,128]{2,1,0:T(8,128)(2,1)S(1)}, bf16[10,80,128]{2,1,0:T(8,128)(2,1)S(1)}, u32[]{:S(2)}, u32[]{:S(2)}) collective-permute-start(bf16[10,80,128]{2,1,0:T(8,128)(2,1)S(1)} %get-tuple-element.20), channel_id=1, source_target_pairs={{0,16},{16,32},{32,48},{48,64},{64,80},{80,96},{96,112},{112,128},... | collective-permute-start | bytes 614408 | tf_op jit(solution)/shard_map/ppermute | solution.py:360
  89.9 1.3 collective-permute-start.5
  91.2 1.0 shard_map.114
  92.2 21.9 %all-to-all-start.3 = ((f32[32,1,128]{2,1,0:T(1,128)}), f32[32,1,128]{2,1,0:T(1,128)S(1)}, u32[]{:S(2)}, u32[]{:S(2)}) async-start(f32[32,1,128]{2,1,0:T(1,128)} %shard_map.114), calls=%async_computation.3 | async-start | bytes 32768 | tf_op jit(solution)/shard_map/all_to_all | solution.py:362
  114.1 0.0 copy-done.5
  114.2 0.0 copy-done.6
  114.2 0.0 copy-done.7
  114.2 0.3 shard_map.117
  114.5 10.9 %all-to-all-done.3.refs_0_ = f32[32,1,128]{2,1,0:T(1,128)S(1)} async-done(((f32[32,1,128]{2,1,0:T(1,128)}), f32[32,1,128]{2,1,0:T(1,128)S(1)}, u32[]{:S(2)}, u32[]{:S(2)}) %all-to-all-start.3) | async-done | bytes 16416 | tf_op jit(solution)/shard_map/all_to_all | solution.py:362
  125.4 0.0 collective-permute-done.4.refs_2_
  125.4 0.0 collective-permute-done.5.refs_3_
  125.4 1.7 %shard_map.119 = bf16[16,10,128]{2,1,0:T(8,128)(2,1)S(1)} custom-call(f32[32,1,128]{2,1,0:T(1,128)S(1)} %all-to-all-done.3.refs_0_, bf16[8,80,128]{2,1,0:T(8,128)(2,1)S(1)} %all-to-all-done.2.refs_0_.refs_1_, bf16[10,80,128]{2,1,0:T(8,128)(2,1)S(1)} %collective-permute-done.4.refs_2_, bf16[10,80,128]{2,1,0:T(8,128)(2,1)S(1)} %collective-permute-done.5.refs_3_, ...), custom_call_target="tpu_custom_call" | custom-call | tf_op jit(solution)/shard_map/pallas_call | solution.py:33
  127.1 23.5 %all_to_all.30 = bf16[16,10,128]{2,1,0:T(8,128)(2,1)S(1)} all-to-all(bf16[16,10,128]{2,1,0:T(8,128)(2,1)S(1)} %shard_map.119), channel_id=1, replica_groups=mesh['y'=4,'l'=8,'x'=4,'h'=2,'k'=2] {'x','h','k'}, dimensions={0} | all-to-all | bytes 81920 | tf_op jit(solution)/shard_map/all_to_all | solution.py:384
  150.6 0.1 reshape.59
  150.8 0.8 reshape.60
  (4 shorter events, 0.1 us)
Async XLA Ops:
  1.6 27.5 %copy-start.2 = (f32[32,3]{1,0:T(8,128)S(1)}, f32[32,3]{1,0:T(8,128)}, u32[]{:S(2)}) copy-start(f32[32,3]{1,0:T(8,128)} %get-tuple-element.17.refs_4_.refs_2_) | copy-start | bytes 1156
  1.6 27.5 %all-to-all-start = ((f32[32,1,128]{2,1,0:T(1,128)}), f32[32,1,128]{2,1,0:T(1,128)S(1)}, u32[]{:S(2)}, u32[]{:S(2)}) async-start(f32[32,1,128]{2,1,0:T(1,128)} %get-tuple-element.15), calls=%async_computation | async-start | bytes 32768 | tf_op jit(solution)/shard_map/all_to_all | solution.py:324
  17.9 5.8 %collective-permute-start = (bf16[3,32,160]{2,1,0:T(8,128)(2,1)}, bf16[3,32,160]{2,1,0:T(8,128)(2,1)S(1)}, u32[]{:S(2)}, u32[]{:S(2)}) collective-permute-start(bf16[3,32,160]{2,1,0:T(8,128)(2,1)} %get-tuple-element.16.refs_1_), channel_id=1, source_target_pairs={{0,16},{16,32},{32,48},{48,64},{64,80},{80,96},{96,112},{112,128},... | collective-permute-start | bytes 92168 | tf_op jit(solution)/shard_map/ppermute | solution.py:327
  21.0 5.4 %collective-permute-start.1 = (bf16[3,32,160]{2,1,0:T(8,128)(2,1)}, bf16[3,32,160]{2,1,0:T(8,128)(2,1)S(1)}, u32[]{:S(2)}, u32[]{:S(2)}) collective-permute-start(bf16[3,32,160]{2,1,0:T(8,128)(2,1)} %get-tuple-element.16.refs_1_), channel_id=1, source_target_pairs={{16,0},{32,16},{48,32},{64,48},{80,64},{96,80},{112,96},{128,112},... | collective-permute-start | bytes 92168 | tf_op jit(solution)/shard_map/ppermute | solution.py:328
  22.3 1.2 copy-start.1
  23.5 5.7 %copy-start.4 = (bf16[3,32,160]{2,1,0:T(8,128)(2,1)S(1)}, bf16[3,32,160]{2,1,0:T(8,128)(2,1)}, u32[]{:S(2)}) copy-start(bf16[3,32,160]{2,1,0:T(8,128)(2,1)} %get-tuple-element.16.refs_1_) | copy-start | bytes 92164
  23.7 13.6 %copy-start.8 = (bf16[2,2,20,512]{3,1,2,0:T(2,128)(2,1)S(1)}, bf16[2,2,20,512]{3,1,2,0:T(2,128)(2,1)}, u32[]{:S(2)}) copy-start(bf16[2,2,20,512]{3,1,2,0:T(2,128)(2,1)} %param.17) | copy-start | bytes 245764
  30.9 21.4 %all-to-all-start.1 = ((f32[8,80,128]{2,1,0:T(8,128)}), f32[8,80,128]{2,1,0:T(8,128)S(1)}, u32[]{:S(2)}, u32[]{:S(2)}) async-start(f32[8,80,128]{2,1,0:T(8,128)} %shard_map.111), calls=%async_computation.1 | async-start | bytes 655360 | tf_op jit(solution)/shard_map/all_to_all | solution.py:334
  37.3 14.6 %collective-permute-start.3 = (bf16[2,2,2,10,512]{4,1,2,3,0:T(2,128)(2,1)S(1)}, bf16[2,2,2,10,512]{4,1,2,3,0:T(2,128)(2,1)S(1)}, u32[]{:S(2)}, u32[]{:S(2)}) collective-permute-start(bf16[2,2,2,10,512]{4,1,2,3,0:T(2,128)(2,1)S(1)} %bitcast.44), channel_id=1, source_target_pairs={{0,2},{2,0},{1,3},{3,1},{4,6},{6,4},{5,7},{7,5},{8,10},{10,8},{9,1... | collective-permute-start | bytes 245768 | tf_op jit(solution)/shard_map/ppermute | solution.py:340
  54.4 5.7 %copy-start.3 = (bf16[1,1,160,32]{2,3,1,0:T(8,128)(2,1)S(1)}, bf16[1,1,160,32]{2,3,1,0:T(8,128)(2,1)}, u32[]{:S(2)}) copy-start(bf16[1,1,160,32]{2,3,1,0:T(8,128)(2,1)} %param.11) | copy-start | bytes 30724
  54.4 23.5 %all-to-all-start.4 = ((bf16[8,2,2,2,2,10,512]{6,4,5,3,2,1,0:T(2,128)(2,1)}), bf16[8,2,2,2,2,10,512]{6,4,5,3,2,1,0:T(2,128)(2,1)S(1)}, u32[]{:S(2)}, u32[]{:S(2)}) async-start(bf16[8,2,2,2,2,10,512]{6,4,5,3,2,1,0:T(2,128)(2,1)} %broadcast_in_dim.27), calls=%async_computation.4 | async-start | bytes 2621440 | tf_op jit(solution)/shard_map/all_to_all | solution.py:343
  60.2 13.5 %collective-permute-start.2 = (f32[80,128]{1,0:T(8,128)S(1)}, f32[80,128]{1,0:T(8,128)S(1)}, u32[]{:S(2)}, u32[]{:S(2)}) collective-permute-start(f32[80,128]{1,0:T(8,128)S(1)} %shard_map.112.refs_0_), channel_id=1, source_target_pairs={{0,2},{2,0},{1,3},{3,1},{4,6},{6,4},{5,7},{7,5},{8,10},{10,8},{9,1... | collective-permute-start | bytes 122888 | tf_op jit(solution)/shard_map/ppermute | solution.py:336
  77.9 9.8 %all-to-all-start.2 = ((bf16[8,80,128]{2,1,0:T(8,128)(2,1)}), bf16[8,80,128]{2,1,0:T(8,128)(2,1)S(1)}, u32[]{:S(2)}, u32[]{:S(2)}) async-start(bf16[8,80,128]{2,1,0:T(8,128)(2,1)} %shard_map.113), calls=%async_computation.2 | async-start | bytes 327680 | tf_op jit(solution)/shard_map/all_to_all | solution.py:338
  83.3 1.2 copy-start
  85.4 28.8 %copy-start.5 = (f32[512]{0:T(512)S(1)}, f32[512]{0:T(512)}, u32[]{:S(2)}) copy-start(f32[512]{0:T(512)} %param.18) | copy-start | bytes 6148
  85.4 28.8 %copy-start.6 = (f32[512]{0:T(512)S(1)}, f32[512]{0:T(512)}, u32[]{:S(2)}) copy-start(f32[512]{0:T(512)} %param.19) | copy-start | bytes 6148
  85.4 28.8 %copy-start.7 = (f32[512]{0:T(512)S(1)}, f32[512]{0:T(512)}, u32[]{:S(2)}) copy-start(f32[512]{0:T(512)} %param.21) | copy-start | bytes 6148
  87.8 37.7 %collective-permute-start.4 = (bf16[10,80,128]{2,1,0:T(8,128)(2,1)S(1)}, bf16[10,80,128]{2,1,0:T(8,128)(2,1)S(1)}, u32[]{:S(2)}, u32[]{:S(2)}) collective-permute-start(bf16[10,80,128]{2,1,0:T(8,128)(2,1)S(1)} %get-tuple-element.20), channel_id=1, source_target_pairs={{0,16},{16,32},{32,48},{48,64},{64,80},{80,96},{96,112},{112,128},... | collective-permute-start | bytes 614408 | tf_op jit(solution)/shard_map/ppermute | solution.py:360
  89.9 35.5 %collective-permute-start.5 = (bf16[10,80,128]{2,1,0:T(8,128)(2,1)S(1)}, bf16[10,80,128]{2,1,0:T(8,128)(2,1)S(1)}, u32[]{:S(2)}, u32[]{:S(2)}) collective-permute-start(bf16[10,80,128]{2,1,0:T(8,128)(2,1)S(1)} %get-tuple-element.21), channel_id=1, source_target_pairs={{16,0},{32,16},{48,32},{64,48},{80,64},{96,80},{112,96},{128,112},... | collective-permute-start | bytes 614408 | tf_op jit(solution)/shard_map/ppermute | solution.py:361
  92.2 33.2 %all-to-all-start.3 = ((f32[32,1,128]{2,1,0:T(1,128)}), f32[32,1,128]{2,1,0:T(1,128)S(1)}, u32[]{:S(2)}, u32[]{:S(2)}) async-start(f32[32,1,128]{2,1,0:T(1,128)} %shard_map.114), calls=%async_computation.3 | async-start | bytes 32768 | tf_op jit(solution)/shard_map/all_to_all | solution.py:362
